TPU v7x, 512 devices: a whole 4x4x16 slice. The times are simulated.
512 devices in a mesh: seq: 64 (over x, z), tp: 8 (over y, core).
Axes of the slice: x: 4, y: 4, z: 16, core: 2. Of those that a mesh axis runs over, the one named last changes fastest.
Arguments:
- queries: bfloat16 [4, 1024], P(None, 'tp'), may hold values from -6 to 6
- keys_new: bfloat16 [4, 1024], P(None, 'tp'), may hold values from -32 to 32
- values_new: bfloat16 [4, 1024], P(None, 'tp'), may hold values from -6 to 6
- key_cache: bfloat16 [4, 4096, 1024], P(None, 'seq', 'tp'), may hold values from -32 to 32
- value_cache: bfloat16 [4, 4096, 1024], P(None, 'seq', 'tp'), may hold values from -6 to 6
- buckets: int32 [4, 4096], P(None, 'seq'), may hold values from 0 to 31
- lengths: int32 [4], replicated, may hold values from 1 to 4096, as said below
- bias_table: float32 [32, 16], replicated, may hold values from -3 to 3
- out_proj: bfloat16 [1024, 1024], P('tp'), may hold values from -0.1875 to 0.1875
- decode_in: bfloat16 [4, 1024], replicated, may hold values from -6 to 6
- prefill_in: bfloat16 [32768, 1024], P(('seq', 'tp')), may hold values from -6 to 6
- routes: int32 [32768, 2], P(('seq', 'tp')), may hold values from 0 to 15, all different within a row; in each aligned block of 64 rows (0 to 63, 64 to 127, ...) at most 10 rows name the same one
- gates: float32 [32768, 2], P(('seq', 'tp')), may hold values from 0.2 to 1
- dec_routes: int32 [4, 2], replicated, may hold values from 0 to 15, as said below
- dec_gates: float32 [4, 2], replicated, may hold values from 0.2 to 1
- norm_gain: float32 [1024], replicated, may hold values from 0.1 to 1.9
- w_gate: bfloat16 [1024, 45056], P('tp', 'seq'), may hold values from -0.1875 to 0.1875
- w_up: bfloat16 [1024, 45056], P('tp', 'seq'), may hold values from -0.1875 to 0.1875
- w_down: bfloat16 [45056, 1024], P('seq', 'tp'), may hold values from -0.109375 to 0.109375
Outputs:
- decode_out: bfloat16 [4, 1024], replicated
- prefill_out: bfloat16 [32768, 1024], P(('seq', 'tp'))
Inputs may be any that keep to these rules, and one draw needn't show every extreme that they name: `routes`: in the 64 rows of one device no expert is named by more than 10 rows, a bound that some block reaches. `dec_routes`: the two experts of a decode token differ; some decode token names expert 0 and some names expert 16 - 1. `lengths`: some request has all 4096 positions and some has exactly 1.
All inputs are finite; a program needn't handle non-finite values.
Results may differ from a plain program's by a relative error of at most 0.0075.
Values may be sent and summed in bfloat16 or wider, within the bound.
A program may use at most 64 MiB of HBM per device.

v0:
```python
import math

import jax
import jax.numpy as jnp
from jax import lax
from jax.sharding import PartitionSpec as P

HD = 64
EXPERTS = 16
TOP = 2
CAP = 10


def combined_all(value, axis, join):
    pieces = jax.tree.map(lambda part: lax.all_gather(part, axis), value)
    head = jax.tree.map(lambda part: part[0], pieces)
    tail = jax.tree.map(lambda part: part[1:], pieces)
    so_far, _ = lax.scan(lambda so_far, section: (join(so_far, section), None), head, tail)
    return so_far


def rms_scale(hidden, norm_gain):
    values = hidden.astype(jnp.float32)
    meansq = jnp.mean(values * values, axis=-1, keepdims=True)
    return (values * lax.rsqrt(meansq + 1e-06) * norm_gain).astype(jnp.bfloat16)


def combine_parts(earlier, later):
    max_early, sum_early, acc_early = earlier
    max_late, sum_late, acc_late = later
    joint_max = jnp.maximum(max_early, max_late)
    scale_early = jnp.exp(max_early - joint_max)
    scale_late = jnp.exp(max_late - joint_max)
    joint_sum = sum_early * scale_early + sum_late * scale_late
    joint_acc = acc_early * scale_early[..., None] + acc_late * scale_late[..., None]
    return (joint_max, joint_sum, joint_acc)


def route_slots(route_rows, capacity):
    flat_routes = route_rows.reshape(-1)
    onehot = (flat_routes[:, None] == jnp.arange(EXPERTS, dtype=jnp.int32)[None, :]).astype(
        jnp.int32
    )
    earlier = jnp.cumsum(onehot, axis=0) - onehot
    slot_rank = jnp.sum(earlier * onehot, axis=1)
    return flat_routes * capacity + slot_rank


def pack_rows(normed, route_rows, capacity, shards):
    flat_index = route_slots(route_rows, capacity)
    source = jnp.repeat(normed, TOP, axis=0)
    feature_width = normed.shape[1]
    packed = jnp.zeros((EXPERTS * capacity, feature_width), jnp.bfloat16).at[flat_index].set(source)
    packed = packed.reshape(EXPERTS, capacity, feature_width)
    return (jnp.repeat(packed, shards, axis=0), flat_index)


def expert_block(row_block, weights):
    gate_full, up_full, down_full = weights
    gate_pre = jnp.dot(row_block, gate_full, preferred_element_type=jnp.float32)
    up_pre = jnp.dot(row_block, up_full, preferred_element_type=jnp.float32)
    act = (jax.nn.gelu(gate_pre, approximate=True) * up_pre).astype(jnp.bfloat16)
    return jnp.dot(act, down_full, preferred_element_type=jnp.float32).astype(jnp.bfloat16)


def expert_apply(received, weights):
    peer_count, slot_count, feature_width = received.shape
    partial_value = expert_block(received.reshape(peer_count * slot_count, feature_width), weights)
    return partial_value.reshape(peer_count, slot_count, feature_width)


def unpack_rows(returned, flat_index, shards, residual, gate_rows):
    peer_count, slot_count, feature_width = returned.shape
    summed = returned.astype(jnp.float32).reshape(EXPERTS, shards, slot_count, feature_width)
    summed = jnp.sum(summed, axis=1).reshape(EXPERTS * slot_count, feature_width)
    picked = jnp.take(summed, flat_index, axis=0).reshape(-1, TOP, feature_width)
    combined = residual.astype(jnp.float32) + jnp.sum(gate_rows[..., None] * picked, axis=1)
    return combined.astype(jnp.bfloat16)


def body(
    queries,
    keys_new,
    values_new,
    key_cache,
    value_cache,
    buckets,
    lengths,
    bias_table,
    out_proj,
    decode_in,
    prefill_in,
    routes,
    gates,
    dec_routes,
    dec_gates,
    norm_gain,
    w_gate,
    w_up,
    w_down,
):
    seq_count = lax.axis_size("seq")
    seq_index = lax.axis_index("seq")
    tp_index = lax.axis_index("tp")
    shards = seq_count // EXPERTS
    weights = (
        lax.all_gather(w_gate, "tp", axis=0, tiled=True),
        lax.all_gather(w_up, "tp", axis=0, tiled=True),
        lax.all_gather(w_down, "tp", axis=1, tiled=True),
    )
    normed_pre = rms_scale(prefill_in, norm_gain)
    request_count, heads_width = queries.shape
    heads_here = heads_width // HD
    ctx_local = key_cache.shape[1]
    score_scale = 1.0 / math.sqrt(HD)
    query_rows = queries.reshape(request_count, heads_here, HD)
    key_rows = key_cache.reshape(request_count, ctx_local, heads_here, HD)
    value_rows = value_cache.reshape(request_count, ctx_local, heads_here, HD).astype(jnp.float32)
    bias_here = lax.dynamic_slice_in_dim(bias_table, tp_index * heads_here, heads_here, 1)
    bucket_hot = (
        buckets[..., None] == jnp.arange(bias_table.shape[0], dtype=jnp.int32)[None, None, :]
    ).astype(jnp.float32)
    bias_rows = jnp.einsum("rcn,nh->rhc", bucket_hot, bias_here, precision=lax.Precision.HIGHEST)
    cache_scores = (
        jnp.einsum("rhd,rchd->rhc", query_rows, key_rows, preferred_element_type=jnp.float32)
        * score_scale
        + bias_rows
    )
    positions = seq_index * ctx_local + jnp.arange(ctx_local, dtype=jnp.int32)
    valid_mask = (positions[None, :] < lengths[:, None])[:, None, :]
    cache_scores = jnp.where(valid_mask, cache_scores, -1e30)
    local_max = jnp.max(cache_scores, axis=-1)
    local_weights = jnp.where(valid_mask, jnp.exp(cache_scores - local_max[..., None]), 0.0)
    local_sum = jnp.sum(local_weights, axis=-1)
    local_acc = jnp.einsum(
        "rhc,rchd->rhd", local_weights, value_rows, precision=lax.Precision.HIGHEST
    )
    part_max, part_sum, part_acc = combined_all(
        (local_max, local_sum, local_acc), "seq", combine_parts
    )
    own_key = keys_new.reshape(request_count, heads_here, HD).astype(jnp.float32)
    own_value = values_new.reshape(request_count, heads_here, HD).astype(jnp.float32)
    own_score = (
        jnp.sum(query_rows.astype(jnp.float32) * own_key, axis=-1) * score_scale
        + bias_here[0][None, :]
    )
    row_peak = jnp.maximum(part_max, own_score)
    keep_scale = jnp.exp(part_max - row_peak)
    own_weight = jnp.exp(own_score - row_peak)
    weight_total = part_sum * keep_scale + own_weight
    weighted = part_acc * keep_scale[..., None] + own_weight[..., None] * own_value
    mixed_rows = (
        (weighted / weight_total[..., None])
        .astype(jnp.bfloat16)
        .reshape(request_count, heads_width)
    )
    head_terms = jnp.dot(mixed_rows, out_proj, preferred_element_type=jnp.float32)
    attended = lax.psum(head_terms, "tp")
    decode_hidden = (decode_in.astype(jnp.float32) + attended).astype(jnp.bfloat16)
    normed_dec = rms_scale(decode_hidden, norm_gain)
    my_expert = seq_index // shards
    dec_part = expert_block(normed_dec, weights).astype(jnp.float32)
    gate_here = jnp.sum(jnp.where(dec_routes == my_expert, dec_gates, 0.0), axis=1)
    dec_terms = lax.psum(gate_here[:, None] * dec_part, "seq")
    decode_out = (decode_hidden.astype(jnp.float32) + dec_terms).astype(jnp.bfloat16)
    send_all, index_all = pack_rows(normed_pre, routes, CAP, shards)
    back_all = lax.all_to_all(
        expert_apply(
            lax.all_to_all(send_all, "seq", split_axis=0, concat_axis=0, tiled=True), weights
        ),
        "seq",
        split_axis=0,
        concat_axis=0,
        tiled=True,
    )
    prefill_out = unpack_rows(back_all, index_all, shards, prefill_in, gates)
    return (decode_out, prefill_out)


def solution(mesh):
    placed = (
        P(None, "tp"),
        P(None, "tp"),
        P(None, "tp"),
        P(None, "seq", "tp"),
        P(None, "seq", "tp"),
        P(None, "seq"),
        P(),
        P(),
        P("tp", None),
        P(),
        P(("seq", "tp"), None),
        P(("seq", "tp"), None),
        P(("seq", "tp"), None),
        P(),
        P(),
        P(),
        P("tp", "seq"),
        P("tp", "seq"),
        P("seq", "tp"),
    )
    return jax.shard_map(
        body, mesh=mesh, in_specs=placed, out_specs=(P(), P(("seq", "tp"), None)), check_vma=False
    )
```

profile of v0, /device:TPU:8, one launch (start us, length us, event | category | flops | bytes accessed | tf_op | source)
XLA Modules:
  0.0 734.8 jit_solution(8691198079200414398)
XLA Ops:
  7.9 0.8 copy.57
  8.8 0.7 broadcast_multiply_fusion
  9.7 1.0 fusion.17
  10.8 1.0 fusion.19
  13.1 1.2 scatter_custom_fusion
  14.5 1.6 broadcast_in_dim.67
  16.1 18.7 %all-to-all-start = ((bf16[64,10,1024]{2,1,0:T(8,128)(2,1)}), bf16[64,10,1024]{2,1,0:T(8,128)(2,1)S(1)}, u32[]{:S(2)}, u32[]{:S(2)}) async-start(bf16[64,10,1024]{2,1,0:T(8,128)(2,1)} %bitcast.19), calls=%async_computation | async-start | bytes 4194304 | tf_op jit(solution)/shard_map/all_to_all | solution.py:169
  34.9 0.7 all-gather.11.cloned.1.call-update
  36.7 0.7 constant_dynamic-slice_fusion.1
  38.2 162.8 %all-gather.2 = f32[256,2,64]{2,1,0:T(2,128)S(1)} all-gather(f32[4,2,64]{2,1,0:T(2,128)S(1)} %bitcast.70), channel_id=4, replica_groups=mesh['seq'=64,'tp'=8] {'seq'}, dimensions={0}, use_global_device_ids=true | all-gather | bytes 133120 | tf_op jit(solution)/shard_map/all_gather | solution.py:15
  201.2 80.8 %all-gather.4 = f32[64,4,2]{1,2,0:T(2,128)S(1)} all-gather(f32[1,4,2]{1,2,0:T(2,128)S(1)} %bitcast.72), channel_id=3, replica_groups=mesh['seq'=64,'tp'=8] {'seq'}, dimensions={0}, use_global_device_ids=true | all-gather | bytes 2080 | tf_op jit(solution)/shard_map/all_gather | solution.py:15
  282.0 88.0 %all-gather.3 = f32[64,4,2]{1,2,0:T(2,128)S(1)} all-gather(f32[1,4,2]{1,2,0:T(2,128)S(1)} %bitcast.71), channel_id=2, replica_groups=mesh['seq'=64,'tp'=8] {'seq'}, dimensions={0}, use_global_device_ids=true | all-gather | bytes 2080 | tf_op jit(solution)/shard_map/all_gather | solution.py:15
  370.0 1.3 reshape.153
  371.3 4.4 fusion.68
  375.8 6.6 convolution_convert_fusion
  382.4 1.6 reshape.154
  384.1 14.8 %all-to-all-start.1 = ((bf16[64,10,1024]{2,1,0:T(8,128)(2,1)}), bf16[64,10,1024]{2,1,0:T(8,128)(2,1)S(1)}, u32[]{:S(2)}, u32[]{:S(2)}) async-start(bf16[64,10,1024]{2,1,0:T(8,128)(2,1)} %reshape.154), calls=%async_computation.1 | async-start | bytes 4194304 | tf_op jit(solution)/shard_map/all_to_all | solution.py:167
  399.0 18.6 %while.14 = (s32[]{:T(128)}, f32[4,2]{0,1:T(2,128)S(1)}, f32[4,2]{0,1:T(2,128)S(1)}, f32[4,2,64]{2,1,0:T(2,128)S(1)}, f32[63,4,2]{1,2,0:T(2,128)S(1)}, /*index=5...) while((s32[]{:T(128)}, f32[4,2]{0,1:T(2,128)S(1)}, f32[4,2]{0,1:T(2,128)S(1)}, ...), condition=%wide.region_3.4_spmd, body=%wide.region_2.3_spmd.sunk | while | flops 1586 | bytes 6685 | solution.py:18
  419.0 21.6 %psum.14 = f32[4,1024]{1,0:T(4,128)S(1)} all-reduce(f32[4,1024]{1,0:T(4,128)S(1)} %fusion.67), channel_id=1, replica_groups=mesh['seq'=64,'tp'=8] {'tp'}, use_global_device_ids=true, to_apply=%region_5.6 | all-reduce | flops 4096 | bytes 32768 | tf_op jit(solution)/shard_map/psum | solution.py:158
  440.8 1.8 fusion.59
  442.6 2.7 fusion.13
  445.3 279.1 %psum.15 = f32[4,1024]{1,0:T(4,128)S(1)} all-reduce(f32[4,1024]{1,0:T(4,128)S(1)} %fusion.13), channel_id=1, replica_groups=mesh['seq'=64,'tp'=8] {'seq'}, use_global_device_ids=true, to_apply=%region_8.9 | all-reduce | flops 4096 | bytes 32768 | tf_op jit(solution)/shard_map/psum | solution.py:164
  725.6 0.8 gather_fusion
  726.7 0.8 multiply_reduce_fusion
  (360 shorter events, 26.7 us)
Async XLA Ops:
  7.2 411.7 %copy-start = (bf16[128,1024]{1,0:T(8,128)(2,1)S(1)}, bf16[128,1024]{1,0:T(8,128)(2,1)}, u32[]{:S(2)}) copy-start(bf16[128,1024]{1,0:T(8,128)(2,1)} %param.29) | copy-start | bytes 786436
  7.2 364.1 %all-gather.9.cloned.1.call-start = ((), (), s32[]{:S(2)}) async-start(), calls=%async_computation.2 | async-start | bytes 1622016 | tf_op jit(solution)/shard_map/all_gather | solution.py:107
  16.1 20.2 %copy-start.6 = (bf16[4,64,128]{2,1,0:T(8,128)(2,1)S(1)}, bf16[4,64,128]{2,1,0:T(8,128)(2,1)}, u32[]{:S(2)}) copy-start(bf16[4,64,128]{2,1,0:T(8,128)(2,1)} %param.24) | copy-start | bytes 196612
  16.1 20.4 %copy-start.11 = (bf16[4,128]{1,0:T(4,128)(2,1)S(1)}, bf16[4,128]{1,0:T(4,128)(2,1)}, u32[]{:S(2)}) copy-start(bf16[4,128]{1,0:T(4,128)(2,1)} %param.21) | copy-start | bytes 3076
  16.1 20.5 %copy-start.7 = (bf16[4,64,128]{2,1,0:T(8,128)(2,1)S(1)}, bf16[4,64,128]{2,1,0:T(8,128)(2,1)}, u32[]{:S(2)}) copy-start(bf16[4,64,128]{2,1,0:T(8,128)(2,1)} %param.25) | copy-start | bytes 196612
  16.1 21.3 %copy-start.20 = (s32[4]{0:T(128)S(1)}, s32[4]{0:T(128)}, u32[]{:S(2)}) copy-start(s32[4]{0:T(128)} %param.27) | copy-start | bytes 52
  16.1 21.5 %copy-start.19 = (s32[4,64]{1,0:T(4,128)S(1)}, s32[4,64]{1,0:T(4,128)}, u32[]{:S(2)}) copy-start(s32[4,64]{1,0:T(4,128)} %param.26) | copy-start | bytes 3076
  16.1 353.8 %all-to-all-start = ((bf16[64,10,1024]{2,1,0:T(8,128)(2,1)}), bf16[64,10,1024]{2,1,0:T(8,128)(2,1)S(1)}, u32[]{:S(2)}, u32[]{:S(2)}) async-start(bf16[64,10,1024]{2,1,0:T(8,128)(2,1)} %bitcast.19), calls=%async_computation | async-start | bytes 4194304 | tf_op jit(solution)/shard_map/all_to_all | solution.py:169
  34.8 340.9 %all-gather.11.cloned.1.call-start = ((), (), s32[]{:S(2)}) async-start(), calls=%async_computation.3 | async-start | bytes 1622016 | tf_op jit(solution)/shard_map/all_gather | solution.py:108
  35.6 340.2 %all-gather.13.cloned.1.call-start = ((), (), s32[]{:S(2)}) async-start(), calls=%async_computation.4 | async-start | bytes 1622016 | tf_op jit(solution)/shard_map/all_gather | solution.py:109
  201.0 174.8 %copy-start.3 = (f32[256,2,64]{2,1,0:T(2,128)}, f32[256,2,64]{2,1,0:T(2,128)S(1)}, u32[]{:S(2)}) copy-start(f32[256,2,64]{2,1,0:T(2,128)S(1)} %all-gather.2) | copy-start | bytes 393220
  282.0 89.3 %copy-start.4 = (f32[64,4,2]{1,2,0:T(2,128)}, f32[64,4,2]{1,2,0:T(2,128)S(1)}, u32[]{:S(2)}) copy-start(f32[64,4,2]{1,2,0:T(2,128)S(1)} %all-gather.4) | copy-start | bytes 6148
  384.0 15.0 %slice-start.1 = ((f32[64,4,2]{1,2,0:T(2,128)}), f32[63,4,2]{1,2,0:T(2,128)S(1)}, s32[]{:S(2)}) async-start(f32[64,4,2]{1,2,0:T(2,128)} %copy-done.4), calls=%async_computation.6 | async-start | bytes 129024 | tf_op jit(solution)/shard_map/slice | solution.py:17
  384.0 15.0 %slice-start.2 = ((f32[64,4,2]{1,2,0:T(2,128)}), f32[63,4,2]{1,2,0:T(2,128)S(1)}, s32[]{:S(2)}) async-start(f32[64,4,2]{1,2,0:T(2,128)} %copy-done.5), calls=%async_computation.7 | async-start | bytes 129024 | tf_op jit(solution)/shard_map/slice | solution.py:17
  384.0 34.0 %copy-start.12 = (bf16[4,128]{1,0:T(4,128)(2,1)S(1)}, bf16[4,128]{1,0:T(4,128)(2,1)}, u32[]{:S(2)}) copy-start(bf16[4,128]{1,0:T(4,128)(2,1)} %param.22) | copy-start | bytes 3076
  384.0 34.0 %copy-start.13 = (bf16[4,128]{1,0:T(4,128)(2,1)S(1)}, bf16[4,128]{1,0:T(4,128)(2,1)}, u32[]{:S(2)}) copy-start(bf16[4,128]{1,0:T(4,128)(2,1)} %param.23) | copy-start | bytes 3076
  384.0 34.6 %copy-start.9 = (s32[64,2]{0,1:T(2,128)S(1)}, s32[64,2]{0,1:T(2,128)}, u32[]{:S(2)}) copy-start(s32[64,2]{0,1:T(2,128)} %param.32) | copy-start | bytes 1540
  384.0 34.7 %copy-start.14 = (f32[64,2]{0,1:T(2,128)S(1)}, f32[64,2]{0,1:T(2,128)}, u32[]{:S(2)}) copy-start(f32[64,2]{0,1:T(2,128)} %param.33) | copy-start | bytes 1540
  384.0 56.6 %copy-start.18 = (s32[128]{0:T(128)S(1)}, s32[128]{0:T(128)}, u32[]{:S(2)}) copy-start(s32[128]{0:T(128)} %copy-done.17) | copy-start | bytes 1540
  384.1 56.6 %copy-start.15 = (f32[4,2]{0,1:T(2,128)S(1)}, f32[4,2]{0,1:T(2,128)}, u32[]{:S(2)}) copy-start(f32[4,2]{0,1:T(2,128)} %param.35) | copy-start | bytes 100
  384.1 56.6 %copy-start.16 = (s32[4,2]{0,1:T(2,128)S(1)}, s32[4,2]{0,1:T(2,128)}, u32[]{:S(2)}) copy-start(s32[4,2]{0,1:T(2,128)} %param.34) | copy-start | bytes 100
  384.1 56.6 %copy-start.10 = (bf16[4,1024]{1,0:T(4,128)(2,1)S(1)}, bf16[4,1024]{1,0:T(4,128)(2,1)}, u32[]{:S(2)}) copy-start(bf16[4,1024]{1,0:T(4,128)(2,1)} %param.30) | copy-start | bytes 24580
  384.1 56.7 %copy-start.8 = (f32[1024]{0:T(1024)S(1)}, f32[1024]{0:T(1024)}, u32[]{:S(2)}) copy-start(f32[1024]{0:T(1024)} %param.36) | copy-start | bytes 12292
  384.1 341.0 %all-to-all-start.1 = ((bf16[64,10,1024]{2,1,0:T(8,128)(2,1)}), bf16[64,10,1024]{2,1,0:T(8,128)(2,1)S(1)}, u32[]{:S(2)}, u32[]{:S(2)}) async-start(bf16[64,10,1024]{2,1,0:T(8,128)(2,1)} %reshape.154), calls=%async_computation.1 | async-start | bytes 4194304 | tf_op jit(solution)/shard_map/all_to_all | solution.py:167
  (5 other events, 22.5 us)
Sparse Core Ops, SparseCore 0:
  10.1 36.1 all-gather.8
  48.5 33.4 all-gather.10
  84.0 33.4 all-gather.12
where the time goes:
time: 735 us
  blocking collectives  632 us (86%)
  starting transfers between devices  33.7 us (5%)
  local copies, waits for them, and re-layouts  23.1 us (3%)
  matrix products  16.3 us (2%)
  between operations  14.2 us (2%)
  other arithmetic  12.9 us (2%)
    all_gather x3, blocking collectives, combined_all(): pieces = jax.tree.map(lambda part: lax.all_gather(part, axis), value)  332 us
    psum x1, blocking collectives, body(): dec_terms = lax.psum(gate_here[:, None] * dec_part, 'seq')  279 us
    psum x1, blocking collectives, body(): attended = lax.psum(head_terms, 'tp')  21.6 us
    all_to_all x1, starting transfers between devices, body(): lax.all_to_all(send_all, 'seq', split_axis=0, concat_axis=0, tiled=True)  18.7 us
    all_to_all x1, starting transfers between devices, body(): lax.all_to_all(expert_apply(lax.all_to_all(send_all, 'seq', split_axis=0,...  14.8 us
  transfers between devices with their start and end apart: 5, of which 0 were waited for; matrix products, arithmetic and copies ran while one was open for 5% of the time, Pallas kernels for 0%

commit v1 on v0

--- a/solution.py
+++ b/solution.py
@@ -1,8 +1,11 @@
+import functools
 import math
 
 import jax
 import jax.numpy as jnp
 from jax import lax
+from jax.experimental import pallas as pl
+from jax.experimental.pallas import tpu as pltpu
 from jax.sharding import PartitionSpec as P
 
 HD = 64
@@ -11,29 +14,73 @@
 CAP = 10
 
 
-def combined_all(value, axis, join):
-    pieces = jax.tree.map(lambda part: lax.all_gather(part, axis), value)
-    head = jax.tree.map(lambda part: part[0], pieces)
-    tail = jax.tree.map(lambda part: part[1:], pieces)
-    so_far, _ = lax.scan(lambda so_far, section: (join(so_far, section), None), head, tail)
-    return so_far
+def peer_device(axis, peer):
+    if axis == "seq":
+        return (peer, lax.axis_index("tp"))
+    return (lax.axis_index("seq"), peer)
+
+
+def gather_kernel(axis, count, x_ref, out_ref, landed, send_sem, recv_sem):
+    me = lax.axis_index(axis)
+    barrier = pltpu.get_barrier_semaphore()
+
+    def greet(step, carry):
+        pl.semaphore_signal(
+            barrier,
+            inc=1,
+            device_id=peer_device(axis, lax.rem(me + step, count)),
+            device_id_type=pl.DeviceIdType.MESH,
+        )
+        return carry
+
+    lax.fori_loop(1, count, greet, 0)
+    pl.semaphore_wait(barrier, count - 1)
+
+    def transfer(step):
+        return pltpu.make_async_remote_copy(
+            src_ref=x_ref,
+            dst_ref=landed.at[me],
+            send_sem=send_sem.at[step],
+            recv_sem=recv_sem.at[step],
+            device_id=peer_device(axis, lax.rem(me + step, count)),
+            device_id_type=pl.DeviceIdType.MESH,
+        )
+
+    def launch(step, carry):
+        transfer(step).start()
+        return carry
+
+    lax.fori_loop(1, count, launch, 0)
+    landed[me] = x_ref[...]
+
+    def finish(step, carry):
+        transfer(step).wait()
+        return carry
+
+    lax.fori_loop(1, count, finish, 0)
+    out_ref[...] = landed[...]
+
+
+def axis_gather(x, axis, count, collective_id):
+    stacked = (count,) + x.shape
+    return pl.pallas_call(
+        functools.partial(gather_kernel, axis, count),
+        out_shape=jax.ShapeDtypeStruct(stacked, x.dtype),
+        in_specs=[pl.BlockSpec(memory_space=pltpu.VMEM)],
+        out_specs=pl.BlockSpec(memory_space=pltpu.VMEM),
+        scratch_shapes=[
+            pltpu.VMEM(stacked, x.dtype),
+            pltpu.SemaphoreType.DMA((count,)),
+            pltpu.SemaphoreType.DMA((count,)),
+        ],
+        compiler_params=pltpu.CompilerParams(collective_id=collective_id, has_side_effects=True),
+    )(x)
 
 
 def rms_scale(hidden, norm_gain):
     values = hidden.astype(jnp.float32)
     meansq = jnp.mean(values * values, axis=-1, keepdims=True)
     return (values * lax.rsqrt(meansq + 1e-06) * norm_gain).astype(jnp.bfloat16)
-
-
-def combine_parts(earlier, later):
-    max_early, sum_early, acc_early = earlier
-    max_late, sum_late, acc_late = later
-    joint_max = jnp.maximum(max_early, max_late)
-    scale_early = jnp.exp(max_early - joint_max)
-    scale_late = jnp.exp(max_late - joint_max)
-    joint_sum = sum_early * scale_early + sum_late * scale_late
-    joint_acc = acc_early * scale_early[..., None] + acc_late * scale_late[..., None]
-    return (joint_max, joint_sum, joint_acc)
 
 
 def route_slots(route_rows, capacity):
@@ -135,9 +182,29 @@
     local_acc = jnp.einsum(
         "rhc,rchd->rhd", local_weights, value_rows, precision=lax.Precision.HIGHEST
     )
-    part_max, part_sum, part_acc = combined_all(
-        (local_max, local_sum, local_acc), "seq", combine_parts
-    )
+    tp_count = lax.axis_size("tp")
+    packed_parts = jnp.concatenate(
+        [
+            local_acc.reshape(request_count, heads_here * HD),
+            jnp.pad(
+                jnp.stack([local_max.reshape(-1), local_sum.reshape(-1)]),
+                ((0, 2), (0, heads_here * HD - request_count * heads_here)),
+            ),
+        ],
+        axis=0,
+    )
+    gathered = axis_gather(packed_parts, "seq", seq_count, 1)
+    slot_max = gathered[:, request_count, : request_count * heads_here].reshape(
+        seq_count, request_count, heads_here
+    )
+    slot_sum = gathered[:, request_count + 1, : request_count * heads_here].reshape(
+        seq_count, request_count, heads_here
+    )
+    slot_acc = gathered[:, :request_count, :].reshape(seq_count, request_count, heads_here, HD)
+    part_max = jnp.max(slot_max, axis=0)
+    slot_scale = jnp.exp(slot_max - part_max[None])
+    part_sum = jnp.sum(slot_sum * slot_scale, axis=0)
+    part_acc = jnp.sum(slot_acc * slot_scale[..., None], axis=0)
     own_key = keys_new.reshape(request_count, heads_here, HD).astype(jnp.float32)
     own_value = values_new.reshape(request_count, heads_here, HD).astype(jnp.float32)
     own_score = (
@@ -155,13 +222,18 @@
         .reshape(request_count, heads_width)
     )
     head_terms = jnp.dot(mixed_rows, out_proj, preferred_element_type=jnp.float32)
-    attended = lax.psum(head_terms, "tp")
+    attended = jnp.sum(axis_gather(head_terms, "tp", tp_count, 2), axis=0)
     decode_hidden = (decode_in.astype(jnp.float32) + attended).astype(jnp.bfloat16)
     normed_dec = rms_scale(decode_hidden, norm_gain)
-    my_expert = seq_index // shards
-    dec_part = expert_block(normed_dec, weights).astype(jnp.float32)
-    gate_here = jnp.sum(jnp.where(dec_routes == my_expert, dec_gates, 0.0), axis=1)
-    dec_terms = lax.psum(gate_here[:, None] * dec_part, "seq")
+    dec_parts = axis_gather(expert_block(normed_dec, weights), "seq", seq_count, 3)
+    slot_expert = jnp.arange(seq_count, dtype=jnp.int32) // shards
+    slot_gate = jnp.sum(
+        jnp.where(dec_routes[:, :, None] == slot_expert[None, None, :], dec_gates[:, :, None], 0.0),
+        axis=1,
+    )
+    dec_terms = jnp.sum(
+        slot_gate.T[:, :, None] * dec_parts.astype(jnp.float32), axis=0
+    )
     decode_out = (decode_hidden.astype(jnp.float32) + dec_terms).astype(jnp.bfloat16)
     send_all, index_all = pack_rows(normed_pre, routes, CAP, shards)
     back_all = lax.all_to_all(

time: 735 us -> 339 us (0.46)
  the two profiles are of different devices: /device:TPU:8 before, /device:TPU:1 now
where the time goes in v1:
time: 339 us; the launch traced here: 338 us
  Pallas kernels  156 us (46%)
  waiting for transfers between devices  95.4 us (28%)
  starting transfers between devices  30.4 us (9%)
  matrix products  17.5 us (5%)
  between operations  14.1 us (4%)
  other arithmetic  12.5 us (4%)
  local copies, waits for them, and re-layouts  12.1 us (4%)
    pallas_call x3, Pallas kernels, axis_gather(): pl.pallas_call(functools.partial(gather_kernel, axis, count), out_shape=j...  156 us
    all_to_all x1, waiting for transfers between devices, body(): lax.all_to_all(send_all, 'seq', split_axis=0, concat_axis=0, tiled=True)  93.3 us
    all_to_all x1, starting transfers between devices, body(): lax.all_to_all(send_all, 'seq', split_axis=0, concat_axis=0, tiled=True)  19.1 us
    all_to_all x1, starting transfers between devices, body(): lax.all_to_all(expert_apply(lax.all_to_all(send_all, 'seq', split_axis=0,...  11.2 us
    dot_general x2, matrix products, expert_block(): jnp.dot(act, down_full, preferred_element_type=jnp.float32)  9.94 us
  transfers between devices with their start and end apart: 5, of which 1 were waited for; matrix products, arithmetic and copies ran while one was open for 9% of the time, Pallas kernels for 46%

profile of v1, /device:TPU:1, one launch (start us, length us, event | category | flops | bytes accessed | tf_op | source)
XLA Modules:
  0.0 337.8 jit_solution(7772500492934809178)
XLA Ops:
  7.9 0.8 copy.47
  9.7 1.0 fusion.12
  10.8 1.0 fusion.14
  12.5 1.2 scatter_custom_fusion
  13.9 1.6 broadcast_in_dim.76
  15.5 19.1 %all-to-all-start = ((bf16[64,10,1024]{2,1,0:T(8,128)(2,1)}), bf16[64,10,1024]{2,1,0:T(8,128)(2,1)S(1)}, u32[]{:S(2)}, u32[]{:S(2)}) async-start(bf16[64,10,1024]{2,1,0:T(8,128)(2,1)} %bitcast.13), calls=%async_computation | async-start | bytes 4194304 | tf_op jit(solution)/shard_map/all_to_all | solution.py:241
  36.1 93.3 %all-to-all-done = bf16[64,10,1024]{2,1,0:T(8,128)(2,1)S(1)} async-done(((bf16[64,10,1024]{2,1,0:T(8,128)(2,1)}), bf16[64,10,1024]{2,1,0:T(8,128)(2,1)S(1)}, u32[]{:S(2)}, u32[]{:S(2)}) %all-to-all-start) | async-done | bytes 1310752 | tf_op jit(solution)/shard_map/all_to_all | solution.py:241
  129.4 1.3 reshape.259
  130.7 4.4 %fusion.64 = f32[640,704]{0,1:T(8,128)} fusion(bf16[640,1024]{1,0:T(8,128)(2,1)} %reshape.259, bf16[1024,704]{0,1:T(8,128)(2,1)} %all-gather.4.cloned.1.call-done), kind=kOutput, calls=%fused_computation.110 | convolution fusion | flops 922746880 | bytes 4554752 | tf_op jit(solution)/shard_map/dot_general | solution.py:107
  135.2 6.6 %convolution_convert_fusion = bf16[640,1024]{1,0:T(8,128)(2,1)S(1)} fusion(bf16[704,1024]{1,0:T(8,128)(2,1)} %all-gather.8.cloned.1.call-done, f32[640,704]{0,1:T(8,128)} %fusion.64, bf16[640,1024]{1,0:T(8,128)(2,1)S(1)} %copy-done.1, bf16[1024,704]{0,1:T(8,128)(2,1)} %all-gather.6.cloned.1.call-done), kind=kOutput, calls=%fused_computation.13 | convolution fusion | flops 1850654720 | bytes 7307264 | tf_op jit(solution)/shard_map/dot_general | solution.py:110
  141.8 1.6 reshape.260
  143.4 11.2 %all-to-all-start.1 = ((bf16[64,10,1024]{2,1,0:T(8,128)(2,1)}), bf16[64,10,1024]{2,1,0:T(8,128)(2,1)S(1)}, u32[]{:S(2)}, u32[]{:S(2)}) async-start(bf16[64,10,1024]{2,1,0:T(8,128)(2,1)} %reshape.260), calls=%async_computation.1 | async-start | bytes 4194304 | tf_op jit(solution)/shard_map/all_to_all | solution.py:239
  157.6 108.2 %shard_map.194 = f32[64,8,128]{2,1,0:T(8,128)} custom-call(f32[8,128]{1,0:T(8,128)} %pad_maximum_fusion.x_ref), custom_call_target="tpu_custom_call" | custom-call | tf_op jit(solution)/shard_map/pallas_call | solution.py:66
  265.9 1.0 fusion.61
  267.8 1.1 multiply_reduce_fusion.3
  269.9 1.0 multiply_reduce_fusion.2
  271.7 10.7 %shard_map.195 = f32[8,4,1024]{2,1,0:T(4,128)} custom-call(f32[4,1024]{1,0:T(4,128)} %fusion.42.x_ref), custom_call_target="tpu_custom_call" | custom-call | tf_op jit(solution)/shard_map/pallas_call | solution.py:66
  283.1 0.9 reduce_sum.119
  284.2 1.8 fusion.56
  286.0 3.3 convolution_convert_fusion.1.x_ref
  289.4 36.7 %shard_map.196 = bf16[64,4,1024]{2,1,0:T(4,128)(2,1)} custom-call(bf16[4,1024]{1,0:T(4,128)(2,1)} %convolution_convert_fusion.1.x_ref), custom_call_target="tpu_custom_call" | custom-call | tf_op jit(solution)/shard_map/pallas_call | solution.py:66
  326.1 1.4 multiply_reduce_fusion
  328.6 0.8 gather_fusion
  329.7 0.8 multiply_reduce_fusion.1
  (106 shorter events, 12.5 us)
Async XLA Ops:
  7.2 263.7 %copy-start = (bf16[128,1024]{1,0:T(8,128)(2,1)S(1)}, bf16[128,1024]{1,0:T(8,128)(2,1)}, u32[]{:S(2)}) copy-start(bf16[128,1024]{1,0:T(8,128)(2,1)} %param.27) | copy-start | bytes 786436
  7.2 123.5 %all-gather.4.cloned.1.call-start = ((), (), s32[]{:S(2)}) async-start(), calls=%async_computation.2 | async-start | bytes 1622016 | tf_op jit(solution)/shard_map/all_gather | solution.py:154
  15.5 113.9 %all-to-all-start = ((bf16[64,10,1024]{2,1,0:T(8,128)(2,1)}), bf16[64,10,1024]{2,1,0:T(8,128)(2,1)S(1)}, u32[]{:S(2)}, u32[]{:S(2)}) async-start(bf16[64,10,1024]{2,1,0:T(8,128)(2,1)} %bitcast.13), calls=%async_computation | async-start | bytes 4194304 | tf_op jit(solution)/shard_map/all_to_all | solution.py:241
  34.6 100.6 %all-gather.6.cloned.1.call-start = ((), (), s32[]{:S(2)}) async-start(), calls=%async_computation.3 | async-start | bytes 1622016 | tf_op jit(solution)/shard_map/all_gather | solution.py:155
  35.3 99.8 %all-gather.8.cloned.1.call-start = ((), (), s32[]{:S(2)}) async-start(), calls=%async_computation.4 | async-start | bytes 1622016 | tf_op jit(solution)/shard_map/all_gather | solution.py:156
  130.7 4.5 %copy-start.1 = (bf16[640,1024]{1,0:T(8,128)(2,1)S(1)}, bf16[640,1024]{1,0:T(8,128)(2,1)}, u32[]{:S(2)}) copy-start(bf16[640,1024]{1,0:T(8,128)(2,1)} %reshape.259) | copy-start | bytes 3932164
  143.3 11.2 %copy-start.8 = (bf16[4,128]{1,0:T(4,128)(2,1)S(1)}, bf16[4,128]{1,0:T(4,128)(2,1)}, u32[]{:S(2)}) copy-start(bf16[4,128]{1,0:T(4,128)(2,1)} %param.19) | copy-start | bytes 3076
  143.3 11.6 %copy-start.3 = (bf16[4,64,128]{2,1,0:T(8,128)(2,1)S(1)}, bf16[4,64,128]{2,1,0:T(8,128)(2,1)}, u32[]{:S(2)}) copy-start(bf16[4,64,128]{2,1,0:T(8,128)(2,1)} %param.22) | copy-start | bytes 196612
  143.3 12.5 %copy-start.15 = (s32[4]{0:T(128)S(1)}, s32[4]{0:T(128)}, u32[]{:S(2)}) copy-start(s32[4]{0:T(128)} %param.25) | copy-start | bytes 52
  143.4 12.7 %copy-start.14 = (s32[4,64]{1,0:T(4,128)S(1)}, s32[4,64]{1,0:T(4,128)}, u32[]{:S(2)}) copy-start(s32[4,64]{1,0:T(4,128)} %param.24) | copy-start | bytes 3076
  143.4 13.2 %copy-start.4 = (bf16[4,64,128]{2,1,0:T(8,128)(2,1)S(1)}, bf16[4,64,128]{2,1,0:T(8,128)(2,1)}, u32[]{:S(2)}) copy-start(bf16[4,64,128]{2,1,0:T(8,128)(2,1)} %param.23) | copy-start | bytes 196612
  143.4 184.7 %all-to-all-start.1 = ((bf16[64,10,1024]{2,1,0:T(8,128)(2,1)}), bf16[64,10,1024]{2,1,0:T(8,128)(2,1)S(1)}, u32[]{:S(2)}, u32[]{:S(2)}) async-start(bf16[64,10,1024]{2,1,0:T(8,128)(2,1)} %reshape.260), calls=%async_computation.1 | async-start | bytes 4194304 | tf_op jit(solution)/shard_map/all_to_all | solution.py:239
  154.6 114.5 %copy-start.10 = (bf16[4,128]{1,0:T(4,128)(2,1)S(1)}, bf16[4,128]{1,0:T(4,128)(2,1)}, u32[]{:S(2)}) copy-start(bf16[4,128]{1,0:T(4,128)(2,1)} %param.20) | copy-start | bytes 3076
  154.6 116.3 %copy-start.9 = (bf16[4,128]{1,0:T(4,128)(2,1)S(1)}, bf16[4,128]{1,0:T(4,128)(2,1)}, u32[]{:S(2)}) copy-start(bf16[4,128]{1,0:T(4,128)(2,1)} %param.21) | copy-start | bytes 3076
  154.9 127.5 %copy-start.11 = (s32[4,2]{0,1:T(2,128)S(1)}, s32[4,2]{0,1:T(2,128)}, u32[]{:S(2)}) copy-start(s32[4,2]{0,1:T(2,128)} %param.32) | copy-start | bytes 100
  154.9 127.6 %copy-start.12 = (f32[4,2]{0,1:T(2,128)S(1)}, f32[4,2]{0,1:T(2,128)}, u32[]{:S(2)}) copy-start(f32[4,2]{0,1:T(2,128)} %param.33) | copy-start | bytes 100
  155.1 127.8 %copy-start.6 = (s32[64,2]{0,1:T(2,128)S(1)}, s32[64,2]{0,1:T(2,128)}, u32[]{:S(2)}) copy-start(s32[64,2]{0,1:T(2,128)} %param.30) | copy-start | bytes 1540
  155.1 127.9 %copy-start.13 = (f32[64,2]{0,1:T(2,128)S(1)}, f32[64,2]{0,1:T(2,128)}, u32[]{:S(2)}) copy-start(f32[64,2]{0,1:T(2,128)} %param.31) | copy-start | bytes 1540
  156.0 128.0 %copy-start.7 = (bf16[4,1024]{1,0:T(4,128)(2,1)S(1)}, bf16[4,1024]{1,0:T(4,128)(2,1)}, u32[]{:S(2)}) copy-start(bf16[4,1024]{1,0:T(4,128)(2,1)} %param.28) | copy-start | bytes 24580
  156.0 128.2 %copy-start.5 = (f32[1024]{0:T(1024)S(1)}, f32[1024]{0:T(1024)}, u32[]{:S(2)}) copy-start(f32[1024]{0:T(1024)} %param.34) | copy-start | bytes 12292
  329.4 1.1 copy-start.2
Sparse Core Ops, SparseCore 0:
  10.1 38.1 all-gather.3
  50.4 33.3 all-gather.5
  86.0 33.4 all-gather.7

commit v2 on v1

--- a/solution.py
+++ b/solution.py
@@ -20,16 +20,19 @@
     return (lax.axis_index("seq"), peer)
 
 
-def gather_kernel(axis, count, x_ref, out_ref, landed, send_sem, recv_sem):
-    me = lax.axis_index(axis)
+def gather_kernel(axis, count, stride, x_ref, out_ref, landed, send_sem, recv_sem):
+    index = lax.axis_index(axis)
+    me = lax.rem(index // stride, count)
+    base = index - me * stride
+
+    def peer_of(step):
+        return peer_device(axis, base + lax.rem(me + step, count) * stride)
+
     barrier = pltpu.get_barrier_semaphore()
 
     def greet(step, carry):
         pl.semaphore_signal(
-            barrier,
-            inc=1,
-            device_id=peer_device(axis, lax.rem(me + step, count)),
-            device_id_type=pl.DeviceIdType.MESH,
+            barrier, inc=1, device_id=peer_of(step), device_id_type=pl.DeviceIdType.MESH
         )
         return carry
 
@@ -42,7 +45,7 @@
             dst_ref=landed.at[me],
             send_sem=send_sem.at[step],
             recv_sem=recv_sem.at[step],
-            device_id=peer_device(axis, lax.rem(me + step, count)),
+            device_id=peer_of(step),
             device_id_type=pl.DeviceIdType.MESH,
         )
 
@@ -61,10 +64,10 @@
     out_ref[...] = landed[...]
 
 
-def axis_gather(x, axis, count, collective_id):
+def axis_gather(x, axis, count, stride, collective_id):
     stacked = (count,) + x.shape
     return pl.pallas_call(
-        functools.partial(gather_kernel, axis, count),
+        functools.partial(gather_kernel, axis, count, stride),
         out_shape=jax.ShapeDtypeStruct(stacked, x.dtype),
         in_specs=[pl.BlockSpec(memory_space=pltpu.VMEM)],
         out_specs=pl.BlockSpec(memory_space=pltpu.VMEM),
@@ -75,6 +78,23 @@
         ],
         compiler_params=pltpu.CompilerParams(collective_id=collective_id, has_side_effects=True),
     )(x)
+
+
+def merge_softmax(stacked, rows, width):
+    slot_max = stacked[:, rows, :width]
+    slot_sum = stacked[:, rows + 1, :width]
+    joint_max = jnp.max(slot_max, axis=0)
+    slot_scale = jnp.exp(slot_max - joint_max[None])
+    joint_sum = jnp.sum(slot_sum * slot_scale, axis=0)
+    lane_scale = jnp.repeat(slot_scale.reshape(slot_scale.shape[0], rows, -1), HD, axis=2)
+    joint_acc = jnp.sum(stacked[:, :rows, :] * lane_scale, axis=0)
+    return joint_max, joint_sum, joint_acc
+
+
+def pack_softmax(joint_max, joint_sum, joint_acc):
+    rows, lanes = joint_acc.shape
+    stats = jnp.stack([joint_max, joint_sum])
+    return jnp.concatenate([joint_acc, jnp.pad(stats, ((0, 2), (0, lanes - stats.shape[1])))], axis=0)
 
 
 def rms_scale(hidden, norm_gain):
@@ -183,28 +203,19 @@
         "rhc,rchd->rhd", local_weights, value_rows, precision=lax.Precision.HIGHEST
     )
     tp_count = lax.axis_size("tp")
-    packed_parts = jnp.concatenate(
-        [
-            local_acc.reshape(request_count, heads_here * HD),
-            jnp.pad(
-                jnp.stack([local_max.reshape(-1), local_sum.reshape(-1)]),
-                ((0, 2), (0, heads_here * HD - request_count * heads_here)),
-            ),
-        ],
-        axis=0,
-    )
-    gathered = axis_gather(packed_parts, "seq", seq_count, 1)
-    slot_max = gathered[:, request_count, : request_count * heads_here].reshape(
-        seq_count, request_count, heads_here
-    )
-    slot_sum = gathered[:, request_count + 1, : request_count * heads_here].reshape(
-        seq_count, request_count, heads_here
-    )
-    slot_acc = gathered[:, :request_count, :].reshape(seq_count, request_count, heads_here, HD)
-    part_max = jnp.max(slot_max, axis=0)
-    slot_scale = jnp.exp(slot_max - part_max[None])
-    part_sum = jnp.sum(slot_sum * slot_scale, axis=0)
-    part_acc = jnp.sum(slot_acc * slot_scale[..., None], axis=0)
+    z_count = 16 if seq_count % 16 == 0 else seq_count
+    x_count = seq_count // z_count
+    flat_width = request_count * heads_here
+    packed_parts = pack_softmax(
+        local_max.reshape(-1), local_sum.reshape(-1), local_acc.reshape(request_count, heads_here * HD)
+    )
+    stage = merge_softmax(axis_gather(packed_parts, "seq", z_count, 1, 1), request_count, flat_width)
+    stage = merge_softmax(
+        axis_gather(pack_softmax(*stage), "seq", x_count, z_count, 2), request_count, flat_width
+    )
+    part_max = stage[0].reshape(request_count, heads_here)
+    part_sum = stage[1].reshape(request_count, heads_here)
+    part_acc = stage[2].reshape(request_count, heads_here, HD)
     own_key = keys_new.reshape(request_count, heads_here, HD).astype(jnp.float32)
     own_value = values_new.reshape(request_count, heads_here, HD).astype(jnp.float32)
     own_score = (
@@ -222,29 +233,25 @@
         .reshape(request_count, heads_width)
     )
     head_terms = jnp.dot(mixed_rows, out_proj, preferred_element_type=jnp.float32)
-    attended = jnp.sum(axis_gather(head_terms, "tp", tp_count, 2), axis=0)
+    attended = jnp.sum(axis_gather(head_terms, "tp", tp_count, 1, 3), axis=0)
+    send_all, index_all = pack_rows(normed_pre, routes, CAP, shards)
+    received = lax.all_to_all(send_all, "seq", split_axis=0, concat_axis=0, tiled=True)
+    received, attended = lax.optimization_barrier((received, attended))
     decode_hidden = (decode_in.astype(jnp.float32) + attended).astype(jnp.bfloat16)
     normed_dec = rms_scale(decode_hidden, norm_gain)
-    dec_parts = axis_gather(expert_block(normed_dec, weights), "seq", seq_count, 3)
-    slot_expert = jnp.arange(seq_count, dtype=jnp.int32) // shards
+    expert_rows = expert_apply(received, weights)
+    expert_rows, normed_dec = lax.optimization_barrier((expert_rows, normed_dec))
+    back_all = lax.all_to_all(expert_rows, "seq", split_axis=0, concat_axis=0, tiled=True)
+    dec_parts = axis_gather(expert_block(normed_dec, weights), "seq", z_count, 1, 4)
+    z_base = (seq_index // z_count) * z_count
+    slot_expert = (z_base + jnp.arange(z_count, dtype=jnp.int32)) // shards
     slot_gate = jnp.sum(
         jnp.where(dec_routes[:, :, None] == slot_expert[None, None, :], dec_gates[:, :, None], 0.0),
         axis=1,
     )
-    dec_terms = jnp.sum(
-        slot_gate.T[:, :, None] * dec_parts.astype(jnp.float32), axis=0
-    )
+    z_terms = jnp.sum(slot_gate.T[:, :, None] * dec_parts.astype(jnp.float32), axis=0)
+    dec_terms = jnp.sum(axis_gather(z_terms, "seq", x_count, z_count, 5), axis=0)
     decode_out = (decode_hidden.astype(jnp.float32) + dec_terms).astype(jnp.bfloat16)
-    send_all, index_all = pack_rows(normed_pre, routes, CAP, shards)
-    back_all = lax.all_to_all(
-        expert_apply(
-            lax.all_to_all(send_all, "seq", split_axis=0, concat_axis=0, tiled=True), weights
-        ),
-        "seq",
-        split_axis=0,
-        concat_axis=0,
-        tiled=True,
-    )
     prefill_out = unpack_rows(back_all, index_all, shards, prefill_in, gates)
     return (decode_out, prefill_out)
 

time: 339 us -> 311 us (0.917)
  waiting for transfers between devices: 95.4 us -> 2.07 us
  Pallas kernels: 156 us -> 224 us
  starting transfers between devices: 30.4 us -> 24.4 us
    all_to_all x1, waiting for transfers between devices: 93.3 us -> 0.01 us  [body(): lax.all_to_all(send_all, 'seq', split_axis=0, concat_axis=0, tiled=True)]
    pallas_call x3 -> x5, Pallas kernels: 156 us -> 224 us  [axis_gather(): pl.pallas_call(functools.partial(gather_kernel, axis, count, stride), out...]
    all_to_all x1, starting transfers between devices: 11.2 us -> 5.02 us  [body(): lax.all_to_all(expert_rows, 'seq', split_axis=0, concat_axis=0, tiled=True)]
  transfers between devices with their start and end apart: 5 -> 5, of which waited for: 1 -> 0; matrix products, arithmetic and copies ran while one was open for 9% -> 11% of each run, Pallas kernels for 46% -> 73%
where the time goes in v2:
time: 311 us; the launch traced here: 310 us
  Pallas kernels  224 us (72%)
  starting transfers between devices  24.4 us (8%)
  matrix products  17.5 us (6%)
  other arithmetic  14.8 us (5%)
  between operations  14.2 us (5%)
  local copies, waits for them, and re-layouts  12.1 us (4%)
    pallas_call x5, Pallas kernels, axis_gather(): pl.pallas_call(functools.partial(gather_kernel, axis, count, stride), out...  224 us
    all_to_all x1, starting transfers between devices, body(): lax.all_to_all(send_all, 'seq', split_axis=0, concat_axis=0, tiled=True)  19.3 us
    dot_general x2, matrix products, expert_block(): jnp.dot(act, down_full, preferred_element_type=jnp.float32)  9.94 us
    dot_general x2, matrix products, expert_block(): gate_pre = jnp.dot(row_block, gate_full, preferred_element_type=jnp.float32)  6.26 us
  transfers between devices with their start and end apart: 5, of which 0 were waited for; matrix products, arithmetic and copies ran while one was open for 11% of the time, Pallas kernels for 73%

profile of v2, /device:TPU:1, one launch (start us, length us, event | category | flops | bytes accessed | tf_op | source)
XLA Modules:
  0.0 309.5 jit_solution(2916472502619445266)
XLA Ops:
  10.5 1.0 fusion.12
  11.5 1.0 fusion.14
  13.3 1.2 scatter_custom_fusion
  14.6 1.6 broadcast_in_dim.81
  16.2 19.3 %all-to-all-start = ((bf16[64,10,1024]{2,1,0:T(8,128)(2,1)}), bf16[64,10,1024]{2,1,0:T(8,128)(2,1)S(1)}, u32[]{:S(2)}, u32[]{:S(2)}) async-start(bf16[64,10,1024]{2,1,0:T(8,128)(2,1)} %bitcast.2), calls=%async_computation | async-start | bytes 4194304 | tf_op jit(solution)/shard_map/all_to_all | solution.py:238
  39.1 98.4 %shard_map.194 = f32[16,8,128]{2,1,0:T(8,128)} custom-call(f32[8,128]{1,0:T(8,128)} %pad_maximum_fusion.x_ref), custom_call_target="tpu_custom_call" | custom-call | tf_op jit(solution)/shard_map/pallas_call | solution.py:69
  137.5 1.0 slice_reduce_fusion.2
  139.3 0.9 multiply_reduce_fusion.2
  140.8 6.4 %shard_map.195 = f32[4,8,128]{2,1,0:T(8,128)} custom-call(f32[8,128]{1,0:T(8,128)} %pad_maximum_fusion.1.x_ref), custom_call_target="tpu_custom_call" | custom-call | tf_op jit(solution)/shard_map/pallas_call | solution.py:69
  147.3 0.8 slice_reduce_fusion.1
  151.0 12.6 %shard_map.196 = f32[8,4,1024]{2,1,0:T(4,128)} custom-call(f32[4,1024]{1,0:T(4,128)} %fusion.45.x_ref), custom_call_target="tpu_custom_call" | custom-call | tf_op jit(solution)/shard_map/pallas_call | solution.py:69
  163.6 0.9 reduce_sum.148
  164.6 1.3 reshape.271
  165.9 4.4 %fusion.62 = f32[640,704]{0,1:T(8,128)} fusion(bf16[640,1024]{1,0:T(8,128)(2,1)} %reshape.271, bf16[1024,704]{0,1:T(8,128)(2,1)} %all-gather.4.cloned.1.call-done), kind=kOutput, calls=%fused_computation.117 | convolution fusion | flops 922746880 | bytes 4554752 | tf_op jit(solution)/shard_map/dot_general | solution.py:127
  170.4 6.6 %convolution_convert_fusion = bf16[640,1024]{1,0:T(8,128)(2,1)S(1)} fusion(bf16[704,1024]{1,0:T(8,128)(2,1)} %all-gather.8.cloned.1.call-done, f32[640,704]{0,1:T(8,128)} %fusion.62, bf16[640,1024]{1,0:T(8,128)(2,1)S(1)} %copy-done.1, bf16[1024,704]{0,1:T(8,128)(2,1)} %all-gather.6.cloned.1.call-done), kind=kOutput, calls=%fused_computation.13 | convolution fusion | flops 1850654720 | bytes 7307264 | tf_op jit(solution)/shard_map/dot_general | solution.py:130
  177.0 1.6 reshape.272
  178.8 5.0 %all-to-all-start.1 = ((bf16[64,10,1024]{2,1,0:T(8,128)(2,1)}), bf16[64,10,1024]{2,1,0:T(8,128)(2,1)S(1)}, u32[]{:S(2)}, u32[]{:S(2)}) async-start(bf16[64,10,1024]{2,1,0:T(8,128)(2,1)} %reshape.272), calls=%async_computation.1 | async-start | bytes 4194304 | tf_op jit(solution)/shard_map/all_to_all | solution.py:244
  184.5 1.8 fusion.63
  186.3 3.3 %convolution_convert_fusion.1.x_ref = bf16[4,1024]{1,0:T(4,128)(2,1)} fusion(bf16[704,1024]{1,0:T(8,128)(2,1)} %all-gather.8.cloned.1.call-done, bf16[4,1024]{1,0:T(4,128)(2,1)S(1)} %fusion.24, bf16[1024,704]{0,1:T(8,128)(2,1)} %all-gather.6.cloned.1.call-done, f32[4,704]{1,0:T(4,128)S(1)} %fusion.63), kind=kOutput, calls=%fused_computation.15 | convolution fusion | flops 11566592 | bytes 2911232 | tf_op jit(solution)/shard_map/dot_general | solution.py:130
  189.7 98.8 %shard_map.197 = bf16[16,4,1024]{2,1,0:T(4,128)(2,1)} custom-call(bf16[4,1024]{1,0:T(4,128)(2,1)} %convolution_convert_fusion.1.x_ref), custom_call_target="tpu_custom_call" | custom-call | tf_op jit(solution)/shard_map/pallas_call | solution.py:69
  288.4 1.6 multiply_reduce_fusion.1.x_ref
  290.1 8.3 %shard_map.198 = f32[4,4,1024]{2,1,0:T(4,128)} custom-call(f32[4,1024]{1,0:T(4,128)} %multiply_reduce_fusion.1.x_ref), custom_call_target="tpu_custom_call" | custom-call | tf_op jit(solution)/shard_map/pallas_call | solution.py:69
  298.4 0.9 reduce_sum.152
  301.5 0.8 multiply_reduce_fusion
  (120 shorter events, 15.7 us)
Async XLA Ops:
  7.2 143.1 %copy-start = (bf16[128,1024]{1,0:T(8,128)(2,1)S(1)}, bf16[128,1024]{1,0:T(8,128)(2,1)}, u32[]{:S(2)}) copy-start(bf16[128,1024]{1,0:T(8,128)(2,1)} %param.27) | copy-start | bytes 786436
  7.2 158.8 %all-gather.4.cloned.1.call-start = ((), (), s32[]{:S(2)}) async-start(), calls=%async_computation.2 | async-start | bytes 1622016 | tf_op jit(solution)/shard_map/all_gather | solution.py:174
  7.9 162.5 %all-gather.6.cloned.1.call-start = ((), (), s32[]{:S(2)}) async-start(), calls=%async_computation.3 | async-start | bytes 1622016 | tf_op jit(solution)/shard_map/all_gather | solution.py:175
  16.2 20.1 %copy-start.8 = (bf16[4,128]{1,0:T(4,128)(2,1)S(1)}, bf16[4,128]{1,0:T(4,128)(2,1)}, u32[]{:S(2)}) copy-start(bf16[4,128]{1,0:T(4,128)(2,1)} %param.19) | copy-start | bytes 3076
  16.2 20.2 %copy-start.3 = (bf16[4,64,128]{2,1,0:T(8,128)(2,1)S(1)}, bf16[4,64,128]{2,1,0:T(8,128)(2,1)}, u32[]{:S(2)}) copy-start(bf16[4,64,128]{2,1,0:T(8,128)(2,1)} %param.22) | copy-start | bytes 196612
  16.2 21.1 %copy-start.15 = (s32[4]{0:T(128)S(1)}, s32[4]{0:T(128)}, u32[]{:S(2)}) copy-start(s32[4]{0:T(128)} %param.25) | copy-start | bytes 52
  16.2 21.3 %copy-start.14 = (s32[4,64]{1,0:T(4,128)S(1)}, s32[4,64]{1,0:T(4,128)}, u32[]{:S(2)}) copy-start(s32[4,64]{1,0:T(4,128)} %param.24) | copy-start | bytes 3076
  16.2 21.9 %copy-start.4 = (bf16[4,64,128]{2,1,0:T(8,128)(2,1)S(1)}, bf16[4,64,128]{2,1,0:T(8,128)(2,1)}, u32[]{:S(2)}) copy-start(bf16[4,64,128]{2,1,0:T(8,128)(2,1)} %param.23) | copy-start | bytes 196612
  16.2 148.3 %all-to-all-start = ((bf16[64,10,1024]{2,1,0:T(8,128)(2,1)}), bf16[64,10,1024]{2,1,0:T(8,128)(2,1)S(1)}, u32[]{:S(2)}, u32[]{:S(2)}) async-start(bf16[64,10,1024]{2,1,0:T(8,128)(2,1)} %bitcast.2), calls=%async_computation | async-start | bytes 4194304 | tf_op jit(solution)/shard_map/all_to_all | solution.py:238
  35.5 113.2 %copy-start.10 = (bf16[4,128]{1,0:T(4,128)(2,1)S(1)}, bf16[4,128]{1,0:T(4,128)(2,1)}, u32[]{:S(2)}) copy-start(bf16[4,128]{1,0:T(4,128)(2,1)} %param.20) | copy-start | bytes 3076
  35.5 114.7 %copy-start.9 = (bf16[4,128]{1,0:T(4,128)(2,1)S(1)}, bf16[4,128]{1,0:T(4,128)(2,1)}, u32[]{:S(2)}) copy-start(bf16[4,128]{1,0:T(4,128)(2,1)} %param.21) | copy-start | bytes 3076
  35.5 134.8 %all-gather.8.cloned.1.call-start = ((), (), s32[]{:S(2)}) async-start(), calls=%async_computation.4 | async-start | bytes 1622016 | tf_op jit(solution)/shard_map/all_gather | solution.py:176
  165.9 4.5 %copy-start.1 = (bf16[640,1024]{1,0:T(8,128)(2,1)S(1)}, bf16[640,1024]{1,0:T(8,128)(2,1)}, u32[]{:S(2)}) copy-start(bf16[640,1024]{1,0:T(8,128)(2,1)} %reshape.271) | copy-start | bytes 3932164
  177.0 1.6 copy-start.7
  177.0 1.7 copy-start.5
  178.8 5.3 %copy-start.6 = (s32[64,2]{0,1:T(2,128)S(1)}, s32[64,2]{0,1:T(2,128)}, u32[]{:S(2)}) copy-start(s32[64,2]{0,1:T(2,128)} %param.30) | copy-start | bytes 1540
  178.8 5.4 %copy-start.11 = (f32[64,2]{0,1:T(2,128)S(1)}, f32[64,2]{0,1:T(2,128)}, u32[]{:S(2)}) copy-start(f32[64,2]{0,1:T(2,128)} %param.31) | copy-start | bytes 1540
  178.8 5.5 %copy-start.12 = (f32[4,2]{0,1:T(2,128)S(1)}, f32[4,2]{0,1:T(2,128)}, u32[]{:S(2)}) copy-start(f32[4,2]{0,1:T(2,128)} %param.33) | copy-start | bytes 100
  178.8 5.5 %copy-start.13 = (s32[4,2]{0,1:T(2,128)S(1)}, s32[4,2]{0,1:T(2,128)}, u32[]{:S(2)}) copy-start(s32[4,2]{0,1:T(2,128)} %param.32) | copy-start | bytes 100
  178.8 121.0 %all-to-all-start.1 = ((bf16[64,10,1024]{2,1,0:T(8,128)(2,1)}), bf16[64,10,1024]{2,1,0:T(8,128)(2,1)S(1)}, u32[]{:S(2)}, u32[]{:S(2)}) async-start(bf16[64,10,1024]{2,1,0:T(8,128)(2,1)} %reshape.272), calls=%async_computation.1 | async-start | bytes 4194304 | tf_op jit(solution)/shard_map/all_to_all | solution.py:244
  301.1 1.1 copy-start.2
Sparse Core Ops, SparseCore 0:
  10.1 38.1 all-gather.3
  50.4 33.3 all-gather.5
  86.0 33.4 all-gather.7

commit v3 on v2

--- a/solution.py
+++ b/solution.py
@@ -73,6 +73,81 @@
         out_specs=pl.BlockSpec(memory_space=pltpu.VMEM),
         scratch_shapes=[
             pltpu.VMEM(stacked, x.dtype),
+            pltpu.SemaphoreType.DMA((count,)),
+            pltpu.SemaphoreType.DMA((count,)),
+        ],
+        compiler_params=pltpu.CompilerParams(collective_id=collective_id, has_side_effects=True),
+    )(x)
+
+
+def exchange_kernel(axis, count, stride, x_ref, out_ref, landed, send_sem, recv_sem):
+    index = lax.axis_index(axis)
+    me = lax.rem(index // stride, count)
+    base = index - me * stride
+
+    def member(slot):
+        return peer_device(axis, base + slot * stride)
+
+    barrier = pltpu.get_barrier_semaphore()
+
+    def greet(step, carry):
+        pl.semaphore_signal(
+            barrier,
+            inc=1,
+            device_id=member(lax.rem(me + step, count)),
+            device_id_type=pl.DeviceIdType.MESH,
+        )
+        return carry
+
+    lax.fori_loop(1, count, greet, 0)
+    pl.semaphore_wait(barrier, count - 1)
+
+    def outgoing(step):
+        target = lax.rem(me + step, count)
+        return pltpu.make_async_remote_copy(
+            src_ref=x_ref.at[target],
+            dst_ref=landed.at[me],
+            send_sem=send_sem.at[step],
+            recv_sem=recv_sem.at[step],
+            device_id=member(target),
+            device_id_type=pl.DeviceIdType.MESH,
+        )
+
+    def incoming(step):
+        source = lax.rem(me - step + count, count)
+        return pltpu.make_async_remote_copy(
+            src_ref=x_ref.at[source],
+            dst_ref=landed.at[source],
+            send_sem=send_sem.at[step],
+            recv_sem=recv_sem.at[step],
+            device_id=member(source),
+            device_id_type=pl.DeviceIdType.MESH,
+        )
+
+    def launch(step, carry):
+        outgoing(step).start()
+        return carry
+
+    lax.fori_loop(1, count, launch, 0)
+    landed[me] = x_ref[me]
+
+    def finish(step, carry):
+        outgoing(step).wait_send()
+        incoming(step).wait_recv()
+        return carry
+
+    lax.fori_loop(1, count, finish, 0)
+    out_ref[...] = landed[...]
+
+
+def axis_exchange(x, axis, count, stride, collective_id):
+    return pl.pallas_call(
+        functools.partial(exchange_kernel, axis, count, stride),
+        out_shape=jax.ShapeDtypeStruct(x.shape, x.dtype),
+        in_specs=[pl.BlockSpec(memory_space=pltpu.VMEM)],
+        out_specs=pl.BlockSpec(memory_space=pltpu.VMEM),
+        scratch_shapes=[
+            pltpu.VMEM(x.shape, x.dtype),
             pltpu.SemaphoreType.DMA((count,)),
             pltpu.SemaphoreType.DMA((count,)),
         ],
@@ -234,14 +309,26 @@
     )
     head_terms = jnp.dot(mixed_rows, out_proj, preferred_element_type=jnp.float32)
     attended = jnp.sum(axis_gather(head_terms, "tp", tp_count, 1, 3), axis=0)
-    send_all, index_all = pack_rows(normed_pre, routes, CAP, shards)
-    received = lax.all_to_all(send_all, "seq", split_axis=0, concat_axis=0, tiled=True)
-    received, attended = lax.optimization_barrier((received, attended))
+    flat_index = route_slots(routes, CAP)
+    slabs = (
+        jnp.zeros((EXPERTS * CAP, normed_pre.shape[1]), jnp.bfloat16)
+        .at[flat_index]
+        .set(jnp.repeat(normed_pre, TOP, axis=0))
+        .reshape(EXPERTS, CAP, normed_pre.shape[1])
+    )
+    group_count = seq_count // shards
+    arrived = axis_exchange(slabs, "seq", group_count, shards, 6)
+    arrived, attended = lax.optimization_barrier((arrived, attended))
     decode_hidden = (decode_in.astype(jnp.float32) + attended).astype(jnp.bfloat16)
     normed_dec = rms_scale(decode_hidden, norm_gain)
-    expert_rows = expert_apply(received, weights)
-    expert_rows, normed_dec = lax.optimization_barrier((expert_rows, normed_dec))
-    back_all = lax.all_to_all(expert_rows, "seq", split_axis=0, concat_axis=0, tiled=True)
+    block_rows = axis_gather(arrived, "seq", shards, 1, 7)
+    block_out = expert_block(block_rows.reshape(-1, block_rows.shape[-1]), weights)
+    block_out, normed_dec = lax.optimization_barrier((block_out, normed_dec))
+    part_rows = axis_exchange(block_out.reshape(block_rows.shape), "seq", shards, 1, 8)
+    summed = jnp.zeros(part_rows.shape[1:], jnp.float32)
+    for part in range(shards):
+        summed = summed + part_rows[part].astype(jnp.float32)
+    returned = axis_exchange(summed, "seq", group_count, shards, 9)
     dec_parts = axis_gather(expert_block(normed_dec, weights), "seq", z_count, 1, 4)
     z_base = (seq_index // z_count) * z_count
     slot_expert = (z_base + jnp.arange(z_count, dtype=jnp.int32)) // shards
@@ -252,7 +339,11 @@
     z_terms = jnp.sum(slot_gate.T[:, :, None] * dec_parts.astype(jnp.float32), axis=0)
     dec_terms = jnp.sum(axis_gather(z_terms, "seq", x_count, z_count, 5), axis=0)
     decode_out = (decode_hidden.astype(jnp.float32) + dec_terms).astype(jnp.bfloat16)
-    prefill_out = unpack_rows(back_all, index_all, shards, prefill_in, gates)
+    picked = jnp.take(returned.reshape(EXPERTS * CAP, -1), flat_index, axis=0)
+    picked = picked.reshape(-1, TOP, picked.shape[-1])
+    prefill_out = (
+        prefill_in.astype(jnp.float32) + jnp.sum(gates[..., None] * picked, axis=1)
+    ).astype(jnp.bfloat16)
     return (decode_out, prefill_out)
 
 

time: 311 us -> 320 us (1.029)
  the two profiles are of different devices: /device:TPU:1 before, /device:TPU:32 now
where the time goes in v3:
time: 320 us; the launch traced here: 318 us
  Pallas kernels  255 us (80%)
  local copies, waits for them, and re-layouts  16.3 us (5%)
  matrix products  16.3 us (5%)
  other arithmetic  14.5 us (5%)
  between operations  14.2 us (4%)
    pallas_call x3, Pallas kernels, axis_exchange(): pl.pallas_call(functools.partial(exchange_kernel, axis, count, stride), o...  141 us
    pallas_call x6, Pallas kernels, axis_gather(): pl.pallas_call(functools.partial(gather_kernel, axis, count, stride), out...  114 us
    dot_general x2, matrix products, expert_block(): jnp.dot(act, down_full, preferred_element_type=jnp.float32)  9.94 us
  transfers between devices with their start and end apart: 3, of which 0 were waited for; matrix products, arithmetic and copies ran while one was open for 8% of the time, Pallas kernels for 40%

profile of v3, /device:TPU:32, one launch (start us, length us, event | category | flops | bytes accessed | tf_op | source)
XLA Modules:
  0.0 318.4 jit_solution(6388659763215256368)
XLA Ops:
  11.0 1.0 copy.71
  13.6 0.9 fusion.60
  14.9 0.9 reshape.263
  16.8 21.2 %shard_map.195 = f32[16,8,128]{2,1,0:T(8,128)} custom-call(f32[8,128]{1,0:T(8,128)} %pad_maximum_fusion.x_ref), custom_call_target="tpu_custom_call" | custom-call | tf_op jit(solution)/shard_map/pallas_call | solution.py:69
  38.0 1.0 slice_reduce_fusion.2
  39.5 0.9 multiply_reduce_fusion.2
  41.3 7.9 %shard_map.196 = f32[4,8,128]{2,1,0:T(8,128)} custom-call(f32[8,128]{1,0:T(8,128)} %pad_maximum_fusion.1.x_ref), custom_call_target="tpu_custom_call" | custom-call | tf_op jit(solution)/shard_map/pallas_call | solution.py:69
  53.2 8.9 %shard_map.197 = f32[8,4,1024]{2,1,0:T(4,128)} custom-call(f32[4,1024]{1,0:T(4,128)} %fusion.45.x_ref), custom_call_target="tpu_custom_call" | custom-call | tf_op jit(solution)/shard_map/pallas_call | solution.py:69
  63.4 1.4 scatter_custom_fusion
  64.8 0.9 reshape.260.x_ref
  65.7 37.1 %shard_map.194.x_ref = bf16[16,10,1024]{2,1,0:T(8,128)(2,1)} custom-call(bf16[16,10,1024]{2,1,0:T(8,128)(2,1)} %reshape.260.x_ref), custom_call_target="tpu_custom_call" | custom-call | tf_op jit(solution)/shard_map/pallas_call | solution.py:144
  102.9 50.8 %shard_map.198 = bf16[4,16,10,1024]{3,2,1,0:T(8,128)(2,1)} custom-call(bf16[16,10,1024]{2,1,0:T(8,128)(2,1)} %shard_map.194.x_ref), custom_call_target="tpu_custom_call" | custom-call | tf_op jit(solution)/shard_map/pallas_call | solution.py:69
  153.7 2.6 reshape.268
  157.0 3.9 %fusion.62 = f32[640,704]{0,1:T(8,128)} fusion(bf16[640,1024]{1,0:T(8,128)(2,1)S(1)} %reshape.268, bf16[1024,704]{0,1:T(8,128)(2,1)} %all-gather.4.cloned.1.call-done), kind=kOutput, calls=%fused_computation.117 | convolution fusion | flops 922746880 | bytes 4554752 | tf_op jit(solution)/shard_map/dot_general | solution.py:202
  161.0 6.6 %convolution_convert_fusion = bf16[640,1024]{1,0:T(8,128)(2,1)S(1)} fusion(bf16[704,1024]{1,0:T(8,128)(2,1)} %all-gather.8.cloned.1.call-done, f32[640,704]{0,1:T(8,128)} %fusion.62, bf16[640,1024]{1,0:T(8,128)(2,1)S(1)} %reshape.268, bf16[1024,704]{0,1:T(8,128)(2,1)} %all-gather.6.cloned.1.call-done), kind=kOutput, calls=%fused_computation.12 | convolution fusion | flops 1850654720 | bytes 7307264 | tf_op jit(solution)/shard_map/dot_general | solution.py:205
  167.6 1.5 reshape.269.x_ref
  169.1 50.5 %shard_map.201 = bf16[4,16,10,1024]{3,2,1,0:T(8,128)(2,1)} custom-call(bf16[4,16,10,1024]{3,2,1,0:T(8,128)(2,1)} %reshape.269.x_ref), custom_call_target="tpu_custom_call" | custom-call | tf_op jit(solution)/shard_map/pallas_call | solution.py:144
  219.6 2.9 add_bitcast_fusion.x_ref
  222.5 52.9 %shard_map.202 = f32[16,10,1024]{2,1,0:T(8,128)} custom-call(f32[16,10,1024]{2,1,0:T(8,128)} %add_bitcast_fusion.x_ref), custom_call_target="tpu_custom_call" | custom-call | tf_op jit(solution)/shard_map/pallas_call | solution.py:144
  275.4 1.3 reshape.270
  279.8 3.3 %convolution_convert_fusion.1.x_ref = bf16[4,1024]{1,0:T(4,128)(2,1)} fusion(bf16[704,1024]{1,0:T(8,128)(2,1)} %all-gather.8.cloned.1.call-done, bf16[4,1024]{1,0:T(4,128)(2,1)S(1)} %fusion.24, bf16[1024,704]{0,1:T(8,128)(2,1)} %all-gather.6.cloned.1.call-done, f32[4,704]{1,0:T(4,128)S(1)} %fusion.63), kind=kOutput, calls=%fused_computation.14 | convolution fusion | flops 11566592 | bytes 2911232 | tf_op jit(solution)/shard_map/dot_general | solution.py:205
  283.1 17.3 %shard_map.199 = bf16[16,4,1024]{2,1,0:T(4,128)(2,1)} custom-call(bf16[4,1024]{1,0:T(4,128)(2,1)} %convolution_convert_fusion.1.x_ref), custom_call_target="tpu_custom_call" | custom-call | tf_op jit(solution)/shard_map/pallas_call | solution.py:69
  300.4 1.6 multiply_reduce_fusion.1.x_ref
  302.1 8.3 %shard_map.200 = f32[4,4,1024]{2,1,0:T(4,128)} custom-call(f32[4,1024]{1,0:T(4,128)} %multiply_reduce_fusion.1.x_ref), custom_call_target="tpu_custom_call" | custom-call | tf_op jit(solution)/shard_map/pallas_call | solution.py:69
  (111 shorter events, 18.5 us)
Async XLA Ops:
  7.2 45.2 %copy-start = (bf16[128,1024]{1,0:T(8,128)(2,1)S(1)}, bf16[128,1024]{1,0:T(8,128)(2,1)}, u32[]{:S(2)}) copy-start(bf16[128,1024]{1,0:T(8,128)(2,1)} %param.27) | copy-start | bytes 786436
  7.2 44.2 %copy-start.8 = (bf16[4,128]{1,0:T(4,128)(2,1)S(1)}, bf16[4,128]{1,0:T(4,128)(2,1)}, u32[]{:S(2)}) copy-start(bf16[4,128]{1,0:T(4,128)(2,1)} %param.20) | copy-start | bytes 3076
  7.2 44.9 %copy-start.5 = (s32[64,2]{0,1:T(2,128)S(1)}, s32[64,2]{0,1:T(2,128)}, u32[]{:S(2)}) copy-start(s32[64,2]{0,1:T(2,128)} %param.30) | copy-start | bytes 1540
  7.2 45.2 %copy-start.7 = (bf16[4,128]{1,0:T(4,128)(2,1)S(1)}, bf16[4,128]{1,0:T(4,128)(2,1)}, u32[]{:S(2)}) copy-start(bf16[4,128]{1,0:T(4,128)(2,1)} %param.21) | copy-start | bytes 3076
  7.2 55.3 %copy-start.2 = (bf16[64,1024]{1,0:T(8,128)(2,1)S(1)}, bf16[64,1024]{1,0:T(8,128)(2,1)}, u32[]{:S(2)}) copy-start(bf16[64,1024]{1,0:T(8,128)(2,1)} %param.29) | copy-start | bytes 393220
  7.2 55.4 %copy-start.4 = (f32[1024]{0:T(1024)S(1)}, f32[1024]{0:T(1024)}, u32[]{:S(2)}) copy-start(f32[1024]{0:T(1024)} %param.34) | copy-start | bytes 12292
  7.2 149.8 %all-gather.4.cloned.1.call-start = ((), (), s32[]{:S(2)}) async-start(), calls=%async_computation | async-start | bytes 1622016 | tf_op jit(solution)/shard_map/all_gather | solution.py:249
  8.0 153.0 %all-gather.6.cloned.1.call-start = ((), (), s32[]{:S(2)}) async-start(), calls=%async_computation.1 | async-start | bytes 1622016 | tf_op jit(solution)/shard_map/all_gather | solution.py:250
  8.7 152.3 %all-gather.8.cloned.1.call-start = ((), (), s32[]{:S(2)}) async-start(), calls=%async_computation.2 | async-start | bytes 1622016 | tf_op jit(solution)/shard_map/all_gather | solution.py:251
  62.9 39.9 %copy-start.3 = (f32[8,4,1024]{2,1,0:T(4,128)S(1)}, f32[8,4,1024]{2,1,0:T(4,128)}, u32[]{:S(2)}) copy-start(f32[8,4,1024]{2,1,0:T(4,128)} %shard_map.197) | copy-start | bytes 393220
  153.7 2.8 copy-start.9
  153.7 3.0 copy-start.10
  153.7 3.0 copy-start.11
  153.7 3.1 copy-start.6
  277.5 1.8 copy-start.1
Sparse Core Ops, SparseCore 0:
  10.2 36.4 all-gather.3
  48.8 33.4 all-gather.5
  84.5 33.4 all-gather.7

commit v4 on v2

--- a/solution.py
+++ b/solution.py
@@ -20,64 +20,91 @@
     return (lax.axis_index("seq"), peer)
 
 
-def gather_kernel(axis, count, stride, x_ref, out_ref, landed, send_sem, recv_sem):
+def share_kernel(axis, count, stride, modes, *refs):
+    width = len(modes)
+    sources = refs[:width]
+    outputs = refs[width : 2 * width]
+    landed = refs[2 * width : 3 * width]
+    send_sems = refs[3 * width : 4 * width]
+    recv_sems = refs[4 * width :]
     index = lax.axis_index(axis)
     me = lax.rem(index // stride, count)
     base = index - me * stride
 
-    def peer_of(step):
-        return peer_device(axis, base + lax.rem(me + step, count) * stride)
+    def member(slot):
+        return peer_device(axis, base + slot * stride)
+
+    def piece(which, slot):
+        return sources[which].at[slot] if modes[which] else sources[which]
 
     barrier = pltpu.get_barrier_semaphore()
 
     def greet(step, carry):
         pl.semaphore_signal(
-            barrier, inc=1, device_id=peer_of(step), device_id_type=pl.DeviceIdType.MESH
+            barrier,
+            inc=1,
+            device_id=member(lax.rem(me + step, count)),
+            device_id_type=pl.DeviceIdType.MESH,
         )
         return carry
 
     lax.fori_loop(1, count, greet, 0)
     pl.semaphore_wait(barrier, count - 1)
 
-    def transfer(step):
+    def outgoing(which, step):
+        target = lax.rem(me + step, count)
         return pltpu.make_async_remote_copy(
-            src_ref=x_ref,
-            dst_ref=landed.at[me],
-            send_sem=send_sem.at[step],
-            recv_sem=recv_sem.at[step],
-            device_id=peer_of(step),
+            src_ref=piece(which, target),
+            dst_ref=landed[which].at[me],
+            send_sem=send_sems[which].at[step],
+            recv_sem=recv_sems[which].at[step],
+            device_id=member(target),
             device_id_type=pl.DeviceIdType.MESH,
         )
 
+    def incoming(which, step):
+        source = lax.rem(me - step + count, count)
+        return pltpu.make_async_remote_copy(
+            src_ref=piece(which, source),
+            dst_ref=landed[which].at[source],
+            send_sem=send_sems[which].at[step],
+            recv_sem=recv_sems[which].at[step],
+            device_id=member(source),
+            device_id_type=pl.DeviceIdType.MESH,
+        )
+
     def launch(step, carry):
-        transfer(step).start()
+        for which in range(width):
+            outgoing(which, step).start()
         return carry
 
     lax.fori_loop(1, count, launch, 0)
-    landed[me] = x_ref[...]
+    for which in range(width):
+        landed[which][me] = piece(which, me)[...]
 
     def finish(step, carry):
-        transfer(step).wait()
+        for which in range(width):
+            outgoing(which, step).wait_send()
+            incoming(which, step).wait_recv()
         return carry
 
     lax.fori_loop(1, count, finish, 0)
-    out_ref[...] = landed[...]
-
-
-def axis_gather(x, axis, count, stride, collective_id):
-    stacked = (count,) + x.shape
+    for which in range(width):
+        outputs[which][...] = landed[which][...]
+
+
+def axis_share(payloads, modes, axis, count, stride, collective_id):
+    shapes = [x.shape if mode else (count,) + x.shape for x, mode in zip(payloads, modes)]
+    width = len(payloads)
     return pl.pallas_call(
-        functools.partial(gather_kernel, axis, count, stride),
-        out_shape=jax.ShapeDtypeStruct(stacked, x.dtype),
-        in_specs=[pl.BlockSpec(memory_space=pltpu.VMEM)],
-        out_specs=pl.BlockSpec(memory_space=pltpu.VMEM),
-        scratch_shapes=[
-            pltpu.VMEM(stacked, x.dtype),
-            pltpu.SemaphoreType.DMA((count,)),
-            pltpu.SemaphoreType.DMA((count,)),
-        ],
+        functools.partial(share_kernel, axis, count, stride, tuple(modes)),
+        out_shape=[jax.ShapeDtypeStruct(s, x.dtype) for s, x in zip(shapes, payloads)],
+        in_specs=[pl.BlockSpec(memory_space=pltpu.VMEM)] * width,
+        out_specs=[pl.BlockSpec(memory_space=pltpu.VMEM)] * width,
+        scratch_shapes=[pltpu.VMEM(s, x.dtype) for s, x in zip(shapes, payloads)]
+        + [pltpu.SemaphoreType.DMA((count,))] * (2 * width),
         compiler_params=pltpu.CompilerParams(collective_id=collective_id, has_side_effects=True),
-    )(x)
+    )(*payloads)
 
 
 def merge_softmax(stacked, rows, width):
@@ -113,36 +140,12 @@
     return flat_routes * capacity + slot_rank
 
 
-def pack_rows(normed, route_rows, capacity, shards):
-    flat_index = route_slots(route_rows, capacity)
-    source = jnp.repeat(normed, TOP, axis=0)
-    feature_width = normed.shape[1]
-    packed = jnp.zeros((EXPERTS * capacity, feature_width), jnp.bfloat16).at[flat_index].set(source)
-    packed = packed.reshape(EXPERTS, capacity, feature_width)
-    return (jnp.repeat(packed, shards, axis=0), flat_index)
-
-
 def expert_block(row_block, weights):
     gate_full, up_full, down_full = weights
     gate_pre = jnp.dot(row_block, gate_full, preferred_element_type=jnp.float32)
     up_pre = jnp.dot(row_block, up_full, preferred_element_type=jnp.float32)
     act = (jax.nn.gelu(gate_pre, approximate=True) * up_pre).astype(jnp.bfloat16)
     return jnp.dot(act, down_full, preferred_element_type=jnp.float32).astype(jnp.bfloat16)
-
-
-def expert_apply(received, weights):
-    peer_count, slot_count, feature_width = received.shape
-    partial_value = expert_block(received.reshape(peer_count * slot_count, feature_width), weights)
-    return partial_value.reshape(peer_count, slot_count, feature_width)
-
-
-def unpack_rows(returned, flat_index, shards, residual, gate_rows):
-    peer_count, slot_count, feature_width = returned.shape
-    summed = returned.astype(jnp.float32).reshape(EXPERTS, shards, slot_count, feature_width)
-    summed = jnp.sum(summed, axis=1).reshape(EXPERTS * slot_count, feature_width)
-    picked = jnp.take(summed, flat_index, axis=0).reshape(-1, TOP, feature_width)
-    combined = residual.astype(jnp.float32) + jnp.sum(gate_rows[..., None] * picked, axis=1)
-    return combined.astype(jnp.bfloat16)
 
 
 def body(
@@ -203,16 +206,27 @@
         "rhc,rchd->rhd", local_weights, value_rows, precision=lax.Precision.HIGHEST
     )
     tp_count = lax.axis_size("tp")
-    z_count = 16 if seq_count % 16 == 0 else seq_count
-    x_count = seq_count // z_count
     flat_width = request_count * heads_here
     packed_parts = pack_softmax(
         local_max.reshape(-1), local_sum.reshape(-1), local_acc.reshape(request_count, heads_here * HD)
     )
-    stage = merge_softmax(axis_gather(packed_parts, "seq", z_count, 1, 1), request_count, flat_width)
-    stage = merge_softmax(
-        axis_gather(pack_softmax(*stage), "seq", x_count, z_count, 2), request_count, flat_width
-    )
+    flat_index = route_slots(routes, CAP)
+    feature_width = normed_pre.shape[1]
+    slabs = (
+        jnp.zeros((EXPERTS * CAP, feature_width), jnp.bfloat16)
+        .at[flat_index]
+        .set(jnp.repeat(normed_pre, TOP, axis=0))
+        .reshape(EXPERTS, CAP, feature_width)
+    )
+    group_count = seq_count // shards
+    arrived, group_parts = axis_share(
+        [slabs, packed_parts], [True, False], "seq", group_count, shards, 1
+    )
+    group_merged = pack_softmax(*merge_softmax(group_parts, request_count, flat_width))
+    block_rows, block_parts = axis_share(
+        [arrived, group_merged], [False, False], "seq", shards, 1, 2
+    )
+    stage = merge_softmax(block_parts, request_count, flat_width)
     part_max = stage[0].reshape(request_count, heads_here)
     part_sum = stage[1].reshape(request_count, heads_here)
     part_acc = stage[2].reshape(request_count, heads_here, HD)
@@ -233,26 +247,35 @@
         .reshape(request_count, heads_width)
     )
     head_terms = jnp.dot(mixed_rows, out_proj, preferred_element_type=jnp.float32)
-    attended = jnp.sum(axis_gather(head_terms, "tp", tp_count, 1, 3), axis=0)
-    send_all, index_all = pack_rows(normed_pre, routes, CAP, shards)
-    received = lax.all_to_all(send_all, "seq", split_axis=0, concat_axis=0, tiled=True)
-    received, attended = lax.optimization_barrier((received, attended))
+    (head_all,) = axis_share([head_terms], [False], "tp", tp_count, 1, 3)
+    attended = jnp.sum(head_all, axis=0)
     decode_hidden = (decode_in.astype(jnp.float32) + attended).astype(jnp.bfloat16)
     normed_dec = rms_scale(decode_hidden, norm_gain)
-    expert_rows = expert_apply(received, weights)
-    expert_rows, normed_dec = lax.optimization_barrier((expert_rows, normed_dec))
-    back_all = lax.all_to_all(expert_rows, "seq", split_axis=0, concat_axis=0, tiled=True)
-    dec_parts = axis_gather(expert_block(normed_dec, weights), "seq", z_count, 1, 4)
-    z_base = (seq_index // z_count) * z_count
-    slot_expert = (z_base + jnp.arange(z_count, dtype=jnp.int32)) // shards
-    slot_gate = jnp.sum(
-        jnp.where(dec_routes[:, :, None] == slot_expert[None, None, :], dec_gates[:, :, None], 0.0),
-        axis=1,
-    )
-    z_terms = jnp.sum(slot_gate.T[:, :, None] * dec_parts.astype(jnp.float32), axis=0)
-    dec_terms = jnp.sum(axis_gather(z_terms, "seq", x_count, z_count, 5), axis=0)
+    block_count = block_rows.shape[0] * block_rows.shape[1] * block_rows.shape[2]
+    all_rows = jnp.concatenate([block_rows.reshape(block_count, feature_width), normed_dec], axis=0)
+    all_out = expert_block(all_rows, weights)
+    block_out = all_out[:block_count].reshape(block_rows.shape)
+    dec_part = all_out[block_count:]
+    part_rows, dec_block = axis_share(
+        [block_out, dec_part], [True, False], "seq", shards, 1, 4
+    )
+    summed = jnp.zeros(part_rows.shape[1:], jnp.float32)
+    dec_expert = jnp.zeros(dec_block.shape[1:], jnp.float32)
+    for part in range(shards):
+        summed = summed + part_rows[part].astype(jnp.float32)
+        dec_expert = dec_expert + dec_block[part].astype(jnp.float32)
+    my_expert = seq_index // shards
+    gate_here = jnp.sum(jnp.where(dec_routes == my_expert, dec_gates, 0.0), axis=1)
+    returned, dec_all = axis_share(
+        [summed, gate_here[:, None] * dec_expert], [True, False], "seq", group_count, shards, 5
+    )
+    dec_terms = jnp.sum(dec_all, axis=0)
     decode_out = (decode_hidden.astype(jnp.float32) + dec_terms).astype(jnp.bfloat16)
-    prefill_out = unpack_rows(back_all, index_all, shards, prefill_in, gates)
+    picked = jnp.take(returned.reshape(EXPERTS * CAP, -1), flat_index, axis=0)
+    picked = picked.reshape(-1, TOP, picked.shape[-1])
+    prefill_out = (
+        prefill_in.astype(jnp.float32) + jnp.sum(gates[..., None] * picked, axis=1)
+    ).astype(jnp.bfloat16)
     return (decode_out, prefill_out)
 
 

time: 311 us -> 283 us (0.910)
  the two profiles are of different devices: /device:TPU:1 before, /device:TPU:96 now
where the time goes in v4:
time: 283 us; the launch traced here: 282 us
  Pallas kernels  222 us (78%)
  local copies, waits for them, and re-layouts  17.4 us (6%)
  other arithmetic  14.5 us (5%)
  between operations  14.2 us (5%)
  matrix products  11.3 us (4%)
    pallas_call x5, Pallas kernels, axis_share(): pl.pallas_call(functools.partial(share_kernel, axis, count, stride, tuple...  222 us
  transfers between devices with their start and end apart: 3, of which 0 were waited for; matrix products, arithmetic and copies ran while one was open for 10% of the time, Pallas kernels for 37%

profile of v4, /device:TPU:96, one launch (start us, length us, event | category | flops | bytes accessed | tf_op | source)
XLA Modules:
  0.0 281.6 jit_solution(8346677119824224854)
XLA Ops:
  9.4 0.8 copy.40
  12.4 1.0 copy.56
  14.9 0.9 fusion.48
  16.2 0.9 reshape.249
  18.4 1.0 fusion.12
  19.5 1.0 fusion.14
  20.7 1.2 scatter_custom_fusion
  22.0 0.9 reshape.246.refs_0_
  23.5 39.7 %shard_map.194 = (bf16[16,10,1024]{2,1,0:T(8,128)(2,1)}, f32[16,8,128]{2,1,0:T(8,128)}) custom-call(bf16[16,10,1024]{2,1,0:T(8,128)(2,1)} %reshape.246.refs_0_, f32[8,128]{1,0:T(8,128)} %pad_maximum_fusion.5.refs_1_), custom_call_target="tpu_custom_call" | custom-call | tf_op jit(solution)/shard_map/pallas_call | solution.py:99
  63.1 1.0 slice_reduce_fusion.2
  64.7 0.9 multiply_reduce_fusion.1
  66.4 55.8 %shard_map.195 = (bf16[4,16,10,1024]{3,2,1,0:T(8,128)(2,1)}, f32[4,8,128]{2,1,0:T(8,128)}) custom-call(bf16[16,10,1024]{2,1,0:T(8,128)(2,1)} %get-tuple-element.10.refs_0_, f32[8,128]{1,0:T(8,128)} %pad_maximum_fusion.6.refs_1_), custom_call_target="tpu_custom_call" | custom-call | tf_op jit(solution)/shard_map/pallas_call | solution.py:99
  122.3 2.6 reshape.254
  127.2 8.9 %shard_map.196 = f32[8,4,1024]{2,1,0:T(4,128)} custom-call(f32[4,1024]{1,0:T(4,128)} %fusion.33.refs_0_), custom_call_target="tpu_custom_call" | custom-call | tf_op jit(solution)/shard_map/pallas_call | solution.py:99
  136.4 0.9 reduce_sum.130
  137.6 3.9 %fusion.11 = f32[644,704]{1,0:T(8,128)} fusion(bf16[1024,704]{0,1:T(8,128)(2,1)} %all-gather.4.cloned.1.call-done, bf16[4,1024]{1,0:T(4,128)(2,1)S(1)} %fusion.24, bf16[640,1024]{1,0:T(8,128)(2,1)S(1)} %reshape.254), kind=kOutput, calls=%fused_computation.18 | convolution fusion | flops 931151872 | bytes 4574208 | tf_op jit(solution)/shard_map/dot_general | solution.py:145
  141.5 5.4 %convolution_convert_fusion = bf16[644,1024]{1,0:T(8,128)(2,1)S(1)} fusion(bf16[704,1024]{1,0:T(8,128)(2,1)} %all-gather.8.cloned.1.call-done, f32[644,704]{1,0:T(8,128)} %fusion.11, bf16[1024,704]{0,1:T(8,128)(2,1)} %all-gather.6.cloned.1.call-done, bf16[4,1024]{1,0:T(4,128)(2,1)S(1)} %fusion.24, bf16[640,1024]{1,0:T(8,128)(2,1)S(1)} %reshape.254), kind=kOutput, calls=%fused_computation.12 | convolution fusion | flops 1864859136 | bytes 7334912 | tf_op jit(solution)/shard_map/dot_general | solution.py:148
  147.6 1.5 reshape.255.refs_0_
  149.1 53.2 %shard_map.197 = (bf16[4,16,10,1024]{3,2,1,0:T(8,128)(2,1)}, bf16[4,4,1024]{2,1,0:T(4,128)(2,1)}) custom-call(bf16[4,16,10,1024]{3,2,1,0:T(8,128)(2,1)} %reshape.255.refs_0_, bf16[4,1024]{1,0:T(4,128)(2,1)} %slice.71.refs_1_), custom_call_target="tpu_custom_call" | custom-call | tf_op jit(solution)/shard_map/pallas_call | solution.py:99
  202.3 2.9 %add_bitcast_fusion.refs_0_ = f32[16,10,1024]{2,1,0:T(8,128)} fusion(bf16[4,16,10,1024]{3,2,1,0:T(8,128)(2,1)} %get-tuple-element.14), kind=kLoop, calls=%fused_computation.17 | loop fusion | flops 1146880 | bytes 1966080 | tf_op jit(solution)/shard_map/add | solution.py:265
  205.9 64.6 %shard_map.198 = (f32[16,10,1024]{2,1,0:T(8,128)}, f32[16,4,1024]{2,1,0:T(4,128)}) custom-call(f32[16,10,1024]{2,1,0:T(8,128)} %add_bitcast_fusion.refs_0_, f32[4,1024]{1,0:T(4,128)} %bitcast_multiply_fusion.refs_1_), custom_call_target="tpu_custom_call" | custom-call | tf_op jit(solution)/shard_map/pallas_call | solution.py:99
  270.5 1.3 reshape.256
  271.8 0.8 gather_fusion
  272.9 0.8 multiply_reduce_fusion
  (107 shorter events, 15.7 us)
Async XLA Ops:
  7.2 119.2 %copy-start = (bf16[128,1024]{1,0:T(8,128)(2,1)S(1)}, bf16[128,1024]{1,0:T(8,128)(2,1)}, u32[]{:S(2)}) copy-start(bf16[128,1024]{1,0:T(8,128)(2,1)} %param.27) | copy-start | bytes 786436
  7.2 130.5 %all-gather.4.cloned.1.call-start = ((), (), s32[]{:S(2)}) async-start(), calls=%async_computation | async-start | bytes 1622016 | tf_op jit(solution)/shard_map/all_gather | solution.py:177
  7.9 133.6 %all-gather.6.cloned.1.call-start = ((), (), s32[]{:S(2)}) async-start(), calls=%async_computation.1 | async-start | bytes 1622016 | tf_op jit(solution)/shard_map/all_gather | solution.py:178
  8.7 132.9 %all-gather.8.cloned.1.call-start = ((), (), s32[]{:S(2)}) async-start(), calls=%async_computation.2 | async-start | bytes 1622016 | tf_op jit(solution)/shard_map/all_gather | solution.py:179
  66.4 59.2 %copy-start.9 = (bf16[4,128]{1,0:T(4,128)(2,1)S(1)}, bf16[4,128]{1,0:T(4,128)(2,1)}, u32[]{:S(2)}) copy-start(bf16[4,128]{1,0:T(4,128)(2,1)} %param.20) | copy-start | bytes 3076
  66.4 60.0 %copy-start.8 = (bf16[4,128]{1,0:T(4,128)(2,1)S(1)}, bf16[4,128]{1,0:T(4,128)(2,1)}, u32[]{:S(2)}) copy-start(bf16[4,128]{1,0:T(4,128)(2,1)} %param.21) | copy-start | bytes 3076
  122.2 2.7 copy-start.6
  122.2 13.9 %copy-start.5 = (s32[64,2]{0,1:T(2,128)S(1)}, s32[64,2]{0,1:T(2,128)}, u32[]{:S(2)}) copy-start(s32[64,2]{0,1:T(2,128)} %param.30) | copy-start | bytes 1540
  122.2 14.1 %copy-start.10 = (f32[64,2]{0,1:T(2,128)S(1)}, f32[64,2]{0,1:T(2,128)}, u32[]{:S(2)}) copy-start(f32[64,2]{0,1:T(2,128)} %param.31) | copy-start | bytes 1540
  122.2 15.1 %copy-start.11 = (f32[4,2]{0,1:T(2,128)S(1)}, f32[4,2]{0,1:T(2,128)}, u32[]{:S(2)}) copy-start(f32[4,2]{0,1:T(2,128)} %param.33) | copy-start | bytes 100
  122.3 15.1 %copy-start.12 = (s32[4,2]{0,1:T(2,128)S(1)}, s32[4,2]{0,1:T(2,128)}, u32[]{:S(2)}) copy-start(s32[4,2]{0,1:T(2,128)} %param.32) | copy-start | bytes 100
  122.3 15.2 %copy-start.7 = (bf16[4,1024]{1,0:T(4,128)(2,1)S(1)}, bf16[4,1024]{1,0:T(4,128)(2,1)}, u32[]{:S(2)}) copy-start(bf16[4,1024]{1,0:T(4,128)(2,1)} %param.28) | copy-start | bytes 24580
  122.3 15.3 %copy-start.4 = (f32[1024]{0:T(1024)S(1)}, f32[1024]{0:T(1024)}, u32[]{:S(2)}) copy-start(f32[1024]{0:T(1024)} %param.34) | copy-start | bytes 12292
  202.3 2.9 %copy-start.3 = (bf16[4,4,1024]{2,1,0:T(4,128)(2,1)S(1)}, bf16[4,4,1024]{2,1,0:T(4,128)(2,1)}, u32[]{:S(2)}) copy-start(bf16[4,4,1024]{2,1,0:T(4,128)(2,1)} %get-tuple-element.15) | copy-start | bytes 98308
  271.8 2.0 copy-start.1
  272.6 1.8 copy-start.2
Sparse Core Ops, SparseCore 0:
  10.1 35.7 all-gather.3
  48.0 33.4 all-gather.5
  83.6 33.4 all-gather.7

commit v5 on v4

--- a/solution.py
+++ b/solution.py
@@ -105,6 +105,150 @@
         + [pltpu.SemaphoreType.DMA((count,))] * (2 * width),
         compiler_params=pltpu.CompilerParams(collective_id=collective_id, has_side_effects=True),
     )(*payloads)
+
+
+def outbound_kernel(groups, shards, slab_ref, part_ref, rows_out, parts_out,
+                    far_rows, far_parts, near_rows, near_parts,
+                    far_send, far_recv, far_psend, far_precv,
+                    near_send, near_recv, near_psend, near_precv, local_sem):
+    index = lax.axis_index("seq")
+    far_me = lax.rem(index // shards, groups)
+    far_base = index - far_me * shards
+    near_me = lax.rem(index, shards)
+    near_base = index - near_me
+
+    def far_member(slot):
+        return peer_device("seq", far_base + slot * shards)
+
+    def near_member(slot):
+        return peer_device("seq", near_base + slot)
+
+    barrier = pltpu.get_barrier_semaphore()
+
+    def greet_far(step, carry):
+        pl.semaphore_signal(barrier, inc=1, device_id=far_member(lax.rem(far_me + step, groups)),
+                            device_id_type=pl.DeviceIdType.MESH)
+        return carry
+
+    def greet_near(step, carry):
+        pl.semaphore_signal(barrier, inc=1, device_id=near_member(lax.rem(near_me + step, shards)),
+                            device_id_type=pl.DeviceIdType.MESH)
+        return carry
+
+    lax.fori_loop(1, groups, greet_far, 0)
+    lax.fori_loop(1, shards, greet_near, 0)
+    pl.semaphore_wait(barrier, groups + shards - 2)
+
+    def far_copy(step, slot, landed_slot):
+        return (
+            pltpu.make_async_remote_copy(
+                src_ref=slab_ref.at[slot], dst_ref=far_rows.at[landed_slot],
+                send_sem=far_send.at[step], recv_sem=far_recv.at[step],
+                device_id=far_member(slot), device_id_type=pl.DeviceIdType.MESH),
+            pltpu.make_async_remote_copy(
+                src_ref=part_ref, dst_ref=far_parts.at[landed_slot],
+                send_sem=far_psend.at[step], recv_sem=far_precv.at[step],
+                device_id=far_member(slot), device_id_type=pl.DeviceIdType.MESH),
+        )
+
+    def far_start(step, carry):
+        for copy in far_copy(step, lax.rem(far_me + step, groups), far_me):
+            copy.start()
+        return carry
+
+    lax.fori_loop(1, groups, far_start, 0)
+    own_slab = pltpu.make_async_copy(slab_ref.at[far_me], far_rows.at[far_me], local_sem.at[0])
+    own_part = pltpu.make_async_copy(part_ref, far_parts.at[far_me], local_sem.at[1])
+    own_slab.start()
+    own_part.start()
+
+    def near_copy(step, slab):
+        target = lax.rem(near_me + step, shards)
+        return pltpu.make_async_remote_copy(
+            src_ref=far_rows.at[slab], dst_ref=near_rows.at[near_me, slab],
+            send_sem=near_send.at[step, slab], recv_sem=near_recv.at[step, slab],
+            device_id=near_member(target), device_id_type=pl.DeviceIdType.MESH)
+
+    def forward(slab):
+        for step in range(1, shards):
+            near_copy(step, slab).start()
+
+    own_slab.wait()
+    forward(far_me)
+
+    def far_finish(step, carry):
+        source = lax.rem(far_me - step + groups, groups)
+        rows_copy, parts_copy = far_copy(step, source, source)
+        rows_copy.wait_send()
+        rows_copy.wait_recv()
+        forward(source)
+        parts_copy.wait_send()
+        parts_copy.wait_recv()
+        return carry
+
+    lax.fori_loop(1, groups, far_finish, 0)
+    own_part.wait()
+    own_rows = pltpu.make_async_copy(far_rows, near_rows.at[near_me], local_sem.at[2])
+    own_parts = pltpu.make_async_copy(far_parts, near_parts.at[near_me], local_sem.at[3])
+    own_rows.start()
+    own_parts.start()
+
+    def near_parts_copy(step, slot):
+        return pltpu.make_async_remote_copy(
+            src_ref=far_parts, dst_ref=near_parts.at[slot],
+            send_sem=near_psend.at[step], recv_sem=near_precv.at[step],
+            device_id=near_member(lax.rem(near_me + step, shards)),
+            device_id_type=pl.DeviceIdType.MESH)
+
+    for step in range(1, shards):
+        near_parts_copy(step, near_me).start()
+
+    def near_finish(step, carry):
+        source = lax.rem(near_me - step + shards, shards)
+
+        def per_slab(slab, inner):
+            copy = pltpu.make_async_remote_copy(
+                src_ref=far_rows.at[slab], dst_ref=near_rows.at[source, slab],
+                send_sem=near_send.at[step, slab], recv_sem=near_recv.at[step, slab],
+                device_id=near_member(source), device_id_type=pl.DeviceIdType.MESH)
+            copy.wait_send()
+            copy.wait_recv()
+            return inner
+
+        lax.fori_loop(0, groups, per_slab, 0)
+        parts_copy = near_parts_copy(step, source)
+        parts_copy.wait_send()
+        parts_copy.wait_recv()
+        return carry
+
+    lax.fori_loop(1, shards, near_finish, 0)
+    own_rows.wait()
+    own_parts.wait()
+    rows_out[...] = near_rows[...]
+    parts_out[...] = near_parts[...]
+
+
+def outbound(slabs, parts, groups, shards, collective_id):
+    rows_shape = (shards,) + slabs.shape
+    parts_shape = (shards, groups) + parts.shape
+    return pl.pallas_call(
+        functools.partial(outbound_kernel, groups, shards),
+        out_shape=[jax.ShapeDtypeStruct(rows_shape, slabs.dtype),
+                   jax.ShapeDtypeStruct(parts_shape, parts.dtype)],
+        in_specs=[pl.BlockSpec(memory_space=pltpu.VMEM)] * 2,
+        out_specs=[pl.BlockSpec(memory_space=pltpu.VMEM)] * 2,
+        scratch_shapes=[
+            pltpu.VMEM(slabs.shape, slabs.dtype),
+            pltpu.VMEM((groups,) + parts.shape, parts.dtype),
+            pltpu.VMEM(rows_shape, slabs.dtype),
+            pltpu.VMEM(parts_shape, parts.dtype),
+        ]
+        + [pltpu.SemaphoreType.DMA((groups,))] * 4
+        + [pltpu.SemaphoreType.DMA((shards, groups))] * 2
+        + [pltpu.SemaphoreType.DMA((shards,))] * 2
+        + [pltpu.SemaphoreType.DMA((4,))],
+        compiler_params=pltpu.CompilerParams(collective_id=collective_id, has_side_effects=True),
+    )(slabs, parts)
 
 
 def merge_softmax(stacked, rows, width):
@@ -219,14 +363,10 @@
         .reshape(EXPERTS, CAP, feature_width)
     )
     group_count = seq_count // shards
-    arrived, group_parts = axis_share(
-        [slabs, packed_parts], [True, False], "seq", group_count, shards, 1
-    )
-    group_merged = pack_softmax(*merge_softmax(group_parts, request_count, flat_width))
-    block_rows, block_parts = axis_share(
-        [arrived, group_merged], [False, False], "seq", shards, 1, 2
-    )
-    stage = merge_softmax(block_parts, request_count, flat_width)
+    block_rows, block_parts = outbound(slabs, packed_parts, group_count, shards, 1)
+    stage = merge_softmax(
+        block_parts.reshape((-1,) + packed_parts.shape), request_count, flat_width
+    )
     part_max = stage[0].reshape(request_count, heads_here)
     part_sum = stage[1].reshape(request_count, heads_here)
     part_acc = stage[2].reshape(request_count, heads_here, HD)

time: 283 us -> 280 us (0.989)
    pallas_call x5 -> x3, Pallas kernels: 222 us -> 125 us  [axis_share(): pl.pallas_call(functools.partial(share_kernel, axis, count, stride, tuple...]
    pallas_call x0 -> x1, Pallas kernels: none -> 96.1 us  [outbound(): pl.pallas_call(functools.partial(outbound_kernel, groups, shards), out_sh...]
  transfers between devices with their start and end apart: 3 -> 3, of which waited for: 0 -> 0; matrix products, arithmetic and copies ran while one was open for 10% -> 9% of each run, Pallas kernels for 37% -> 38%
where the time goes in v5:
time: 280 us; the launch traced here: 279 us
  Pallas kernels  221 us (79%)
  local copies, waits for them, and re-layouts  17.3 us (6%)
  between operations  14.1 us (5%)
  other arithmetic  13.2 us (5%)
  matrix products  11.2 us (4%)
    pallas_call x3, Pallas kernels, axis_share(): pl.pallas_call(functools.partial(share_kernel, axis, count, stride, tuple...  125 us
    pallas_call x1, Pallas kernels, outbound(): pl.pallas_call(functools.partial(outbound_kernel, groups, shards), out_sh...  96.1 us
  transfers between devices with their start and end apart: 3, of which 0 were waited for; matrix products, arithmetic and copies ran while one was open for 9% of the time, Pallas kernels for 38%

profile of v5, /device:TPU:96, one launch (start us, length us, event | category | flops | bytes accessed | tf_op | source)
XLA Modules:
  0.0 278.8 jit_solution(6595181159682416393)
XLA Ops:
  9.4 0.8 copy.32
  10.9 0.8 reshape.272
  11.6 0.8 reshape.239
  12.4 1.0 copy.45
  14.9 0.9 fusion.48
  16.2 0.9 reshape.241
  18.4 1.0 fusion.12
  19.5 1.0 fusion.14
  20.7 1.2 scatter_custom_fusion
  22.0 0.9 reshape.238.slab_ref
  23.5 96.1 %shard_map.194 = (bf16[4,16,10,1024]{3,2,1,0:T(8,128)(2,1)}, f32[4,16,8,128]{3,2,1,0:T(8,128)}) custom-call(bf16[16,10,1024]{2,1,0:T(8,128)(2,1)} %reshape.238.slab_ref, f32[8,128]{1,0:T(8,128)} %pad_maximum_fusion.5.part_ref), custom_call_target="tpu_custom_call" | custom-call | tf_op jit(solution)/shard_map/pallas_call | solution.py:234
  119.6 1.1 slice_reduce_fusion.1
  122.8 1.1 fusion.18
  124.7 9.1 %shard_map.195 = f32[8,4,1024]{2,1,0:T(4,128)} custom-call(f32[4,1024]{1,0:T(4,128)} %fusion.33.refs_0_), custom_call_target="tpu_custom_call" | custom-call | tf_op jit(solution)/shard_map/pallas_call | solution.py:99
  133.8 2.6 reshape.246
  137.0 3.9 %fusion.11 = f32[644,704]{1,0:T(8,128)} fusion(bf16[1024,704]{0,1:T(8,128)(2,1)} %all-gather.4.cloned.1.call-done, bf16[4,1024]{1,0:T(4,128)(2,1)S(1)} %fusion.25, bf16[640,1024]{1,0:T(8,128)(2,1)S(1)} %reshape.246), kind=kOutput, calls=%fused_computation.18 | convolution fusion | flops 931151872 | bytes 4574208 | tf_op jit(solution)/shard_map/dot_general | solution.py:289
  140.9 5.3 %convolution_convert_fusion = bf16[644,1024]{1,0:T(8,128)(2,1)S(1)} fusion(bf16[704,1024]{1,0:T(8,128)(2,1)} %all-gather.8.cloned.1.call-done, f32[644,704]{1,0:T(8,128)} %fusion.11, bf16[1024,704]{0,1:T(8,128)(2,1)} %all-gather.6.cloned.1.call-done, bf16[4,1024]{1,0:T(4,128)(2,1)S(1)} %fusion.25, bf16[640,1024]{1,0:T(8,128)(2,1)S(1)} %reshape.246), kind=kOutput, calls=%fused_computation.12 | convolution fusion | flops 1864859136 | bytes 7334912 | tf_op jit(solution)/shard_map/dot_general | solution.py:292
  147.0 1.5 reshape.247.refs_0_
  148.5 53.2 %shard_map.196 = (bf16[4,16,10,1024]{3,2,1,0:T(8,128)(2,1)}, bf16[4,4,1024]{2,1,0:T(4,128)(2,1)}) custom-call(bf16[4,16,10,1024]{3,2,1,0:T(8,128)(2,1)} %reshape.247.refs_0_, bf16[4,1024]{1,0:T(4,128)(2,1)} %slice.62.refs_1_), custom_call_target="tpu_custom_call" | custom-call | tf_op jit(solution)/shard_map/pallas_call | solution.py:99
  201.7 2.9 %add_bitcast_fusion.refs_0_ = f32[16,10,1024]{2,1,0:T(8,128)} fusion(bf16[4,16,10,1024]{3,2,1,0:T(8,128)(2,1)} %get-tuple-element.10), kind=kLoop, calls=%fused_computation.17 | loop fusion | flops 1146880 | bytes 1966080 | tf_op jit(solution)/shard_map/add | solution.py:405
  205.2 62.4 %shard_map.197 = (f32[16,10,1024]{2,1,0:T(8,128)}, f32[16,4,1024]{2,1,0:T(4,128)}) custom-call(f32[16,10,1024]{2,1,0:T(8,128)} %add_bitcast_fusion.refs_0_, f32[4,1024]{1,0:T(4,128)} %bitcast_multiply_fusion.refs_1_), custom_call_target="tpu_custom_call" | custom-call | tf_op jit(solution)/shard_map/pallas_call | solution.py:99
  267.6 1.3 reshape.248
  269.0 0.8 gather_fusion
  270.1 0.8 multiply_reduce_fusion
  (95 shorter events, 13.3 us)
Async XLA Ops:
  7.2 116.7 %copy-start = (bf16[128,1024]{1,0:T(8,128)(2,1)S(1)}, bf16[128,1024]{1,0:T(8,128)(2,1)}, u32[]{:S(2)}) copy-start(bf16[128,1024]{1,0:T(8,128)(2,1)} %param.27) | copy-start | bytes 786436
  7.2 129.8 %all-gather.4.cloned.1.call-start = ((), (), s32[]{:S(2)}) async-start(), calls=%async_computation | async-start | bytes 1622016 | tf_op jit(solution)/shard_map/all_gather | solution.py:321
  7.9 133.0 %all-gather.6.cloned.1.call-start = ((), (), s32[]{:S(2)}) async-start(), calls=%async_computation.1 | async-start | bytes 1622016 | tf_op jit(solution)/shard_map/all_gather | solution.py:322
  8.7 132.3 %all-gather.8.cloned.1.call-start = ((), (), s32[]{:S(2)}) async-start(), calls=%async_computation.2 | async-start | bytes 1622016 | tf_op jit(solution)/shard_map/all_gather | solution.py:323
  19.4 102.6 %copy-start.9 = (bf16[4,128]{1,0:T(4,128)(2,1)S(1)}, bf16[4,128]{1,0:T(4,128)(2,1)}, u32[]{:S(2)}) copy-start(bf16[4,128]{1,0:T(4,128)(2,1)} %param.20) | copy-start | bytes 3076
  20.5 103.4 %copy-start.8 = (bf16[4,128]{1,0:T(4,128)(2,1)S(1)}, bf16[4,128]{1,0:T(4,128)(2,1)}, u32[]{:S(2)}) copy-start(bf16[4,128]{1,0:T(4,128)(2,1)} %param.21) | copy-start | bytes 3076
  123.9 12.6 %copy-start.6 = (s32[64,2]{0,1:T(2,128)S(1)}, s32[64,2]{0,1:T(2,128)}, u32[]{:S(2)}) copy-start(s32[64,2]{0,1:T(2,128)} %param.30) | copy-start | bytes 1540
  123.9 12.7 %copy-start.10 = (f32[64,2]{0,1:T(2,128)S(1)}, f32[64,2]{0,1:T(2,128)}, u32[]{:S(2)}) copy-start(f32[64,2]{0,1:T(2,128)} %param.31) | copy-start | bytes 1540
  123.9 12.9 %copy-start.11 = (f32[4,2]{0,1:T(2,128)S(1)}, f32[4,2]{0,1:T(2,128)}, u32[]{:S(2)}) copy-start(f32[4,2]{0,1:T(2,128)} %param.33) | copy-start | bytes 100
  123.9 12.9 %copy-start.12 = (s32[4,2]{0,1:T(2,128)S(1)}, s32[4,2]{0,1:T(2,128)}, u32[]{:S(2)}) copy-start(s32[4,2]{0,1:T(2,128)} %param.32) | copy-start | bytes 100
  123.9 12.9 %copy-start.7 = (bf16[4,1024]{1,0:T(4,128)(2,1)S(1)}, bf16[4,1024]{1,0:T(4,128)(2,1)}, u32[]{:S(2)}) copy-start(bf16[4,1024]{1,0:T(4,128)(2,1)} %param.28) | copy-start | bytes 24580
  124.7 12.3 %copy-start.5 = (f32[1024]{0:T(1024)S(1)}, f32[1024]{0:T(1024)}, u32[]{:S(2)}) copy-start(f32[1024]{0:T(1024)} %param.34) | copy-start | bytes 12292
  133.7 2.9 %copy-start.2 = (f32[8,4,1024]{2,1,0:T(4,128)S(1)}, f32[8,4,1024]{2,1,0:T(4,128)}, u32[]{:S(2)}) copy-start(f32[8,4,1024]{2,1,0:T(4,128)} %shard_map.195) | copy-start | bytes 393220
  201.7 2.9 %copy-start.4 = (bf16[4,4,1024]{2,1,0:T(4,128)(2,1)S(1)}, bf16[4,4,1024]{2,1,0:T(4,128)(2,1)}, u32[]{:S(2)}) copy-start(bf16[4,4,1024]{2,1,0:T(4,128)(2,1)} %get-tuple-element.11) | copy-start | bytes 98308
  269.0 2.0 copy-start.1
  269.8 1.8 copy-start.3
Sparse Core Ops, SparseCore 0:
  10.1 35.7 all-gather.3
  48.0 33.4 all-gather.5
  83.6 33.4 all-gather.7

commit v6 on v5

--- a/solution.py
+++ b/solution.py
@@ -108,14 +108,16 @@
 
 
 def outbound_kernel(groups, shards, slab_ref, part_ref, rows_out, parts_out,
-                    far_rows, far_parts, near_rows, near_parts,
+                    far_parts, near_rows, near_parts,
                     far_send, far_recv, far_psend, far_precv,
                     near_send, near_recv, near_psend, near_precv, local_sem):
     index = lax.axis_index("seq")
     far_me = lax.rem(index // shards, groups)
     far_base = index - far_me * shards
-    near_me = lax.rem(index, shards)
-    near_base = index - near_me
+    place = lax.rem(index, shards)
+    near_base = index - place
+    has_right = place < shards - 1
+    has_left = place > 0
 
     def far_member(slot):
         return peer_device("seq", far_base + slot * shards)
@@ -131,7 +133,7 @@
         return carry
 
     def greet_near(step, carry):
-        pl.semaphore_signal(barrier, inc=1, device_id=near_member(lax.rem(near_me + step, shards)),
+        pl.semaphore_signal(barrier, inc=1, device_id=near_member(lax.rem(place + step, shards)),
                             device_id_type=pl.DeviceIdType.MESH)
         return carry
 
@@ -142,7 +144,7 @@
     def far_copy(step, slot, landed_slot):
         return (
             pltpu.make_async_remote_copy(
-                src_ref=slab_ref.at[slot], dst_ref=far_rows.at[landed_slot],
+                src_ref=slab_ref.at[slot], dst_ref=near_rows.at[place, landed_slot],
                 send_sem=far_send.at[step], recv_sem=far_recv.at[step],
                 device_id=far_member(slot), device_id_type=pl.DeviceIdType.MESH),
             pltpu.make_async_remote_copy(
@@ -157,72 +159,94 @@
         return carry
 
     lax.fori_loop(1, groups, far_start, 0)
-    own_slab = pltpu.make_async_copy(slab_ref.at[far_me], far_rows.at[far_me], local_sem.at[0])
+    own_slab = pltpu.make_async_copy(slab_ref.at[far_me], near_rows.at[place, far_me], local_sem.at[0])
     own_part = pltpu.make_async_copy(part_ref, far_parts.at[far_me], local_sem.at[1])
     own_slab.start()
     own_part.start()
 
-    def near_copy(step, slab):
-        target = lax.rem(near_me + step, shards)
+    def chain_copy(direction, origin, slab):
         return pltpu.make_async_remote_copy(
-            src_ref=far_rows.at[slab], dst_ref=near_rows.at[near_me, slab],
-            send_sem=near_send.at[step, slab], recv_sem=near_recv.at[step, slab],
-            device_id=near_member(target), device_id_type=pl.DeviceIdType.MESH)
-
-    def forward(slab):
-        for step in range(1, shards):
-            near_copy(step, slab).start()
+            src_ref=near_rows.at[origin, slab], dst_ref=near_rows.at[origin, slab],
+            send_sem=near_send.at[direction, origin, slab], recv_sem=near_recv.at[origin, slab],
+            device_id=near_member(place + 1 - 2 * direction), device_id_type=pl.DeviceIdType.MESH)
+
+    def pass_on(origin, slab, to_right, to_left):
+        @pl.when(to_right)
+        def _():
+            chain_copy(0, origin, slab).start()
+
+        @pl.when(to_left)
+        def _():
+            chain_copy(1, origin, slab).start()
 
     own_slab.wait()
-    forward(far_me)
+    pass_on(place, far_me, has_right, has_left)
 
     def far_finish(step, carry):
         source = lax.rem(far_me - step + groups, groups)
         rows_copy, parts_copy = far_copy(step, source, source)
         rows_copy.wait_send()
         rows_copy.wait_recv()
-        forward(source)
+        pass_on(place, source, has_right, has_left)
         parts_copy.wait_send()
         parts_copy.wait_recv()
         return carry
 
     lax.fori_loop(1, groups, far_finish, 0)
     own_part.wait()
-    own_rows = pltpu.make_async_copy(far_rows, near_rows.at[near_me], local_sem.at[2])
-    own_parts = pltpu.make_async_copy(far_parts, near_parts.at[near_me], local_sem.at[3])
-    own_rows.start()
+    own_parts = pltpu.make_async_copy(far_parts, near_parts.at[place], local_sem.at[2])
     own_parts.start()
 
     def near_parts_copy(step, slot):
         return pltpu.make_async_remote_copy(
             src_ref=far_parts, dst_ref=near_parts.at[slot],
             send_sem=near_psend.at[step], recv_sem=near_precv.at[step],
-            device_id=near_member(lax.rem(near_me + step, shards)),
+            device_id=near_member(lax.rem(place + step, shards)),
             device_id_type=pl.DeviceIdType.MESH)
 
     for step in range(1, shards):
-        near_parts_copy(step, near_me).start()
-
-    def near_finish(step, carry):
-        source = lax.rem(near_me - step + shards, shards)
-
-        def per_slab(slab, inner):
-            copy = pltpu.make_async_remote_copy(
-                src_ref=far_rows.at[slab], dst_ref=near_rows.at[source, slab],
-                send_sem=near_send.at[step, slab], recv_sem=near_recv.at[step, slab],
-                device_id=near_member(source), device_id_type=pl.DeviceIdType.MESH)
-            copy.wait_send()
-            copy.wait_recv()
-            return inner
-
-        lax.fori_loop(0, groups, per_slab, 0)
-        parts_copy = near_parts_copy(step, source)
+        near_parts_copy(step, place).start()
+
+    for distance in range(1, shards):
+        def relay(slab, carry, distance=distance):
+            from_left = place - distance
+            from_right = place + distance
+
+            @pl.when(from_left >= 0)
+            def _():
+                chain_copy(0, from_left, slab).wait_recv()
+                pass_on(from_left, slab, has_right, False)
+
+            @pl.when(from_right < shards)
+            def _():
+                chain_copy(1, from_right, slab).wait_recv()
+                pass_on(from_right, slab, False, has_left)
+
+            return carry
+
+        lax.fori_loop(0, groups, relay, 0)
+
+    for origin in range(shards):
+        def drain(slab, carry, origin=origin):
+            @pl.when((origin <= place) & has_right)
+            def _():
+                chain_copy(0, origin, slab).wait_send()
+
+            @pl.when((origin >= place) & has_left)
+            def _():
+                chain_copy(1, origin, slab).wait_send()
+
+            return carry
+
+        lax.fori_loop(0, groups, drain, 0)
+
+    def parts_finish(step, carry):
+        parts_copy = near_parts_copy(step, lax.rem(place - step + shards, shards))
         parts_copy.wait_send()
         parts_copy.wait_recv()
         return carry
 
-    lax.fori_loop(1, shards, near_finish, 0)
-    own_rows.wait()
+    lax.fori_loop(1, shards, parts_finish, 0)
     own_parts.wait()
     rows_out[...] = near_rows[...]
     parts_out[...] = near_parts[...]
@@ -238,13 +262,12 @@
         in_specs=[pl.BlockSpec(memory_space=pltpu.VMEM)] * 2,
         out_specs=[pl.BlockSpec(memory_space=pltpu.VMEM)] * 2,
         scratch_shapes=[
-            pltpu.VMEM(slabs.shape, slabs.dtype),
             pltpu.VMEM((groups,) + parts.shape, parts.dtype),
             pltpu.VMEM(rows_shape, slabs.dtype),
             pltpu.VMEM(parts_shape, parts.dtype),
         ]
         + [pltpu.SemaphoreType.DMA((groups,))] * 4
-        + [pltpu.SemaphoreType.DMA((shards, groups))] * 2
+        + [pltpu.SemaphoreType.DMA((2, shards, groups)), pltpu.SemaphoreType.DMA((shards, groups))]
         + [pltpu.SemaphoreType.DMA((shards,))] * 2
         + [pltpu.SemaphoreType.DMA((4,))],
         compiler_params=pltpu.CompilerParams(collective_id=collective_id, has_side_effects=True),

time: 280 us -> 270 us (0.964)
  the two profiles are of different devices: /device:TPU:96 before, /device:TPU:99 now
where the time goes in v6:
time: 270 us; the launch traced here: 269 us
  Pallas kernels  211 us (78%)
  local copies, waits for them, and re-layouts  17.3 us (6%)
  between operations  14.1 us (5%)
  other arithmetic  13.2 us (5%)
  matrix products  11.2 us (4%)
    pallas_call x3, Pallas kernels, axis_share(): pl.pallas_call(functools.partial(share_kernel, axis, count, stride, tuple...  128 us
    pallas_call x1, Pallas kernels, outbound(): pl.pallas_call(functools.partial(outbound_kernel, groups, shards), out_sh...  82.8 us
  transfers between devices with their start and end apart: 3, of which 0 were waited for; matrix products, arithmetic and copies ran while one was open for 10% of the time, Pallas kernels for 34%

profile of v6, /device:TPU:99, one launch (start us, length us, event | category | flops | bytes accessed | tf_op | source)
XLA Modules:
  0.0 268.7 jit_solution(1218116826267287933)
XLA Ops:
  9.4 0.8 copy.32
  10.9 0.8 reshape.272
  11.6 0.8 reshape.239
  12.4 1.0 copy.45
  14.9 0.9 fusion.48
  16.2 0.9 reshape.241
  18.4 1.0 fusion.12
  19.5 1.0 fusion.14
  20.7 1.2 scatter_custom_fusion
  22.0 0.9 reshape.238.slab_ref
  23.5 82.8 %shard_map.194 = (bf16[4,16,10,1024]{3,2,1,0:T(8,128)(2,1)}, f32[4,16,8,128]{3,2,1,0:T(8,128)}) custom-call(bf16[16,10,1024]{2,1,0:T(8,128)(2,1)} %reshape.238.slab_ref, f32[8,128]{1,0:T(8,128)} %pad_maximum_fusion.5.part_ref), custom_call_target="tpu_custom_call" | custom-call | tf_op jit(solution)/shard_map/pallas_call | solution.py:258
  106.4 1.1 slice_reduce_fusion.1
  109.5 1.1 fusion.18
  111.4 9.6 %shard_map.195 = f32[8,4,1024]{2,1,0:T(4,128)} custom-call(f32[4,1024]{1,0:T(4,128)} %fusion.33.refs_0_), custom_call_target="tpu_custom_call" | custom-call | tf_op jit(solution)/shard_map/pallas_call | solution.py:99
  121.0 2.6 reshape.246
  124.3 3.9 %fusion.11 = f32[644,704]{1,0:T(8,128)} fusion(bf16[1024,704]{0,1:T(8,128)(2,1)} %all-gather.4.cloned.1.call-done, bf16[4,1024]{1,0:T(4,128)(2,1)S(1)} %fusion.25, bf16[640,1024]{1,0:T(8,128)(2,1)S(1)} %reshape.246), kind=kOutput, calls=%fused_computation.18 | convolution fusion | flops 931151872 | bytes 4574208 | tf_op jit(solution)/shard_map/dot_general | solution.py:312
  128.2 5.3 %convolution_convert_fusion = bf16[644,1024]{1,0:T(8,128)(2,1)S(1)} fusion(bf16[704,1024]{1,0:T(8,128)(2,1)} %all-gather.8.cloned.1.call-done, f32[644,704]{1,0:T(8,128)} %fusion.11, bf16[1024,704]{0,1:T(8,128)(2,1)} %all-gather.6.cloned.1.call-done, bf16[4,1024]{1,0:T(4,128)(2,1)S(1)} %fusion.25, bf16[640,1024]{1,0:T(8,128)(2,1)S(1)} %reshape.246), kind=kOutput, calls=%fused_computation.12 | convolution fusion | flops 1864859136 | bytes 7334912 | tf_op jit(solution)/shard_map/dot_general | solution.py:315
  134.2 1.5 reshape.247.refs_0_
  135.7 52.3 %shard_map.196 = (bf16[4,16,10,1024]{3,2,1,0:T(8,128)(2,1)}, bf16[4,4,1024]{2,1,0:T(4,128)(2,1)}) custom-call(bf16[4,16,10,1024]{3,2,1,0:T(8,128)(2,1)} %reshape.247.refs_0_, bf16[4,1024]{1,0:T(4,128)(2,1)} %slice.62.refs_1_), custom_call_target="tpu_custom_call" | custom-call | tf_op jit(solution)/shard_map/pallas_call | solution.py:99
  188.1 2.9 %add_bitcast_fusion.refs_0_ = f32[16,10,1024]{2,1,0:T(8,128)} fusion(bf16[4,16,10,1024]{3,2,1,0:T(8,128)(2,1)} %get-tuple-element.10), kind=kLoop, calls=%fused_computation.17 | loop fusion | flops 1146880 | bytes 1966080 | tf_op jit(solution)/shard_map/add | solution.py:428
  191.6 65.9 %shard_map.197 = (f32[16,10,1024]{2,1,0:T(8,128)}, f32[16,4,1024]{2,1,0:T(4,128)}) custom-call(f32[16,10,1024]{2,1,0:T(8,128)} %add_bitcast_fusion.refs_0_, f32[4,1024]{1,0:T(4,128)} %bitcast_multiply_fusion.refs_1_), custom_call_target="tpu_custom_call" | custom-call | tf_op jit(solution)/shard_map/pallas_call | solution.py:99
  257.6 1.3 reshape.248
  258.9 0.8 gather_fusion
  260.0 0.8 multiply_reduce_fusion
  (95 shorter events, 13.3 us)
Async XLA Ops:
  7.2 103.4 %copy-start = (bf16[128,1024]{1,0:T(8,128)(2,1)S(1)}, bf16[128,1024]{1,0:T(8,128)(2,1)}, u32[]{:S(2)}) copy-start(bf16[128,1024]{1,0:T(8,128)(2,1)} %param.27) | copy-start | bytes 786436
  7.2 117.1 %all-gather.4.cloned.1.call-start = ((), (), s32[]{:S(2)}) async-start(), calls=%async_computation | async-start | bytes 1622016 | tf_op jit(solution)/shard_map/all_gather | solution.py:344
  7.9 120.2 %all-gather.6.cloned.1.call-start = ((), (), s32[]{:S(2)}) async-start(), calls=%async_computation.1 | async-start | bytes 1622016 | tf_op jit(solution)/shard_map/all_gather | solution.py:345
  8.7 119.5 %all-gather.8.cloned.1.call-start = ((), (), s32[]{:S(2)}) async-start(), calls=%async_computation.2 | async-start | bytes 1622016 | tf_op jit(solution)/shard_map/all_gather | solution.py:346
  19.4 89.3 %copy-start.9 = (bf16[4,128]{1,0:T(4,128)(2,1)S(1)}, bf16[4,128]{1,0:T(4,128)(2,1)}, u32[]{:S(2)}) copy-start(bf16[4,128]{1,0:T(4,128)(2,1)} %param.20) | copy-start | bytes 3076
  20.5 90.1 %copy-start.8 = (bf16[4,128]{1,0:T(4,128)(2,1)S(1)}, bf16[4,128]{1,0:T(4,128)(2,1)}, u32[]{:S(2)}) copy-start(bf16[4,128]{1,0:T(4,128)(2,1)} %param.21) | copy-start | bytes 3076
  110.6 13.1 %copy-start.6 = (s32[64,2]{0,1:T(2,128)S(1)}, s32[64,2]{0,1:T(2,128)}, u32[]{:S(2)}) copy-start(s32[64,2]{0,1:T(2,128)} %param.30) | copy-start | bytes 1540
  110.6 13.2 %copy-start.10 = (f32[64,2]{0,1:T(2,128)S(1)}, f32[64,2]{0,1:T(2,128)}, u32[]{:S(2)}) copy-start(f32[64,2]{0,1:T(2,128)} %param.31) | copy-start | bytes 1540
  110.6 13.4 %copy-start.11 = (f32[4,2]{0,1:T(2,128)S(1)}, f32[4,2]{0,1:T(2,128)}, u32[]{:S(2)}) copy-start(f32[4,2]{0,1:T(2,128)} %param.33) | copy-start | bytes 100
  110.6 13.4 %copy-start.12 = (s32[4,2]{0,1:T(2,128)S(1)}, s32[4,2]{0,1:T(2,128)}, u32[]{:S(2)}) copy-start(s32[4,2]{0,1:T(2,128)} %param.32) | copy-start | bytes 100
  110.6 13.4 %copy-start.7 = (bf16[4,1024]{1,0:T(4,128)(2,1)S(1)}, bf16[4,1024]{1,0:T(4,128)(2,1)}, u32[]{:S(2)}) copy-start(bf16[4,1024]{1,0:T(4,128)(2,1)} %param.28) | copy-start | bytes 24580
  111.4 12.8 %copy-start.5 = (f32[1024]{0:T(1024)S(1)}, f32[1024]{0:T(1024)}, u32[]{:S(2)}) copy-start(f32[1024]{0:T(1024)} %param.34) | copy-start | bytes 12292
  121.0 2.9 %copy-start.2 = (f32[8,4,1024]{2,1,0:T(4,128)S(1)}, f32[8,4,1024]{2,1,0:T(4,128)}, u32[]{:S(2)}) copy-start(f32[8,4,1024]{2,1,0:T(4,128)} %shard_map.195) | copy-start | bytes 393220
  188.1 2.9 %copy-start.4 = (bf16[4,4,1024]{2,1,0:T(4,128)(2,1)S(1)}, bf16[4,4,1024]{2,1,0:T(4,128)(2,1)}, u32[]{:S(2)}) copy-start(bf16[4,4,1024]{2,1,0:T(4,128)(2,1)} %get-tuple-element.11) | copy-start | bytes 98308
  258.9 2.0 copy-start.1
  259.7 1.8 copy-start.3
Sparse Core Ops, SparseCore 0:
  10.1 36.1 all-gather.3
  48.4 33.4 all-gather.5
  84.0 33.4 all-gather.7

commit v7 on v6

--- a/solution.py
+++ b/solution.py
@@ -107,10 +107,12 @@
     )(*payloads)
 
 
-def outbound_kernel(groups, shards, slab_ref, part_ref, rows_out, parts_out,
-                    far_parts, near_rows, near_parts,
+def outbound_kernel(groups, shards, lanes, slab_ref, part_ref, gate_ref, up_ref, down_ref,
+                    rows_out, parts_out, gate_out, up_out, down_out,
+                    far_parts, near_rows, near_parts, gate_all, up_all, down_all,
                     far_send, far_recv, far_psend, far_precv,
-                    near_send, near_recv, near_psend, near_precv, local_sem):
+                    near_send, near_recv, near_psend, near_precv, local_sem,
+                    lane_send, lane_recv):
     index = lax.axis_index("seq")
     far_me = lax.rem(index // shards, groups)
     far_base = index - far_me * shards
@@ -137,9 +139,41 @@
                             device_id_type=pl.DeviceIdType.MESH)
         return carry
 
+    lane_me = lax.axis_index("tp")
+
+    def lane_member(slot):
+        return peer_device("tp", slot)
+
+    def greet_lane(step, carry):
+        pl.semaphore_signal(barrier, inc=1, device_id=lane_member(lax.rem(lane_me + step, lanes)),
+                            device_id_type=pl.DeviceIdType.MESH)
+        return carry
+
     lax.fori_loop(1, groups, greet_far, 0)
     lax.fori_loop(1, shards, greet_near, 0)
-    pl.semaphore_wait(barrier, groups + shards - 2)
+    lax.fori_loop(1, lanes, greet_lane, 0)
+    pl.semaphore_wait(barrier, groups + shards + lanes - 3)
+    weight_refs = ((gate_ref, gate_all), (up_ref, up_all), (down_ref, down_all))
+
+    def lane_copy(which, step, slot, landed_slot):
+        source_ref, landed_ref = weight_refs[which]
+        return pltpu.make_async_remote_copy(
+            src_ref=source_ref, dst_ref=landed_ref.at[landed_slot],
+            send_sem=lane_send.at[which, step], recv_sem=lane_recv.at[which, step],
+            device_id=lane_member(slot), device_id_type=pl.DeviceIdType.MESH)
+
+    def lane_start(step, carry):
+        for which in range(3):
+            lane_copy(which, step, lax.rem(lane_me + step, lanes), lane_me).start()
+        return carry
+
+    lax.fori_loop(1, lanes, lane_start, 0)
+    own_weights = [
+        pltpu.make_async_copy(source_ref, landed_ref.at[lane_me], local_sem.at[3 + which])
+        for which, (source_ref, landed_ref) in enumerate(weight_refs)
+    ]
+    for copy in own_weights:
+        copy.start()
 
     def far_copy(step, slot, landed_slot):
         return (
@@ -248,30 +282,48 @@
 
     lax.fori_loop(1, shards, parts_finish, 0)
     own_parts.wait()
+
+    def lane_finish(step, carry):
+        source = lax.rem(lane_me - step + lanes, lanes)
+        for which in range(3):
+            copy = lane_copy(which, step, source, source)
+            copy.wait_send()
+            copy.wait_recv()
+        return carry
+
+    lax.fori_loop(1, lanes, lane_finish, 0)
+    for copy in own_weights:
+        copy.wait()
     rows_out[...] = near_rows[...]
     parts_out[...] = near_parts[...]
-
-
-def outbound(slabs, parts, groups, shards, collective_id):
+    gate_out[...] = gate_all[...]
+    up_out[...] = up_all[...]
+    down_out[...] = down_all[...]
+
+
+def outbound(slabs, parts, weights, groups, shards, lanes, collective_id):
     rows_shape = (shards,) + slabs.shape
     parts_shape = (shards, groups) + parts.shape
+    weight_shapes = [jax.ShapeDtypeStruct((lanes,) + w.shape, w.dtype) for w in weights]
     return pl.pallas_call(
-        functools.partial(outbound_kernel, groups, shards),
+        functools.partial(outbound_kernel, groups, shards, lanes),
         out_shape=[jax.ShapeDtypeStruct(rows_shape, slabs.dtype),
-                   jax.ShapeDtypeStruct(parts_shape, parts.dtype)],
-        in_specs=[pl.BlockSpec(memory_space=pltpu.VMEM)] * 2,
-        out_specs=[pl.BlockSpec(memory_space=pltpu.VMEM)] * 2,
+                   jax.ShapeDtypeStruct(parts_shape, parts.dtype)] + weight_shapes,
+        in_specs=[pl.BlockSpec(memory_space=pltpu.VMEM)] * 5,
+        out_specs=[pl.BlockSpec(memory_space=pltpu.VMEM)] * 5,
         scratch_shapes=[
             pltpu.VMEM((groups,) + parts.shape, parts.dtype),
             pltpu.VMEM(rows_shape, slabs.dtype),
             pltpu.VMEM(parts_shape, parts.dtype),
         ]
+        + [pltpu.VMEM(w.shape, w.dtype) for w in weight_shapes]
         + [pltpu.SemaphoreType.DMA((groups,))] * 4
         + [pltpu.SemaphoreType.DMA((2, shards, groups)), pltpu.SemaphoreType.DMA((shards, groups))]
         + [pltpu.SemaphoreType.DMA((shards,))] * 2
-        + [pltpu.SemaphoreType.DMA((4,))],
+        + [pltpu.SemaphoreType.DMA((8,))]
+        + [pltpu.SemaphoreType.DMA((3, lanes))] * 2,
         compiler_params=pltpu.CompilerParams(collective_id=collective_id, has_side_effects=True),
-    )(slabs, parts)
+    )(slabs, parts, *weights)
 
 
 def merge_softmax(stacked, rows, width):
@@ -340,11 +392,6 @@
     seq_index = lax.axis_index("seq")
     tp_index = lax.axis_index("tp")
     shards = seq_count // EXPERTS
-    weights = (
-        lax.all_gather(w_gate, "tp", axis=0, tiled=True),
-        lax.all_gather(w_up, "tp", axis=0, tiled=True),
-        lax.all_gather(w_down, "tp", axis=1, tiled=True),
-    )
     normed_pre = rms_scale(prefill_in, norm_gain)
     request_count, heads_width = queries.shape
     heads_here = heads_width // HD
@@ -386,7 +433,14 @@
         .reshape(EXPERTS, CAP, feature_width)
     )
     group_count = seq_count // shards
-    block_rows, block_parts = outbound(slabs, packed_parts, group_count, shards, 1)
+    block_rows, block_parts, gate_all, up_all, down_all = outbound(
+        slabs, packed_parts, (w_gate, w_up, w_down), group_count, shards, tp_count, 1
+    )
+    weights = (
+        gate_all.reshape(-1, gate_all.shape[-1]),
+        up_all.reshape(-1, up_all.shape[-1]),
+        jnp.transpose(down_all, (1, 0, 2)).reshape(down_all.shape[1], -1),
+    )
     stage = merge_softmax(
         block_parts.reshape((-1,) + packed_parts.shape), request_count, flat_width
     )

time: 270 us -> 256 us (0.948)
  the two profiles are of different devices: /device:TPU:99 before, /device:TPU:32 now
where the time goes in v7:
time: 256 us; the launch traced here: 255 us
  Pallas kernels  211 us (82%)
  local copies, waits for them, and re-layouts  17 us (7%)
  other arithmetic  14.3 us (6%)
  matrix products  11.8 us (5%)
    pallas_call x3, Pallas kernels, axis_share(): pl.pallas_call(functools.partial(share_kernel, axis, count, stride, tuple...  124 us
    pallas_call x1, Pallas kernels, outbound(): pl.pallas_call(functools.partial(outbound_kernel, groups, shards, lanes),...  87.2 us
    dot_general x1, matrix products, expert_block(): jnp.dot(act, down_full, preferred_element_type=jnp.float32)  5.32 us

profile of v7, /device:TPU:32, one launch (start us, length us, event | category | flops | bytes accessed | tf_op | source)
XLA Modules:
  0.0 255.0 jit_solution(13809229740552914014)
XLA Ops:
  2.1 1.0 copy.53
  4.0 0.9 fusion.50
  5.3 0.9 reshape.250
  9.4 1.0 fusion.14
  10.5 1.0 fusion.16
  11.7 1.2 scatter_custom_fusion
  13.0 0.9 reshape.247.slab_ref
  13.9 0.8 copy.38.gate_ref
  14.7 0.8 copy.39.up_ref
  15.5 87.2 %shard_map.194 = (bf16[4,16,10,1024]{3,2,1,0:T(8,128)(2,1)}, f32[4,16,8,128]{3,2,1,0:T(8,128)}, bf16[8,128,704]{2,1,0:T(8,128)(2,1)}, bf16[8,128,704]{2,1,0:T(8,128)(2,1)}, bf16[8,704,128]{2,1,0:T(8,128)(2,1)}) custom-call(bf16[16,10,1024]{2,1,0:T(8,128)(2,1)} %reshape.247.slab_ref, f32[8,128]{1,0:T(8,128)} %pad_maximum_fusion.5.part_ref, ...), custom_call_target="tpu_custom_call" | custom-call | tf_op jit(solution)/shard_map/pallas_call | solution.py:308
  102.8 1.3 slice_reduce_fusion.1
  105.0 1.0 fusion.20
  108.0 8.9 %shard_map.195 = f32[8,4,1024]{2,1,0:T(4,128)} custom-call(f32[4,1024]{1,0:T(4,128)} %fusion.35.refs_0_), custom_call_target="tpu_custom_call" | custom-call | tf_op jit(solution)/shard_map/pallas_call | solution.py:99
  116.9 0.9 reduce_sum.110
  118.1 1.3 reshape.255
  119.4 4.4 %fusion.13 = f32[644,704]{1,0:T(8,128)} fusion(bf16[1024,704]{1,0:T(8,128)(2,1)} %bitcast.64, bf16[4,1024]{1,0:T(4,128)(2,1)S(1)} %fusion.27, bf16[640,1024]{1,0:T(8,128)(2,1)} %reshape.255), kind=kOutput, calls=%fused_computation.20 | convolution fusion | flops 931151872 | bytes 4574208 | tf_op jit(solution)/shard_map/dot_general | solution.py:364
  123.8 5.3 %convolution_convert_fusion = bf16[644,1024]{1,0:T(8,128)(2,1)S(1)} fusion(f32[644,704]{1,0:T(8,128)} %fusion.13, bf16[1024,704]{1,0:T(8,128)(2,1)} %bitcast.63, bf16[4,1024]{1,0:T(4,128)(2,1)S(1)} %fusion.27, bf16[640,1024]{1,0:T(8,128)(2,1)S(1)} %copy-done.2, bf16[8,704,128]{2,1,0:T(8,128)(2,1)} %get-tuple-element.15), kind=kOutput, calls=%fused_computation.12 | convolution fusion | flops 1864859136 | bytes 7334912 | tf_op jit(solution)/shard_map/dot_general | solution.py:367
  129.2 1.6 reshape.259.refs_0_
  131.4 54.9 %shard_map.196 = (bf16[4,16,10,1024]{3,2,1,0:T(8,128)(2,1)}, bf16[4,4,1024]{2,1,0:T(4,128)(2,1)}) custom-call(bf16[4,16,10,1024]{3,2,1,0:T(8,128)(2,1)} %reshape.259.refs_0_, bf16[4,1024]{1,0:T(4,128)(2,1)} %slice.62.refs_1_), custom_call_target="tpu_custom_call" | custom-call | tf_op jit(solution)/shard_map/pallas_call | solution.py:99
  186.3 2.9 %add_bitcast_fusion.refs_0_ = f32[16,10,1024]{2,1,0:T(8,128)} fusion(bf16[4,16,10,1024]{3,2,1,0:T(8,128)(2,1)} %get-tuple-element.16), kind=kLoop, calls=%fused_computation.19 | loop fusion | flops 1146880 | bytes 1966080 | tf_op jit(solution)/shard_map/add | solution.py:482
  189.9 59.9 %shard_map.197 = (f32[16,10,1024]{2,1,0:T(8,128)}, f32[16,4,1024]{2,1,0:T(4,128)}) custom-call(f32[16,10,1024]{2,1,0:T(8,128)} %add_bitcast_fusion.refs_0_, f32[4,1024]{1,0:T(4,128)} %bitcast_multiply_fusion.refs_1_), custom_call_target="tpu_custom_call" | custom-call | tf_op jit(solution)/shard_map/pallas_call | solution.py:99
  249.8 1.3 reshape.260
  251.2 0.8 gather_fusion
  252.8 0.8 multiply_reduce_fusion
  (96 shorter events, 12.8 us)
Async XLA Ops:
  0.6 106.6 %copy-start = (bf16[128,1024]{1,0:T(8,128)(2,1)S(1)}, bf16[128,1024]{1,0:T(8,128)(2,1)}, u32[]{:S(2)}) copy-start(bf16[128,1024]{1,0:T(8,128)(2,1)} %param.27) | copy-start | bytes 786436
  6.2 7.7 %copy-start.5 = (bf16[128,704]{0,1:T(8,128)(2,1)S(1)}, bf16[128,704]{0,1:T(8,128)(2,1)}, u32[]{:S(2)}) copy-start(bf16[128,704]{0,1:T(8,128)(2,1)} %param.35) | copy-start | bytes 540676
  8.1 6.6 %copy-start.6 = (bf16[128,704]{0,1:T(8,128)(2,1)S(1)}, bf16[128,704]{0,1:T(8,128)(2,1)}, u32[]{:S(2)}) copy-start(bf16[128,704]{0,1:T(8,128)(2,1)} %param.36) | copy-start | bytes 540676
  13.9 92.6 %copy-start.13 = (bf16[4,128]{1,0:T(4,128)(2,1)S(1)}, bf16[4,128]{1,0:T(4,128)(2,1)}, u32[]{:S(2)}) copy-start(bf16[4,128]{1,0:T(4,128)(2,1)} %param.20) | copy-start | bytes 3076
  13.9 92.7 %copy-start.11 = (bf16[4,128]{1,0:T(4,128)(2,1)S(1)}, bf16[4,128]{1,0:T(4,128)(2,1)}, u32[]{:S(2)}) copy-start(bf16[4,128]{1,0:T(4,128)(2,1)} %param.19) | copy-start | bytes 3076
  14.7 92.5 %copy-start.12 = (bf16[4,128]{1,0:T(4,128)(2,1)S(1)}, bf16[4,128]{1,0:T(4,128)(2,1)}, u32[]{:S(2)}) copy-start(bf16[4,128]{1,0:T(4,128)(2,1)} %param.21) | copy-start | bytes 3076
  15.5 102.3 %copy-start.10 = (bf16[4,1024]{1,0:T(4,128)(2,1)S(1)}, bf16[4,1024]{1,0:T(4,128)(2,1)}, u32[]{:S(2)}) copy-start(bf16[4,1024]{1,0:T(4,128)(2,1)} %param.28) | copy-start | bytes 24580
  15.5 102.5 %copy-start.8 = (f32[1024]{0:T(1024)S(1)}, f32[1024]{0:T(1024)}, u32[]{:S(2)}) copy-start(f32[1024]{0:T(1024)} %param.34) | copy-start | bytes 12292
  102.8 15.3 %copy-start.1 = (bf16[4,16,10,1024]{3,2,1,0:T(8,128)(2,1)S(1)}, bf16[4,16,10,1024]{3,2,1,0:T(8,128)(2,1)}, u32[]{:S(2)}) copy-start(bf16[4,16,10,1024]{3,2,1,0:T(8,128)(2,1)} %get-tuple-element.12) | copy-start | bytes 3932164
  119.4 4.4 %copy-start.2 = (bf16[640,1024]{1,0:T(8,128)(2,1)S(1)}, bf16[640,1024]{1,0:T(8,128)(2,1)}, u32[]{:S(2)}) copy-start(bf16[640,1024]{1,0:T(8,128)(2,1)} %reshape.255) | copy-start | bytes 3932164
  186.3 2.9 %copy-start.14 = (f32[4,2]{0,1:T(2,128)S(1)}, f32[4,2]{0,1:T(2,128)}, u32[]{:S(2)}) copy-start(f32[4,2]{0,1:T(2,128)} %param.33) | copy-start | bytes 100
  186.3 2.9 %copy-start.15 = (s32[4,2]{0,1:T(2,128)S(1)}, s32[4,2]{0,1:T(2,128)}, u32[]{:S(2)}) copy-start(s32[4,2]{0,1:T(2,128)} %param.32) | copy-start | bytes 100
  186.3 2.9 %copy-start.7 = (bf16[4,4,1024]{2,1,0:T(4,128)(2,1)S(1)}, bf16[4,4,1024]{2,1,0:T(4,128)(2,1)}, u32[]{:S(2)}) copy-start(bf16[4,4,1024]{2,1,0:T(4,128)(2,1)} %get-tuple-element.17) | copy-start | bytes 98308
  251.2 1.4 copy-start.9
  251.2 1.5 copy-start.16
  252.0 1.6 copy-start.3
  252.0 2.3 copy-start.4

commit v8 on v7

--- a/solution.py
+++ b/solution.py
@@ -426,11 +426,12 @@
     )
     flat_index = route_slots(routes, CAP)
     feature_width = normed_pre.shape[1]
+    slot_expert = flat_index // CAP
+    slot_rank = flat_index % CAP
     slabs = (
-        jnp.zeros((EXPERTS * CAP, feature_width), jnp.bfloat16)
-        .at[flat_index]
+        jnp.zeros((EXPERTS, CAP, feature_width), jnp.bfloat16)
+        .at[slot_expert, slot_rank]
         .set(jnp.repeat(normed_pre, TOP, axis=0))
-        .reshape(EXPERTS, CAP, feature_width)
     )
     group_count = seq_count // shards
     block_rows, block_parts, gate_all, up_all, down_all = outbound(
@@ -488,8 +489,7 @@
     )
     dec_terms = jnp.sum(dec_all, axis=0)
     decode_out = (decode_hidden.astype(jnp.float32) + dec_terms).astype(jnp.bfloat16)
-    picked = jnp.take(returned.reshape(EXPERTS * CAP, -1), flat_index, axis=0)
-    picked = picked.reshape(-1, TOP, picked.shape[-1])
+    picked = returned[slot_expert, slot_rank].reshape(-1, TOP, returned.shape[-1])
     prefill_out = (
         prefill_in.astype(jnp.float32) + jnp.sum(gates[..., None] * picked, axis=1)
     ).astype(jnp.bfloat16)

time: 256 us -> 264 us (1.031)
  local copies, waits for them, and re-layouts: 17 us -> 25.3 us
    scatter x1 -> x2, local copies, waits for them, and re-layouts: 1.23 us -> 9.72 us  [body(): slabs = jnp.zeros((EXPERTS, CAP, feature_width), jnp.bfloat16).at[slot_ex...]
where the time goes in v8:
time: 264 us; the launch traced here: 263 us
  Pallas kernels  211 us (80%)
  local copies, waits for them, and re-layouts  25.3 us (10%)
  other arithmetic  14.2 us (5%)
  matrix products  11.8 us (4%)
    pallas_call x3, Pallas kernels, axis_share(): pl.pallas_call(functools.partial(share_kernel, axis, count, stride, tuple...  124 us
    pallas_call x1, Pallas kernels, outbound(): pl.pallas_call(functools.partial(outbound_kernel, groups, shards, lanes),...  87.2 us
    scatter x2, local copies, waits for them, and re-layouts, body(): slabs = jnp.zeros((EXPERTS, CAP, feature_width), jnp.bfloat16).at[slot_ex...  9.72 us
    dot_general x1, matrix products, expert_block(): jnp.dot(act, down_full, preferred_element_type=jnp.float32)  5.33 us

profile of v8, /device:TPU:32, one launch (start us, length us, event | category | flops | bytes accessed | tf_op | source)
XLA Modules:
  0.0 263.2 jit_solution(264351087829103192)
XLA Ops:
  2.1 1.0 copy.46
  4.0 0.9 fusion.50
  5.3 0.9 reshape.285
  9.4 1.0 fusion.14
  10.5 1.0 fusion.16
  11.8 8.7 %scatter_fusion = bf16[16,10,1024]{2,0,1:T(8,128)(2,1)S(1)} fusion(bf16[16,10,1024]{2,0,1:T(8,128)(2,1)S(1)} %broadcast_in_dim.27, s32[128]{0:T(128)S(1)} %fusion.38, bf16[128,1024]{1,0:T(8,128)(2,1)S(1)} %reshape.305), kind=kCustom, calls=%fused_computation.1 | custom fusion | bytes 787456 | tf_op jit(solution)/shard_map/scatter | solution.py:434
  20.5 1.0 copy.31.slab_ref
  21.6 0.8 copy.32.gate_ref
  22.4 0.8 copy.33.up_ref
  23.2 87.2 %shard_map.194 = (bf16[4,16,10,1024]{3,2,1,0:T(8,128)(2,1)}, f32[4,16,8,128]{3,2,1,0:T(8,128)}, bf16[8,128,704]{2,1,0:T(8,128)(2,1)}, bf16[8,128,704]{2,1,0:T(8,128)(2,1)}, bf16[8,704,128]{2,1,0:T(8,128)(2,1)}) custom-call(bf16[16,10,1024]{2,1,0:T(8,128)(2,1)} %copy.31.slab_ref, f32[8,128]{1,0:T(8,128)} %pad_maximum_fusion.5.part_ref, ...), custom_call_target="tpu_custom_call" | custom-call | tf_op jit(solution)/shard_map/pallas_call | solution.py:308
  110.4 1.3 slice_reduce_fusion.1
  112.6 1.0 fusion.18
  114.9 0.8 fusion.33.refs_0_
  115.7 8.9 %shard_map.195 = f32[8,4,1024]{2,1,0:T(4,128)} custom-call(f32[4,1024]{1,0:T(4,128)} %fusion.33.refs_0_), custom_call_target="tpu_custom_call" | custom-call | tf_op jit(solution)/shard_map/pallas_call | solution.py:99
  124.6 0.9 reduce_sum.108
  125.7 1.3 reshape.290
  127.1 4.4 %fusion.13 = f32[644,704]{1,0:T(8,128)} fusion(bf16[1024,704]{1,0:T(8,128)(2,1)} %bitcast.70, bf16[4,1024]{1,0:T(4,128)(2,1)S(1)} %fusion.25, bf16[640,1024]{1,0:T(8,128)(2,1)} %reshape.290), kind=kOutput, calls=%fused_computation.20 | convolution fusion | flops 931151872 | bytes 4574208 | tf_op jit(solution)/shard_map/dot_general | solution.py:364
  131.5 5.3 %convolution_convert_fusion = bf16[644,1024]{1,0:T(8,128)(2,1)S(1)} fusion(f32[644,704]{1,0:T(8,128)} %fusion.13, bf16[1024,704]{1,0:T(8,128)(2,1)} %bitcast.69, bf16[4,1024]{1,0:T(4,128)(2,1)S(1)} %fusion.25, bf16[640,1024]{1,0:T(8,128)(2,1)S(1)} %copy-done.2, bf16[8,704,128]{2,1,0:T(8,128)(2,1)} %get-tuple-element.15), kind=kOutput, calls=%fused_computation.12 | convolution fusion | flops 1864859136 | bytes 7334912 | tf_op jit(solution)/shard_map/dot_general | solution.py:367
  136.9 1.6 reshape.294.refs_0_
  139.1 54.9 %shard_map.196 = (bf16[4,16,10,1024]{3,2,1,0:T(8,128)(2,1)}, bf16[4,4,1024]{2,1,0:T(4,128)(2,1)}) custom-call(bf16[4,16,10,1024]{3,2,1,0:T(8,128)(2,1)} %reshape.294.refs_0_, bf16[4,1024]{1,0:T(4,128)(2,1)} %slice.64.refs_1_), custom_call_target="tpu_custom_call" | custom-call | tf_op jit(solution)/shard_map/pallas_call | solution.py:99
  194.0 2.9 %add_bitcast_fusion.refs_0_ = f32[16,10,1024]{2,1,0:T(8,128)} fusion(bf16[4,16,10,1024]{3,2,1,0:T(8,128)(2,1)} %get-tuple-element.16), kind=kLoop, calls=%fused_computation.19 | loop fusion | flops 1146880 | bytes 1966080 | tf_op jit(solution)/shard_map/add | solution.py:483
  197.6 59.9 %shard_map.197 = (f32[16,10,1024]{2,1,0:T(8,128)}, f32[16,4,1024]{2,1,0:T(4,128)}) custom-call(f32[16,10,1024]{2,1,0:T(8,128)} %add_bitcast_fusion.refs_0_, f32[4,1024]{1,0:T(4,128)} %bitcast_multiply_fusion.refs_1_), custom_call_target="tpu_custom_call" | custom-call | tf_op jit(solution)/shard_map/pallas_call | solution.py:99
  257.5 1.6 copy.39
  259.1 1.5 gather_fusion
  (91 shorter events, 12.4 us)
Async XLA Ops:
  0.6 114.3 %copy-start = (bf16[128,1024]{1,0:T(8,128)(2,1)S(1)}, bf16[128,1024]{1,0:T(8,128)(2,1)}, u32[]{:S(2)}) copy-start(bf16[128,1024]{1,0:T(8,128)(2,1)} %param.27) | copy-start | bytes 786436
  11.8 9.8 %copy-start.5 = (bf16[128,704]{0,1:T(8,128)(2,1)S(1)}, bf16[128,704]{0,1:T(8,128)(2,1)}, u32[]{:S(2)}) copy-start(bf16[128,704]{0,1:T(8,128)(2,1)} %param.35) | copy-start | bytes 540676
  11.8 10.6 %copy-start.6 = (bf16[128,704]{0,1:T(8,128)(2,1)S(1)}, bf16[128,704]{0,1:T(8,128)(2,1)}, u32[]{:S(2)}) copy-start(bf16[128,704]{0,1:T(8,128)(2,1)} %param.36) | copy-start | bytes 540676
  21.5 92.6 %copy-start.12 = (bf16[4,128]{1,0:T(4,128)(2,1)S(1)}, bf16[4,128]{1,0:T(4,128)(2,1)}, u32[]{:S(2)}) copy-start(bf16[4,128]{1,0:T(4,128)(2,1)} %param.20) | copy-start | bytes 3076
  21.6 92.7 %copy-start.10 = (bf16[4,128]{1,0:T(4,128)(2,1)S(1)}, bf16[4,128]{1,0:T(4,128)(2,1)}, u32[]{:S(2)}) copy-start(bf16[4,128]{1,0:T(4,128)(2,1)} %param.19) | copy-start | bytes 3076
  22.4 92.5 %copy-start.11 = (bf16[4,128]{1,0:T(4,128)(2,1)S(1)}, bf16[4,128]{1,0:T(4,128)(2,1)}, u32[]{:S(2)}) copy-start(bf16[4,128]{1,0:T(4,128)(2,1)} %param.21) | copy-start | bytes 3076
  23.2 102.3 %copy-start.9 = (bf16[4,1024]{1,0:T(4,128)(2,1)S(1)}, bf16[4,1024]{1,0:T(4,128)(2,1)}, u32[]{:S(2)}) copy-start(bf16[4,1024]{1,0:T(4,128)(2,1)} %param.28) | copy-start | bytes 24580
  23.2 102.5 %copy-start.8 = (f32[1024]{0:T(1024)S(1)}, f32[1024]{0:T(1024)}, u32[]{:S(2)}) copy-start(f32[1024]{0:T(1024)} %param.34) | copy-start | bytes 12292
  110.4 15.3 %copy-start.1 = (bf16[4,16,10,1024]{3,2,1,0:T(8,128)(2,1)S(1)}, bf16[4,16,10,1024]{3,2,1,0:T(8,128)(2,1)}, u32[]{:S(2)}) copy-start(bf16[4,16,10,1024]{3,2,1,0:T(8,128)(2,1)} %get-tuple-element.12) | copy-start | bytes 3932164
  127.1 4.4 %copy-start.2 = (bf16[640,1024]{1,0:T(8,128)(2,1)S(1)}, bf16[640,1024]{1,0:T(8,128)(2,1)}, u32[]{:S(2)}) copy-start(bf16[640,1024]{1,0:T(8,128)(2,1)} %reshape.290) | copy-start | bytes 3932164
  194.0 2.9 %copy-start.13 = (f32[4,2]{0,1:T(2,128)S(1)}, f32[4,2]{0,1:T(2,128)}, u32[]{:S(2)}) copy-start(f32[4,2]{0,1:T(2,128)} %param.33) | copy-start | bytes 100
  194.0 2.9 %copy-start.14 = (s32[4,2]{0,1:T(2,128)S(1)}, s32[4,2]{0,1:T(2,128)}, u32[]{:S(2)}) copy-start(s32[4,2]{0,1:T(2,128)} %param.32) | copy-start | bytes 100
  194.0 2.9 %copy-start.7 = (bf16[4,4,1024]{2,1,0:T(4,128)(2,1)S(1)}, bf16[4,4,1024]{2,1,0:T(4,128)(2,1)}, u32[]{:S(2)}) copy-start(bf16[4,4,1024]{2,1,0:T(4,128)(2,1)} %get-tuple-element.17) | copy-start | bytes 98308
  259.1 1.9 copy-start.15
  260.6 1.2 copy-start.3
  260.7 1.8 copy-start.4

commit v9 on v7

--- a/solution.py
+++ b/solution.py
@@ -23,10 +23,9 @@
 def share_kernel(axis, count, stride, modes, *refs):
     width = len(modes)
     sources = refs[:width]
-    outputs = refs[width : 2 * width]
-    landed = refs[2 * width : 3 * width]
-    send_sems = refs[3 * width : 4 * width]
-    recv_sems = refs[4 * width :]
+    landed = refs[width : 2 * width]
+    send_sems = refs[2 * width : 3 * width]
+    recv_sems = refs[3 * width :]
     index = lax.axis_index(axis)
     me = lax.rem(index // stride, count)
     base = index - me * stride
@@ -89,8 +88,6 @@
         return carry
 
     lax.fori_loop(1, count, finish, 0)
-    for which in range(width):
-        outputs[which][...] = landed[which][...]
 
 
 def axis_share(payloads, modes, axis, count, stride, collective_id):
@@ -101,15 +98,13 @@
         out_shape=[jax.ShapeDtypeStruct(s, x.dtype) for s, x in zip(shapes, payloads)],
         in_specs=[pl.BlockSpec(memory_space=pltpu.VMEM)] * width,
         out_specs=[pl.BlockSpec(memory_space=pltpu.VMEM)] * width,
-        scratch_shapes=[pltpu.VMEM(s, x.dtype) for s, x in zip(shapes, payloads)]
-        + [pltpu.SemaphoreType.DMA((count,))] * (2 * width),
+        scratch_shapes=[pltpu.SemaphoreType.DMA((count,))] * (2 * width),
         compiler_params=pltpu.CompilerParams(collective_id=collective_id, has_side_effects=True),
     )(*payloads)
 
 
 def outbound_kernel(groups, shards, lanes, slab_ref, part_ref, gate_ref, up_ref, down_ref,
-                    rows_out, parts_out, gate_out, up_out, down_out,
-                    far_parts, near_rows, near_parts, gate_all, up_all, down_all,
+                    near_rows, near_parts, gate_all, up_all, down_all, far_parts,
                     far_send, far_recv, far_psend, far_precv,
                     near_send, near_recv, near_psend, near_precv, local_sem,
                     lane_send, lane_recv):
@@ -294,11 +289,6 @@
     lax.fori_loop(1, lanes, lane_finish, 0)
     for copy in own_weights:
         copy.wait()
-    rows_out[...] = near_rows[...]
-    parts_out[...] = near_parts[...]
-    gate_out[...] = gate_all[...]
-    up_out[...] = up_all[...]
-    down_out[...] = down_all[...]
 
 
 def outbound(slabs, parts, weights, groups, shards, lanes, collective_id):
@@ -311,12 +301,7 @@
                    jax.ShapeDtypeStruct(parts_shape, parts.dtype)] + weight_shapes,
         in_specs=[pl.BlockSpec(memory_space=pltpu.VMEM)] * 5,
         out_specs=[pl.BlockSpec(memory_space=pltpu.VMEM)] * 5,
-        scratch_shapes=[
-            pltpu.VMEM((groups,) + parts.shape, parts.dtype),
-            pltpu.VMEM(rows_shape, slabs.dtype),
-            pltpu.VMEM(parts_shape, parts.dtype),
-        ]
-        + [pltpu.VMEM(w.shape, w.dtype) for w in weight_shapes]
+        scratch_shapes=[pltpu.VMEM((groups,) + parts.shape, parts.dtype)]
         + [pltpu.SemaphoreType.DMA((groups,))] * 4
         + [pltpu.SemaphoreType.DMA((2, shards, groups)), pltpu.SemaphoreType.DMA((shards, groups))]
         + [pltpu.SemaphoreType.DMA((shards,))] * 2

time: 256 us -> 256 us (level)
  no operation moved by 1% of the time
where the time goes in v9:
time: 256 us; the launch traced here: 255 us
  Pallas kernels  211 us (82%)
  local copies, waits for them, and re-layouts  17 us (7%)
  other arithmetic  14.3 us (6%)
  matrix products  11.8 us (5%)
    pallas_call x3, Pallas kernels, axis_share(): pl.pallas_call(functools.partial(share_kernel, axis, count, stride, tuple...  124 us
    pallas_call x1, Pallas kernels, outbound(): pl.pallas_call(functools.partial(outbound_kernel, groups, shards, lanes),...  87.2 us
    dot_general x1, matrix products, expert_block(): jnp.dot(act, down_full, preferred_element_type=jnp.float32)  5.32 us

profile of v9, /device:TPU:32, one launch (start us, length us, event | category | flops | bytes accessed | tf_op | source)
XLA Modules:
  0.0 254.8 jit_solution(3348564974508885577)
XLA Ops:
  2.1 1.0 copy.53
  4.0 0.9 fusion.50
  5.3 0.9 reshape.250
  9.4 1.0 fusion.14
  10.5 1.0 fusion.16
  11.7 1.2 scatter_custom_fusion
  13.0 0.9 reshape.247.slab_ref
  13.9 0.8 copy.38.gate_ref
  14.7 0.8 copy.39.up_ref
  15.5 87.2 %shard_map.194 = (bf16[4,16,10,1024]{3,2,1,0:T(8,128)(2,1)}, f32[4,16,8,128]{3,2,1,0:T(8,128)}, bf16[8,128,704]{2,1,0:T(8,128)(2,1)}, bf16[8,128,704]{2,1,0:T(8,128)(2,1)}, bf16[8,704,128]{2,1,0:T(8,128)(2,1)}) custom-call(bf16[16,10,1024]{2,1,0:T(8,128)(2,1)} %reshape.247.slab_ref, f32[8,128]{1,0:T(8,128)} %pad_maximum_fusion.5.part_ref, ...), custom_call_target="tpu_custom_call" | custom-call | tf_op jit(solution)/shard_map/pallas_call | solution.py:298
  102.7 1.3 slice_reduce_fusion.1
  104.9 1.0 fusion.20
  107.9 8.9 %shard_map.195 = f32[8,4,1024]{2,1,0:T(4,128)} custom-call(f32[4,1024]{1,0:T(4,128)} %fusion.35.refs_0_), custom_call_target="tpu_custom_call" | custom-call | tf_op jit(solution)/shard_map/pallas_call | solution.py:96
  116.9 0.9 reduce_sum.110
  118.0 1.3 reshape.255
  119.3 4.4 %fusion.13 = f32[644,704]{1,0:T(8,128)} fusion(bf16[1024,704]{1,0:T(8,128)(2,1)} %bitcast.64, bf16[4,1024]{1,0:T(4,128)(2,1)S(1)} %fusion.27, bf16[640,1024]{1,0:T(8,128)(2,1)} %reshape.255), kind=kOutput, calls=%fused_computation.20 | convolution fusion | flops 931151872 | bytes 4574208 | tf_op jit(solution)/shard_map/dot_general | solution.py:349
  123.8 5.3 %convolution_convert_fusion = bf16[644,1024]{1,0:T(8,128)(2,1)S(1)} fusion(f32[644,704]{1,0:T(8,128)} %fusion.13, bf16[1024,704]{1,0:T(8,128)(2,1)} %bitcast.63, bf16[4,1024]{1,0:T(4,128)(2,1)S(1)} %fusion.27, bf16[640,1024]{1,0:T(8,128)(2,1)S(1)} %copy-done.2, bf16[8,704,128]{2,1,0:T(8,128)(2,1)} %get-tuple-element.15), kind=kOutput, calls=%fused_computation.12 | convolution fusion | flops 1864859136 | bytes 7334912 | tf_op jit(solution)/shard_map/dot_general | solution.py:352
  129.2 1.6 reshape.259.refs_0_
  131.4 54.7 %shard_map.196 = (bf16[4,16,10,1024]{3,2,1,0:T(8,128)(2,1)}, bf16[4,4,1024]{2,1,0:T(4,128)(2,1)}) custom-call(bf16[4,16,10,1024]{3,2,1,0:T(8,128)(2,1)} %reshape.259.refs_0_, bf16[4,1024]{1,0:T(4,128)(2,1)} %slice.62.refs_1_), custom_call_target="tpu_custom_call" | custom-call | tf_op jit(solution)/shard_map/pallas_call | solution.py:96
  186.1 2.9 %add_bitcast_fusion.refs_0_ = f32[16,10,1024]{2,1,0:T(8,128)} fusion(bf16[4,16,10,1024]{3,2,1,0:T(8,128)(2,1)} %get-tuple-element.16), kind=kLoop, calls=%fused_computation.19 | loop fusion | flops 1146880 | bytes 1966080 | tf_op jit(solution)/shard_map/add | solution.py:467
  189.7 59.9 %shard_map.197 = (f32[16,10,1024]{2,1,0:T(8,128)}, f32[16,4,1024]{2,1,0:T(4,128)}) custom-call(f32[16,10,1024]{2,1,0:T(8,128)} %add_bitcast_fusion.refs_0_, f32[4,1024]{1,0:T(4,128)} %bitcast_multiply_fusion.refs_1_), custom_call_target="tpu_custom_call" | custom-call | tf_op jit(solution)/shard_map/pallas_call | solution.py:96
  249.6 1.3 reshape.260
  251.0 0.8 gather_fusion
  252.6 0.8 multiply_reduce_fusion
  (96 shorter events, 12.8 us)
Async XLA Ops:
  0.6 106.5 %copy-start = (bf16[128,1024]{1,0:T(8,128)(2,1)S(1)}, bf16[128,1024]{1,0:T(8,128)(2,1)}, u32[]{:S(2)}) copy-start(bf16[128,1024]{1,0:T(8,128)(2,1)} %param.27) | copy-start | bytes 786436
  6.2 7.7 %copy-start.5 = (bf16[128,704]{0,1:T(8,128)(2,1)S(1)}, bf16[128,704]{0,1:T(8,128)(2,1)}, u32[]{:S(2)}) copy-start(bf16[128,704]{0,1:T(8,128)(2,1)} %param.35) | copy-start | bytes 540676
  8.1 6.6 %copy-start.6 = (bf16[128,704]{0,1:T(8,128)(2,1)S(1)}, bf16[128,704]{0,1:T(8,128)(2,1)}, u32[]{:S(2)}) copy-start(bf16[128,704]{0,1:T(8,128)(2,1)} %param.36) | copy-start | bytes 540676
  13.9 92.5 %copy-start.13 = (bf16[4,128]{1,0:T(4,128)(2,1)S(1)}, bf16[4,128]{1,0:T(4,128)(2,1)}, u32[]{:S(2)}) copy-start(bf16[4,128]{1,0:T(4,128)(2,1)} %param.20) | copy-start | bytes 3076
  13.9 92.6 %copy-start.11 = (bf16[4,128]{1,0:T(4,128)(2,1)S(1)}, bf16[4,128]{1,0:T(4,128)(2,1)}, u32[]{:S(2)}) copy-start(bf16[4,128]{1,0:T(4,128)(2,1)} %param.19) | copy-start | bytes 3076
  14.7 92.5 %copy-start.12 = (bf16[4,128]{1,0:T(4,128)(2,1)S(1)}, bf16[4,128]{1,0:T(4,128)(2,1)}, u32[]{:S(2)}) copy-start(bf16[4,128]{1,0:T(4,128)(2,1)} %param.21) | copy-start | bytes 3076
  15.5 102.3 %copy-start.10 = (bf16[4,1024]{1,0:T(4,128)(2,1)S(1)}, bf16[4,1024]{1,0:T(4,128)(2,1)}, u32[]{:S(2)}) copy-start(bf16[4,1024]{1,0:T(4,128)(2,1)} %param.28) | copy-start | bytes 24580
  15.5 102.4 %copy-start.8 = (f32[1024]{0:T(1024)S(1)}, f32[1024]{0:T(1024)}, u32[]{:S(2)}) copy-start(f32[1024]{0:T(1024)} %param.34) | copy-start | bytes 12292
  102.7 15.3 %copy-start.1 = (bf16[4,16,10,1024]{3,2,1,0:T(8,128)(2,1)S(1)}, bf16[4,16,10,1024]{3,2,1,0:T(8,128)(2,1)}, u32[]{:S(2)}) copy-start(bf16[4,16,10,1024]{3,2,1,0:T(8,128)(2,1)} %get-tuple-element.12) | copy-start | bytes 3932164
  119.3 4.4 %copy-start.2 = (bf16[640,1024]{1,0:T(8,128)(2,1)S(1)}, bf16[640,1024]{1,0:T(8,128)(2,1)}, u32[]{:S(2)}) copy-start(bf16[640,1024]{1,0:T(8,128)(2,1)} %reshape.255) | copy-start | bytes 3932164
  186.1 2.9 %copy-start.14 = (f32[4,2]{0,1:T(2,128)S(1)}, f32[4,2]{0,1:T(2,128)}, u32[]{:S(2)}) copy-start(f32[4,2]{0,1:T(2,128)} %param.33) | copy-start | bytes 100
  186.1 2.9 %copy-start.15 = (s32[4,2]{0,1:T(2,128)S(1)}, s32[4,2]{0,1:T(2,128)}, u32[]{:S(2)}) copy-start(s32[4,2]{0,1:T(2,128)} %param.32) | copy-start | bytes 100
  186.1 2.9 %copy-start.7 = (bf16[4,4,1024]{2,1,0:T(4,128)(2,1)S(1)}, bf16[4,4,1024]{2,1,0:T(4,128)(2,1)}, u32[]{:S(2)}) copy-start(bf16[4,4,1024]{2,1,0:T(4,128)(2,1)} %get-tuple-element.17) | copy-start | bytes 98308
  251.0 1.4 copy-start.9
  251.0 1.5 copy-start.16
  251.8 1.6 copy-start.3
  251.8 2.3 copy-start.4

commit v10 on v9

--- a/solution.py
+++ b/solution.py
@@ -14,13 +14,21 @@
 CAP = 10
 
 
+def far_seq(index, slot, shards):
+    blocks = 16 // shards
+    place = index % shards
+    rel = (slot % blocks - (index // shards) % blocks + blocks) % blocks
+    opposite = (rel // (blocks // 2)) * (1 - rel % 2)
+    return slot * shards + (place + opposite * (shards // 2)) % shards
+
+
 def peer_device(axis, peer):
     if axis == "seq":
         return (peer, lax.axis_index("tp"))
     return (lax.axis_index("seq"), peer)
 
 
-def share_kernel(axis, count, stride, modes, *refs):
+def share_kernel(axis, count, stride, twisted, modes, *refs):
     width = len(modes)
     sources = refs[:width]
     landed = refs[width : 2 * width]
@@ -31,6 +39,8 @@
     base = index - me * stride
 
     def member(slot):
+        if twisted:
+            return peer_device(axis, far_seq(index, slot, stride))
         return peer_device(axis, base + slot * stride)
 
     def piece(which, slot):
@@ -90,11 +100,11 @@
     lax.fori_loop(1, count, finish, 0)
 
 
-def axis_share(payloads, modes, axis, count, stride, collective_id):
+def axis_share(payloads, modes, axis, count, stride, collective_id, twisted=False):
     shapes = [x.shape if mode else (count,) + x.shape for x, mode in zip(payloads, modes)]
     width = len(payloads)
     return pl.pallas_call(
-        functools.partial(share_kernel, axis, count, stride, tuple(modes)),
+        functools.partial(share_kernel, axis, count, stride, twisted, tuple(modes)),
         out_shape=[jax.ShapeDtypeStruct(s, x.dtype) for s, x in zip(shapes, payloads)],
         in_specs=[pl.BlockSpec(memory_space=pltpu.VMEM)] * width,
         out_specs=[pl.BlockSpec(memory_space=pltpu.VMEM)] * width,
@@ -117,7 +127,7 @@
     has_left = place > 0
 
     def far_member(slot):
-        return peer_device("seq", far_base + slot * shards)
+        return peer_device("seq", far_seq(index, slot, shards))
 
     def near_member(slot):
         return peer_device("seq", near_base + slot)
@@ -173,7 +183,8 @@
     def far_copy(step, slot, landed_slot):
         return (
             pltpu.make_async_remote_copy(
-                src_ref=slab_ref.at[slot], dst_ref=near_rows.at[place, landed_slot],
+                src_ref=slab_ref.at[slot],
+                dst_ref=near_rows.at[far_seq(index, slot, shards) % shards, landed_slot],
                 send_sem=far_send.at[step], recv_sem=far_recv.at[step],
                 device_id=far_member(slot), device_id_type=pl.DeviceIdType.MESH),
             pltpu.make_async_remote_copy(
@@ -469,7 +480,7 @@
     my_expert = seq_index // shards
     gate_here = jnp.sum(jnp.where(dec_routes == my_expert, dec_gates, 0.0), axis=1)
     returned, dec_all = axis_share(
-        [summed, gate_here[:, None] * dec_expert], [True, False], "seq", group_count, shards, 5
+        [summed, gate_here[:, None] * dec_expert], [True, False], "seq", group_count, shards, 5, twisted=True
     )
     dec_terms = jnp.sum(dec_all, axis=0)
     decode_out = (decode_hidden.astype(jnp.float32) + dec_terms).astype(jnp.bfloat16)

time: 256 us -> 260 us (1.016)
  the two profiles are of different devices: /device:TPU:32 before, /device:TPU:1 now
where the time goes in v10:
time: 260 us; the launch traced here: 259 us
  Pallas kernels  215 us (83%)
  local copies, waits for them, and re-layouts  17.1 us (7%)
  other arithmetic  14.3 us (6%)
  matrix products  11.8 us (5%)
    pallas_call x3, Pallas kernels, axis_share(): pl.pallas_call(functools.partial(share_kernel, axis, count, stride, twist...  129 us
    pallas_call x1, Pallas kernels, outbound(): pl.pallas_call(functools.partial(outbound_kernel, groups, shards, lanes),...  86.4 us
    dot_general x1, matrix products, expert_block(): jnp.dot(act, down_full, preferred_element_type=jnp.float32)  5.32 us

profile of v10, /device:TPU:1, one launch (start us, length us, event | category | flops | bytes accessed | tf_op | source)
XLA Modules:
  0.0 259.2 jit_solution(679424193078836391)
XLA Ops:
  2.1 1.0 copy.53
  4.0 0.9 fusion.50
  5.3 0.9 reshape.250
  9.4 1.0 fusion.14
  10.5 1.0 fusion.16
  11.7 1.2 scatter_custom_fusion
  13.0 0.9 reshape.247.slab_ref
  13.9 0.8 copy.38.gate_ref
  14.7 0.8 copy.39.up_ref
  15.5 86.4 %shard_map.194 = (bf16[4,16,10,1024]{3,2,1,0:T(8,128)(2,1)}, f32[4,16,8,128]{3,2,1,0:T(8,128)}, bf16[8,128,704]{2,1,0:T(8,128)(2,1)}, bf16[8,128,704]{2,1,0:T(8,128)(2,1)}, bf16[8,704,128]{2,1,0:T(8,128)(2,1)}) custom-call(bf16[16,10,1024]{2,1,0:T(8,128)(2,1)} %reshape.247.slab_ref, f32[8,128]{1,0:T(8,128)} %pad_maximum_fusion.5.part_ref, ...), custom_call_target="tpu_custom_call" | custom-call | tf_op jit(solution)/shard_map/pallas_call | solution.py:309
  102.0 1.3 slice_reduce_fusion.1
  104.2 1.0 fusion.20
  107.2 9.8 %shard_map.195 = f32[8,4,1024]{2,1,0:T(4,128)} custom-call(f32[4,1024]{1,0:T(4,128)} %fusion.35.refs_0_), custom_call_target="tpu_custom_call" | custom-call | tf_op jit(solution)/shard_map/pallas_call | solution.py:106
  116.9 0.9 reduce_sum.110
  118.1 1.3 reshape.255
  119.4 4.4 %fusion.13 = f32[644,704]{1,0:T(8,128)} fusion(bf16[1024,704]{1,0:T(8,128)(2,1)} %bitcast.64, bf16[4,1024]{1,0:T(4,128)(2,1)S(1)} %fusion.27, bf16[640,1024]{1,0:T(8,128)(2,1)} %reshape.255), kind=kOutput, calls=%fused_computation.20 | convolution fusion | flops 931151872 | bytes 4574208 | tf_op jit(solution)/shard_map/dot_general | solution.py:360
  123.9 5.3 %convolution_convert_fusion = bf16[644,1024]{1,0:T(8,128)(2,1)S(1)} fusion(f32[644,704]{1,0:T(8,128)} %fusion.13, bf16[1024,704]{1,0:T(8,128)(2,1)} %bitcast.63, bf16[4,1024]{1,0:T(4,128)(2,1)S(1)} %fusion.27, bf16[640,1024]{1,0:T(8,128)(2,1)S(1)} %copy-done.2, bf16[8,704,128]{2,1,0:T(8,128)(2,1)} %get-tuple-element.15), kind=kOutput, calls=%fused_computation.12 | convolution fusion | flops 1864859136 | bytes 7334912 | tf_op jit(solution)/shard_map/dot_general | solution.py:363
  129.3 1.6 reshape.259.refs_0_
  131.5 40.8 %shard_map.196 = (bf16[4,16,10,1024]{3,2,1,0:T(8,128)(2,1)}, bf16[4,4,1024]{2,1,0:T(4,128)(2,1)}) custom-call(bf16[4,16,10,1024]{3,2,1,0:T(8,128)(2,1)} %reshape.259.refs_0_, bf16[4,1024]{1,0:T(4,128)(2,1)} %slice.62.refs_1_), custom_call_target="tpu_custom_call" | custom-call | tf_op jit(solution)/shard_map/pallas_call | solution.py:106
  172.4 2.9 %add_bitcast_fusion.refs_0_ = f32[16,10,1024]{2,1,0:T(8,128)} fusion(bf16[4,16,10,1024]{3,2,1,0:T(8,128)(2,1)} %get-tuple-element.16), kind=kLoop, calls=%fused_computation.19 | loop fusion | flops 1146880 | bytes 1966080 | tf_op jit(solution)/shard_map/add | solution.py:478
  176.0 78.1 %shard_map.197 = (f32[16,10,1024]{2,1,0:T(8,128)}, f32[16,4,1024]{2,1,0:T(4,128)}) custom-call(f32[16,10,1024]{2,1,0:T(8,128)} %add_bitcast_fusion.refs_0_, f32[4,1024]{1,0:T(4,128)} %bitcast_multiply_fusion.refs_1_), custom_call_target="tpu_custom_call" | custom-call | tf_op jit(solution)/shard_map/pallas_call | solution.py:106
  254.0 1.3 reshape.260
  255.4 0.8 gather_fusion
  257.0 0.8 multiply_reduce_fusion
  (96 shorter events, 12.8 us)
Async XLA Ops:
  0.6 105.8 %copy-start = (bf16[128,1024]{1,0:T(8,128)(2,1)S(1)}, bf16[128,1024]{1,0:T(8,128)(2,1)}, u32[]{:S(2)}) copy-start(bf16[128,1024]{1,0:T(8,128)(2,1)} %param.27) | copy-start | bytes 786436
  6.2 7.7 %copy-start.5 = (bf16[128,704]{0,1:T(8,128)(2,1)S(1)}, bf16[128,704]{0,1:T(8,128)(2,1)}, u32[]{:S(2)}) copy-start(bf16[128,704]{0,1:T(8,128)(2,1)} %param.35) | copy-start | bytes 540676
  8.1 6.6 %copy-start.6 = (bf16[128,704]{0,1:T(8,128)(2,1)S(1)}, bf16[128,704]{0,1:T(8,128)(2,1)}, u32[]{:S(2)}) copy-start(bf16[128,704]{0,1:T(8,128)(2,1)} %param.36) | copy-start | bytes 540676
  13.9 91.8 %copy-start.13 = (bf16[4,128]{1,0:T(4,128)(2,1)S(1)}, bf16[4,128]{1,0:T(4,128)(2,1)}, u32[]{:S(2)}) copy-start(bf16[4,128]{1,0:T(4,128)(2,1)} %param.20) | copy-start | bytes 3076
  13.9 91.9 %copy-start.11 = (bf16[4,128]{1,0:T(4,128)(2,1)S(1)}, bf16[4,128]{1,0:T(4,128)(2,1)}, u32[]{:S(2)}) copy-start(bf16[4,128]{1,0:T(4,128)(2,1)} %param.19) | copy-start | bytes 3076
  14.7 91.7 %copy-start.12 = (bf16[4,128]{1,0:T(4,128)(2,1)S(1)}, bf16[4,128]{1,0:T(4,128)(2,1)}, u32[]{:S(2)}) copy-start(bf16[4,128]{1,0:T(4,128)(2,1)} %param.21) | copy-start | bytes 3076
  15.5 102.3 %copy-start.10 = (bf16[4,1024]{1,0:T(4,128)(2,1)S(1)}, bf16[4,1024]{1,0:T(4,128)(2,1)}, u32[]{:S(2)}) copy-start(bf16[4,1024]{1,0:T(4,128)(2,1)} %param.28) | copy-start | bytes 24580
  15.5 102.5 %copy-start.8 = (f32[1024]{0:T(1024)S(1)}, f32[1024]{0:T(1024)}, u32[]{:S(2)}) copy-start(f32[1024]{0:T(1024)} %param.34) | copy-start | bytes 12292
  102.0 16.1 %copy-start.1 = (bf16[4,16,10,1024]{3,2,1,0:T(8,128)(2,1)S(1)}, bf16[4,16,10,1024]{3,2,1,0:T(8,128)(2,1)}, u32[]{:S(2)}) copy-start(bf16[4,16,10,1024]{3,2,1,0:T(8,128)(2,1)} %get-tuple-element.12) | copy-start | bytes 3932164
  119.4 4.4 %copy-start.2 = (bf16[640,1024]{1,0:T(8,128)(2,1)S(1)}, bf16[640,1024]{1,0:T(8,128)(2,1)}, u32[]{:S(2)}) copy-start(bf16[640,1024]{1,0:T(8,128)(2,1)} %reshape.255) | copy-start | bytes 3932164
  172.3 2.9 %copy-start.14 = (f32[4,2]{0,1:T(2,128)S(1)}, f32[4,2]{0,1:T(2,128)}, u32[]{:S(2)}) copy-start(f32[4,2]{0,1:T(2,128)} %param.33) | copy-start | bytes 100
  172.3 2.9 %copy-start.15 = (s32[4,2]{0,1:T(2,128)S(1)}, s32[4,2]{0,1:T(2,128)}, u32[]{:S(2)}) copy-start(s32[4,2]{0,1:T(2,128)} %param.32) | copy-start | bytes 100
  172.3 2.9 %copy-start.7 = (bf16[4,4,1024]{2,1,0:T(4,128)(2,1)S(1)}, bf16[4,4,1024]{2,1,0:T(4,128)(2,1)}, u32[]{:S(2)}) copy-start(bf16[4,4,1024]{2,1,0:T(4,128)(2,1)} %get-tuple-element.17) | copy-start | bytes 98308
  255.4 1.4 copy-start.9
  255.4 1.5 copy-start.16
  256.2 1.6 copy-start.3
  256.2 2.3 copy-start.4

commit v11 on v9

--- a/solution.py
+++ b/solution.py
@@ -162,13 +162,6 @@
             lane_copy(which, step, lax.rem(lane_me + step, lanes), lane_me).start()
         return carry
 
-    lax.fori_loop(1, lanes, lane_start, 0)
-    own_weights = [
-        pltpu.make_async_copy(source_ref, landed_ref.at[lane_me], local_sem.at[3 + which])
-        for which, (source_ref, landed_ref) in enumerate(weight_refs)
-    ]
-    for copy in own_weights:
-        copy.start()
 
     def far_copy(step, slot, landed_slot):
         return (
@@ -192,6 +185,13 @@
     own_part = pltpu.make_async_copy(part_ref, far_parts.at[far_me], local_sem.at[1])
     own_slab.start()
     own_part.start()
+    lax.fori_loop(1, lanes, lane_start, 0)
+    own_weights = [
+        pltpu.make_async_copy(source_ref, landed_ref.at[lane_me], local_sem.at[3 + which])
+        for which, (source_ref, landed_ref) in enumerate(weight_refs)
+    ]
+    for copy in own_weights:
+        copy.start()
 
     def chain_copy(direction, origin, slab):
         return pltpu.make_async_remote_copy(

time: 256 us -> 255 us (level)
  no operation moved by 1% of the time
where the time goes in v11:
time: 255 us; the launch traced here: 254 us
  Pallas kernels  210 us (82%)
  local copies, waits for them, and re-layouts  17 us (7%)
  other arithmetic  14.3 us (6%)
  matrix products  11.8 us (5%)
    pallas_call x3, Pallas kernels, axis_share(): pl.pallas_call(functools.partial(share_kernel, axis, count, stride, tuple...  123 us
    pallas_call x1, Pallas kernels, outbound(): pl.pallas_call(functools.partial(outbound_kernel, groups, shards, lanes),...  86.4 us
    dot_general x1, matrix products, expert_block(): jnp.dot(act, down_full, preferred_element_type=jnp.float32)  5.32 us

profile of v11, /device:TPU:32, one launch (start us, length us, event | category | flops | bytes accessed | tf_op | source)
XLA Modules:
  0.0 253.8 jit_solution(5295436479522084089)
XLA Ops:
  2.1 1.0 copy.53
  4.0 0.9 fusion.50
  5.3 0.9 reshape.250
  9.4 1.0 fusion.14
  10.5 1.0 fusion.16
  11.7 1.2 scatter_custom_fusion
  13.0 0.9 reshape.247.slab_ref
  13.9 0.8 copy.38.gate_ref
  14.7 0.8 copy.39.up_ref
  15.5 86.4 %shard_map.194 = (bf16[4,16,10,1024]{3,2,1,0:T(8,128)(2,1)}, f32[4,16,8,128]{3,2,1,0:T(8,128)}, bf16[8,128,704]{2,1,0:T(8,128)(2,1)}, bf16[8,128,704]{2,1,0:T(8,128)(2,1)}, bf16[8,704,128]{2,1,0:T(8,128)(2,1)}) custom-call(bf16[16,10,1024]{2,1,0:T(8,128)(2,1)} %reshape.247.slab_ref, f32[8,128]{1,0:T(8,128)} %pad_maximum_fusion.5.part_ref, ...), custom_call_target="tpu_custom_call" | custom-call | tf_op jit(solution)/shard_map/pallas_call | solution.py:298
  101.9 1.3 slice_reduce_fusion.1
  104.1 1.0 fusion.20
  107.1 8.9 %shard_map.195 = f32[8,4,1024]{2,1,0:T(4,128)} custom-call(f32[4,1024]{1,0:T(4,128)} %fusion.35.refs_0_), custom_call_target="tpu_custom_call" | custom-call | tf_op jit(solution)/shard_map/pallas_call | solution.py:96
  116.1 0.9 reduce_sum.110
  117.2 1.3 reshape.255
  118.6 4.4 %fusion.13 = f32[644,704]{1,0:T(8,128)} fusion(bf16[1024,704]{1,0:T(8,128)(2,1)} %bitcast.64, bf16[4,1024]{1,0:T(4,128)(2,1)S(1)} %fusion.27, bf16[640,1024]{1,0:T(8,128)(2,1)} %reshape.255), kind=kOutput, calls=%fused_computation.20 | convolution fusion | flops 931151872 | bytes 4574208 | tf_op jit(solution)/shard_map/dot_general | solution.py:349
  123.0 5.3 %convolution_convert_fusion = bf16[644,1024]{1,0:T(8,128)(2,1)S(1)} fusion(f32[644,704]{1,0:T(8,128)} %fusion.13, bf16[1024,704]{1,0:T(8,128)(2,1)} %bitcast.63, bf16[4,1024]{1,0:T(4,128)(2,1)S(1)} %fusion.27, bf16[640,1024]{1,0:T(8,128)(2,1)S(1)} %copy-done.2, bf16[8,704,128]{2,1,0:T(8,128)(2,1)} %get-tuple-element.15), kind=kOutput, calls=%fused_computation.12 | convolution fusion | flops 1864859136 | bytes 7334912 | tf_op jit(solution)/shard_map/dot_general | solution.py:352
  128.4 1.6 reshape.259.refs_0_
  130.6 54.6 %shard_map.196 = (bf16[4,16,10,1024]{3,2,1,0:T(8,128)(2,1)}, bf16[4,4,1024]{2,1,0:T(4,128)(2,1)}) custom-call(bf16[4,16,10,1024]{3,2,1,0:T(8,128)(2,1)} %reshape.259.refs_0_, bf16[4,1024]{1,0:T(4,128)(2,1)} %slice.62.refs_1_), custom_call_target="tpu_custom_call" | custom-call | tf_op jit(solution)/shard_map/pallas_call | solution.py:96
  185.2 2.9 %add_bitcast_fusion.refs_0_ = f32[16,10,1024]{2,1,0:T(8,128)} fusion(bf16[4,16,10,1024]{3,2,1,0:T(8,128)(2,1)} %get-tuple-element.16), kind=kLoop, calls=%fused_computation.19 | loop fusion | flops 1146880 | bytes 1966080 | tf_op jit(solution)/shard_map/add | solution.py:467
  188.8 59.8 %shard_map.197 = (f32[16,10,1024]{2,1,0:T(8,128)}, f32[16,4,1024]{2,1,0:T(4,128)}) custom-call(f32[16,10,1024]{2,1,0:T(8,128)} %add_bitcast_fusion.refs_0_, f32[4,1024]{1,0:T(4,128)} %bitcast_multiply_fusion.refs_1_), custom_call_target="tpu_custom_call" | custom-call | tf_op jit(solution)/shard_map/pallas_call | solution.py:96
  248.7 1.3 reshape.260
  250.0 0.8 gather_fusion
  251.6 0.8 multiply_reduce_fusion
  (96 shorter events, 12.8 us)
Async XLA Ops:
  0.6 105.7 %copy-start = (bf16[128,1024]{1,0:T(8,128)(2,1)S(1)}, bf16[128,1024]{1,0:T(8,128)(2,1)}, u32[]{:S(2)}) copy-start(bf16[128,1024]{1,0:T(8,128)(2,1)} %param.27) | copy-start | bytes 786436
  6.2 7.7 %copy-start.5 = (bf16[128,704]{0,1:T(8,128)(2,1)S(1)}, bf16[128,704]{0,1:T(8,128)(2,1)}, u32[]{:S(2)}) copy-start(bf16[128,704]{0,1:T(8,128)(2,1)} %param.35) | copy-start | bytes 540676
  8.1 6.6 %copy-start.6 = (bf16[128,704]{0,1:T(8,128)(2,1)S(1)}, bf16[128,704]{0,1:T(8,128)(2,1)}, u32[]{:S(2)}) copy-start(bf16[128,704]{0,1:T(8,128)(2,1)} %param.36) | copy-start | bytes 540676
  13.9 91.7 %copy-start.13 = (bf16[4,128]{1,0:T(4,128)(2,1)S(1)}, bf16[4,128]{1,0:T(4,128)(2,1)}, u32[]{:S(2)}) copy-start(bf16[4,128]{1,0:T(4,128)(2,1)} %param.20) | copy-start | bytes 3076
  13.9 91.8 %copy-start.11 = (bf16[4,128]{1,0:T(4,128)(2,1)S(1)}, bf16[4,128]{1,0:T(4,128)(2,1)}, u32[]{:S(2)}) copy-start(bf16[4,128]{1,0:T(4,128)(2,1)} %param.19) | copy-start | bytes 3076
  14.7 91.7 %copy-start.12 = (bf16[4,128]{1,0:T(4,128)(2,1)S(1)}, bf16[4,128]{1,0:T(4,128)(2,1)}, u32[]{:S(2)}) copy-start(bf16[4,128]{1,0:T(4,128)(2,1)} %param.21) | copy-start | bytes 3076
  15.5 101.5 %copy-start.10 = (bf16[4,1024]{1,0:T(4,128)(2,1)S(1)}, bf16[4,1024]{1,0:T(4,128)(2,1)}, u32[]{:S(2)}) copy-start(bf16[4,1024]{1,0:T(4,128)(2,1)} %param.28) | copy-start | bytes 24580
  15.5 101.6 %copy-start.8 = (f32[1024]{0:T(1024)S(1)}, f32[1024]{0:T(1024)}, u32[]{:S(2)}) copy-start(f32[1024]{0:T(1024)} %param.34) | copy-start | bytes 12292
  101.9 15.3 %copy-start.1 = (bf16[4,16,10,1024]{3,2,1,0:T(8,128)(2,1)S(1)}, bf16[4,16,10,1024]{3,2,1,0:T(8,128)(2,1)}, u32[]{:S(2)}) copy-start(bf16[4,16,10,1024]{3,2,1,0:T(8,128)(2,1)} %get-tuple-element.12) | copy-start | bytes 3932164
  118.5 4.4 %copy-start.2 = (bf16[640,1024]{1,0:T(8,128)(2,1)S(1)}, bf16[640,1024]{1,0:T(8,128)(2,1)}, u32[]{:S(2)}) copy-start(bf16[640,1024]{1,0:T(8,128)(2,1)} %reshape.255) | copy-start | bytes 3932164
  185.2 2.9 %copy-start.14 = (f32[4,2]{0,1:T(2,128)S(1)}, f32[4,2]{0,1:T(2,128)}, u32[]{:S(2)}) copy-start(f32[4,2]{0,1:T(2,128)} %param.33) | copy-start | bytes 100
  185.2 2.9 %copy-start.15 = (s32[4,2]{0,1:T(2,128)S(1)}, s32[4,2]{0,1:T(2,128)}, u32[]{:S(2)}) copy-start(s32[4,2]{0,1:T(2,128)} %param.32) | copy-start | bytes 100
  185.2 2.9 %copy-start.7 = (bf16[4,4,1024]{2,1,0:T(4,128)(2,1)S(1)}, bf16[4,4,1024]{2,1,0:T(4,128)(2,1)}, u32[]{:S(2)}) copy-start(bf16[4,4,1024]{2,1,0:T(4,128)(2,1)} %get-tuple-element.17) | copy-start | bytes 98308
  250.0 1.4 copy-start.9
  250.0 1.5 copy-start.16
  250.8 1.6 copy-start.3
  250.8 2.3 copy-start.4

commit v12 on v11

--- a/solution.py
+++ b/solution.py
@@ -12,6 +12,11 @@
 EXPERTS = 16
 TOP = 2
 CAP = 10
+
+
+def spread(turn, count):
+    odd = turn % 2
+    return odd * ((turn + 1) // 2) + (1 - odd) * (count - turn // 2)
 
 
 def peer_device(axis, peer):
@@ -72,7 +77,8 @@
             device_id_type=pl.DeviceIdType.MESH,
         )
 
-    def launch(step, carry):
+    def launch(turn, carry):
+        step = spread(turn, count)
         for which in range(width):
             outgoing(which, step).start()
         return carry
@@ -157,7 +163,8 @@
             send_sem=lane_send.at[which, step], recv_sem=lane_recv.at[which, step],
             device_id=lane_member(slot), device_id_type=pl.DeviceIdType.MESH)
 
-    def lane_start(step, carry):
+    def lane_start(turn, carry):
+        step = spread(turn, lanes)
         for which in range(3):
             lane_copy(which, step, lax.rem(lane_me + step, lanes), lane_me).start()
         return carry
@@ -175,7 +182,8 @@
                 device_id=far_member(slot), device_id_type=pl.DeviceIdType.MESH),
         )
 
-    def far_start(step, carry):
+    def far_start(turn, carry):
+        step = spread(turn, groups)
         for copy in far_copy(step, lax.rem(far_me + step, groups), far_me):
             copy.start()
         return carry

time: 255 us -> 264 us (1.035)
  the two profiles are of different devices: /device:TPU:32 before, /device:TPU:1 now
where the time goes in v12:
time: 264 us; the launch traced here: 263 us
  Pallas kernels  219 us (83%)
  local copies, waits for them, and re-layouts  17.1 us (6%)
  other arithmetic  14.3 us (5%)
  matrix products  11.8 us (4%)
    pallas_call x3, Pallas kernels, axis_share(): pl.pallas_call(functools.partial(share_kernel, axis, count, stride, tuple...  129 us
    pallas_call x1, Pallas kernels, outbound(): pl.pallas_call(functools.partial(outbound_kernel, groups, shards, lanes),...  89.7 us
    dot_general x1, matrix products, expert_block(): jnp.dot(act, down_full, preferred_element_type=jnp.float32)  5.32 us

profile of v12, /device:TPU:1, one launch (start us, length us, event | category | flops | bytes accessed | tf_op | source)
XLA Modules:
  0.0 263.2 jit_solution(15981619344129978378)
XLA Ops:
  2.1 1.0 copy.53
  4.0 0.9 fusion.50
  5.3 0.9 reshape.250
  9.4 1.0 fusion.14
  10.5 1.0 fusion.16
  11.7 1.2 scatter_custom_fusion
  13.0 0.9 reshape.247.slab_ref
  13.9 0.8 copy.38.gate_ref
  14.7 0.8 copy.39.up_ref
  15.5 89.7 %shard_map.194 = (bf16[4,16,10,1024]{3,2,1,0:T(8,128)(2,1)}, f32[4,16,8,128]{3,2,1,0:T(8,128)}, bf16[8,128,704]{2,1,0:T(8,128)(2,1)}, bf16[8,128,704]{2,1,0:T(8,128)(2,1)}, bf16[8,704,128]{2,1,0:T(8,128)(2,1)}) custom-call(bf16[16,10,1024]{2,1,0:T(8,128)(2,1)} %reshape.247.slab_ref, f32[8,128]{1,0:T(8,128)} %pad_maximum_fusion.5.part_ref, ...), custom_call_target="tpu_custom_call" | custom-call | tf_op jit(solution)/shard_map/pallas_call | solution.py:306
  105.3 1.3 slice_reduce_fusion.1
  107.5 1.0 fusion.20
  110.5 9.3 %shard_map.195 = f32[8,4,1024]{2,1,0:T(4,128)} custom-call(f32[4,1024]{1,0:T(4,128)} %fusion.35.refs_0_), custom_call_target="tpu_custom_call" | custom-call | tf_op jit(solution)/shard_map/pallas_call | solution.py:102
  119.8 0.9 reduce_sum.110
  121.0 1.3 reshape.255
  122.3 4.4 %fusion.13 = f32[644,704]{1,0:T(8,128)} fusion(bf16[1024,704]{1,0:T(8,128)(2,1)} %bitcast.64, bf16[4,1024]{1,0:T(4,128)(2,1)S(1)} %fusion.27, bf16[640,1024]{1,0:T(8,128)(2,1)} %reshape.255), kind=kOutput, calls=%fused_computation.20 | convolution fusion | flops 931151872 | bytes 4574208 | tf_op jit(solution)/shard_map/dot_general | solution.py:357
  126.8 5.3 %convolution_convert_fusion = bf16[644,1024]{1,0:T(8,128)(2,1)S(1)} fusion(f32[644,704]{1,0:T(8,128)} %fusion.13, bf16[1024,704]{1,0:T(8,128)(2,1)} %bitcast.63, bf16[4,1024]{1,0:T(4,128)(2,1)S(1)} %fusion.27, bf16[640,1024]{1,0:T(8,128)(2,1)S(1)} %copy-done.2, bf16[8,704,128]{2,1,0:T(8,128)(2,1)} %get-tuple-element.15), kind=kOutput, calls=%fused_computation.12 | convolution fusion | flops 1864859136 | bytes 7334912 | tf_op jit(solution)/shard_map/dot_general | solution.py:360
  132.2 1.6 reshape.259.refs_0_
  134.4 52.0 %shard_map.196 = (bf16[4,16,10,1024]{3,2,1,0:T(8,128)(2,1)}, bf16[4,4,1024]{2,1,0:T(4,128)(2,1)}) custom-call(bf16[4,16,10,1024]{3,2,1,0:T(8,128)(2,1)} %reshape.259.refs_0_, bf16[4,1024]{1,0:T(4,128)(2,1)} %slice.62.refs_1_), custom_call_target="tpu_custom_call" | custom-call | tf_op jit(solution)/shard_map/pallas_call | solution.py:102
  186.4 2.9 %add_bitcast_fusion.refs_0_ = f32[16,10,1024]{2,1,0:T(8,128)} fusion(bf16[4,16,10,1024]{3,2,1,0:T(8,128)(2,1)} %get-tuple-element.16), kind=kLoop, calls=%fused_computation.19 | loop fusion | flops 1146880 | bytes 1966080 | tf_op jit(solution)/shard_map/add | solution.py:475
  190.0 68.1 %shard_map.197 = (f32[16,10,1024]{2,1,0:T(8,128)}, f32[16,4,1024]{2,1,0:T(4,128)}) custom-call(f32[16,10,1024]{2,1,0:T(8,128)} %add_bitcast_fusion.refs_0_, f32[4,1024]{1,0:T(4,128)} %bitcast_multiply_fusion.refs_1_), custom_call_target="tpu_custom_call" | custom-call | tf_op jit(solution)/shard_map/pallas_call | solution.py:102
  258.1 1.3 reshape.260
  259.5 0.8 gather_fusion
  261.1 0.8 multiply_reduce_fusion
  (96 shorter events, 12.8 us)
Async XLA Ops:
  0.6 109.1 %copy-start = (bf16[128,1024]{1,0:T(8,128)(2,1)S(1)}, bf16[128,1024]{1,0:T(8,128)(2,1)}, u32[]{:S(2)}) copy-start(bf16[128,1024]{1,0:T(8,128)(2,1)} %param.27) | copy-start | bytes 786436
  6.2 7.7 %copy-start.5 = (bf16[128,704]{0,1:T(8,128)(2,1)S(1)}, bf16[128,704]{0,1:T(8,128)(2,1)}, u32[]{:S(2)}) copy-start(bf16[128,704]{0,1:T(8,128)(2,1)} %param.35) | copy-start | bytes 540676
  8.1 6.6 %copy-start.6 = (bf16[128,704]{0,1:T(8,128)(2,1)S(1)}, bf16[128,704]{0,1:T(8,128)(2,1)}, u32[]{:S(2)}) copy-start(bf16[128,704]{0,1:T(8,128)(2,1)} %param.36) | copy-start | bytes 540676
  13.9 95.1 %copy-start.13 = (bf16[4,128]{1,0:T(4,128)(2,1)S(1)}, bf16[4,128]{1,0:T(4,128)(2,1)}, u32[]{:S(2)}) copy-start(bf16[4,128]{1,0:T(4,128)(2,1)} %param.20) | copy-start | bytes 3076
  13.9 95.2 %copy-start.11 = (bf16[4,128]{1,0:T(4,128)(2,1)S(1)}, bf16[4,128]{1,0:T(4,128)(2,1)}, u32[]{:S(2)}) copy-start(bf16[4,128]{1,0:T(4,128)(2,1)} %param.19) | copy-start | bytes 3076
  14.7 95.0 %copy-start.12 = (bf16[4,128]{1,0:T(4,128)(2,1)S(1)}, bf16[4,128]{1,0:T(4,128)(2,1)}, u32[]{:S(2)}) copy-start(bf16[4,128]{1,0:T(4,128)(2,1)} %param.21) | copy-start | bytes 3076
  15.5 105.2 %copy-start.10 = (bf16[4,1024]{1,0:T(4,128)(2,1)S(1)}, bf16[4,1024]{1,0:T(4,128)(2,1)}, u32[]{:S(2)}) copy-start(bf16[4,1024]{1,0:T(4,128)(2,1)} %param.28) | copy-start | bytes 24580
  15.5 105.4 %copy-start.8 = (f32[1024]{0:T(1024)S(1)}, f32[1024]{0:T(1024)}, u32[]{:S(2)}) copy-start(f32[1024]{0:T(1024)} %param.34) | copy-start | bytes 12292
  105.3 15.7 %copy-start.1 = (bf16[4,16,10,1024]{3,2,1,0:T(8,128)(2,1)S(1)}, bf16[4,16,10,1024]{3,2,1,0:T(8,128)(2,1)}, u32[]{:S(2)}) copy-start(bf16[4,16,10,1024]{3,2,1,0:T(8,128)(2,1)} %get-tuple-element.12) | copy-start | bytes 3932164
  122.3 4.4 %copy-start.2 = (bf16[640,1024]{1,0:T(8,128)(2,1)S(1)}, bf16[640,1024]{1,0:T(8,128)(2,1)}, u32[]{:S(2)}) copy-start(bf16[640,1024]{1,0:T(8,128)(2,1)} %reshape.255) | copy-start | bytes 3932164
  186.4 2.9 %copy-start.14 = (f32[4,2]{0,1:T(2,128)S(1)}, f32[4,2]{0,1:T(2,128)}, u32[]{:S(2)}) copy-start(f32[4,2]{0,1:T(2,128)} %param.33) | copy-start | bytes 100
  186.4 2.9 %copy-start.15 = (s32[4,2]{0,1:T(2,128)S(1)}, s32[4,2]{0,1:T(2,128)}, u32[]{:S(2)}) copy-start(s32[4,2]{0,1:T(2,128)} %param.32) | copy-start | bytes 100
  186.4 2.9 %copy-start.7 = (bf16[4,4,1024]{2,1,0:T(4,128)(2,1)S(1)}, bf16[4,4,1024]{2,1,0:T(4,128)(2,1)}, u32[]{:S(2)}) copy-start(bf16[4,4,1024]{2,1,0:T(4,128)(2,1)} %get-tuple-element.17) | copy-start | bytes 98308
  259.4 1.4 copy-start.9
  259.5 1.5 copy-start.16
  260.3 1.6 copy-start.3
  260.3 2.3 copy-start.4

commit v13 on v11

--- a/solution.py
+++ b/solution.py
@@ -150,10 +150,17 @@
     pl.semaphore_wait(barrier, groups + shards + lanes - 3)
     weight_refs = ((gate_ref, gate_all), (up_ref, up_all), (down_ref, down_all))
 
+    def lane_target(which, landed_slot):
+        source_ref, landed_ref = weight_refs[which]
+        if which == 2:
+            return landed_ref.at[landed_slot]
+        width = source_ref.shape[1]
+        return landed_ref.at[:, pl.ds(pl.multiple_of(landed_slot * width, width), width)]
+
     def lane_copy(which, step, slot, landed_slot):
         source_ref, landed_ref = weight_refs[which]
         return pltpu.make_async_remote_copy(
-            src_ref=source_ref, dst_ref=landed_ref.at[landed_slot],
+            src_ref=source_ref, dst_ref=lane_target(which, landed_slot),
             send_sem=lane_send.at[which, step], recv_sem=lane_recv.at[which, step],
             device_id=lane_member(slot), device_id_type=pl.DeviceIdType.MESH)
 
@@ -187,7 +194,7 @@
     own_part.start()
     lax.fori_loop(1, lanes, lane_start, 0)
     own_weights = [
-        pltpu.make_async_copy(source_ref, landed_ref.at[lane_me], local_sem.at[3 + which])
+        pltpu.make_async_copy(source_ref, lane_target(which, lane_me), local_sem.at[3 + which])
         for which, (source_ref, landed_ref) in enumerate(weight_refs)
     ]
     for copy in own_weights:
@@ -294,7 +301,9 @@
 def outbound(slabs, parts, weights, groups, shards, lanes, collective_id):
     rows_shape = (shards,) + slabs.shape
     parts_shape = (shards, groups) + parts.shape
-    weight_shapes = [jax.ShapeDtypeStruct((lanes,) + w.shape, w.dtype) for w in weights]
+    weight_shapes = [
+        jax.ShapeDtypeStruct((w.shape[0], lanes * w.shape[1]), w.dtype) for w in weights[:2]
+    ] + [jax.ShapeDtypeStruct((lanes,) + weights[2].shape, weights[2].dtype)]
     return pl.pallas_call(
         functools.partial(outbound_kernel, groups, shards, lanes),
         out_shape=[jax.ShapeDtypeStruct(rows_shape, slabs.dtype),
@@ -419,11 +428,11 @@
     )
     group_count = seq_count // shards
     block_rows, block_parts, gate_all, up_all, down_all = outbound(
-        slabs, packed_parts, (w_gate, w_up, w_down), group_count, shards, tp_count, 1
+        slabs, packed_parts, (w_gate.T, w_up.T, w_down), group_count, shards, tp_count, 1
     )
     weights = (
-        gate_all.reshape(-1, gate_all.shape[-1]),
-        up_all.reshape(-1, up_all.shape[-1]),
+        gate_all.T,
+        up_all.T,
         jnp.transpose(down_all, (1, 0, 2)).reshape(down_all.shape[1], -1),
     )
     stage = merge_softmax(

time: 255 us -> 253 us (level)
  no operation moved by 1% of the time
where the time goes in v13:
time: 253 us; the launch traced here: 252 us
  Pallas kernels  210 us (83%)
  local copies, waits for them, and re-layouts  15.4 us (6%)
  other arithmetic  14.3 us (6%)
  matrix products  11.7 us (5%)
    pallas_call x3, Pallas kernels, axis_share(): pl.pallas_call(functools.partial(share_kernel, axis, count, stride, tuple...  123 us
    pallas_call x1, Pallas kernels, outbound(): pl.pallas_call(functools.partial(outbound_kernel, groups, shards, lanes),...  86.3 us
    dot_general x1, matrix products, expert_block(): jnp.dot(act, down_full, preferred_element_type=jnp.float32)  5.33 us

profile of v13, /device:TPU:32, one launch (start us, length us, event | category | flops | bytes accessed | tf_op | source)
XLA Modules:
  0.0 252.1 jit_solution(3852148359778016004)
XLA Ops:
  2.1 1.0 copy.47
  4.0 0.9 fusion.50
  5.3 0.9 reshape.244
  7.1 0.8 copy.33
  9.4 1.0 fusion.14
  10.5 1.0 fusion.16
  11.7 1.2 scatter_custom_fusion
  13.0 0.9 reshape.241.slab_ref
  13.9 86.3 %shard_map.194 = (bf16[4,16,10,1024]{3,2,1,0:T(8,128)(2,1)}, f32[4,16,8,128]{3,2,1,0:T(8,128)}, bf16[704,1024]{1,0:T(8,128)(2,1)}, bf16[704,1024]{1,0:T(8,128)(2,1)}, bf16[8,704,128]{2,1,0:T(8,128)(2,1)}) custom-call(bf16[16,10,1024]{2,1,0:T(8,128)(2,1)} %reshape.241.slab_ref, f32[8,128]{1,0:T(8,128)} %pad_maximum_fusion.5.part_ref, ...), custom_call_target="tpu_custom_call" | custom-call | tf_op jit(solution)/shard_map/pallas_call | solution.py:307
  100.2 1.3 slice_reduce_fusion.1
  102.4 1.0 fusion.20
  104.7 0.8 fusion.35.refs_0_
  105.4 8.9 %shard_map.195 = f32[8,4,1024]{2,1,0:T(4,128)} custom-call(f32[4,1024]{1,0:T(4,128)} %fusion.35.refs_0_), custom_call_target="tpu_custom_call" | custom-call | tf_op jit(solution)/shard_map/pallas_call | solution.py:96
  114.4 0.9 reduce_sum.110
  115.5 1.3 reshape.249
  116.8 4.4 %fusion.13 = f32[644,704]{1,0:T(8,128)} fusion(bf16[704,1024]{1,0:T(8,128)(2,1)} %get-tuple-element.13, bf16[4,1024]{1,0:T(4,128)(2,1)S(1)} %fusion.27, bf16[640,1024]{1,0:T(8,128)(2,1)} %reshape.249), kind=kOutput, calls=%fused_computation.20 | convolution fusion | flops 931151872 | bytes 4574208 | tf_op jit(solution)/shard_map/dot_general | solution.py:358
  121.2 5.3 %convolution_convert_fusion = bf16[644,1024]{1,0:T(8,128)(2,1)S(1)} fusion(f32[644,704]{1,0:T(8,128)} %fusion.13, bf16[704,1024]{1,0:T(8,128)(2,1)} %get-tuple-element.14, bf16[4,1024]{1,0:T(4,128)(2,1)S(1)} %fusion.27, bf16[640,1024]{1,0:T(8,128)(2,1)S(1)} %copy-done.2, bf16[8,704,128]{2,1,0:T(8,128)(2,1)} %get-tuple-element.15), kind=kOutput, calls=%fused_computation.12 | convolution fusion | flops 1864859136 | bytes 7334912 | tf_op jit(solution)/shard_map/dot_general | solution.py:361
  126.7 1.6 reshape.251.refs_0_
  128.9 54.6 %shard_map.196 = (bf16[4,16,10,1024]{3,2,1,0:T(8,128)(2,1)}, bf16[4,4,1024]{2,1,0:T(4,128)(2,1)}) custom-call(bf16[4,16,10,1024]{3,2,1,0:T(8,128)(2,1)} %reshape.251.refs_0_, bf16[4,1024]{1,0:T(4,128)(2,1)} %slice.62.refs_1_), custom_call_target="tpu_custom_call" | custom-call | tf_op jit(solution)/shard_map/pallas_call | solution.py:96
  183.5 2.9 %add_bitcast_fusion.refs_0_ = f32[16,10,1024]{2,1,0:T(8,128)} fusion(bf16[4,16,10,1024]{3,2,1,0:T(8,128)(2,1)} %get-tuple-element.16), kind=kLoop, calls=%fused_computation.19 | loop fusion | flops 1146880 | bytes 1966080 | tf_op jit(solution)/shard_map/add | solution.py:476
  187.1 59.8 %shard_map.197 = (f32[16,10,1024]{2,1,0:T(8,128)}, f32[16,4,1024]{2,1,0:T(4,128)}) custom-call(f32[16,10,1024]{2,1,0:T(8,128)} %add_bitcast_fusion.refs_0_, f32[4,1024]{1,0:T(4,128)} %bitcast_multiply_fusion.refs_1_), custom_call_target="tpu_custom_call" | custom-call | tf_op jit(solution)/shard_map/pallas_call | solution.py:96
  246.9 1.3 reshape.252
  248.3 0.8 gather_fusion
  249.9 0.8 multiply_reduce_fusion
  (90 shorter events, 11.2 us)
Async XLA Ops:
  0.6 104.0 %copy-start = (bf16[128,1024]{1,0:T(8,128)(2,1)S(1)}, bf16[128,1024]{1,0:T(8,128)(2,1)}, u32[]{:S(2)}) copy-start(bf16[128,1024]{1,0:T(8,128)(2,1)} %param.27) | copy-start | bytes 786436
  13.9 90.0 %copy-start.11 = (bf16[4,128]{1,0:T(4,128)(2,1)S(1)}, bf16[4,128]{1,0:T(4,128)(2,1)}, u32[]{:S(2)}) copy-start(bf16[4,128]{1,0:T(4,128)(2,1)} %param.20) | copy-start | bytes 3076
  13.9 90.1 %copy-start.9 = (bf16[4,128]{1,0:T(4,128)(2,1)S(1)}, bf16[4,128]{1,0:T(4,128)(2,1)}, u32[]{:S(2)}) copy-start(bf16[4,128]{1,0:T(4,128)(2,1)} %param.19) | copy-start | bytes 3076
  13.9 90.8 %copy-start.10 = (bf16[4,128]{1,0:T(4,128)(2,1)S(1)}, bf16[4,128]{1,0:T(4,128)(2,1)}, u32[]{:S(2)}) copy-start(bf16[4,128]{1,0:T(4,128)(2,1)} %param.21) | copy-start | bytes 3076
  13.9 101.4 %copy-start.8 = (bf16[4,1024]{1,0:T(4,128)(2,1)S(1)}, bf16[4,1024]{1,0:T(4,128)(2,1)}, u32[]{:S(2)}) copy-start(bf16[4,1024]{1,0:T(4,128)(2,1)} %param.28) | copy-start | bytes 24580
  13.9 101.5 %copy-start.6 = (f32[1024]{0:T(1024)S(1)}, f32[1024]{0:T(1024)}, u32[]{:S(2)}) copy-start(f32[1024]{0:T(1024)} %param.34) | copy-start | bytes 12292
  100.2 15.3 %copy-start.1 = (bf16[4,16,10,1024]{3,2,1,0:T(8,128)(2,1)S(1)}, bf16[4,16,10,1024]{3,2,1,0:T(8,128)(2,1)}, u32[]{:S(2)}) copy-start(bf16[4,16,10,1024]{3,2,1,0:T(8,128)(2,1)} %get-tuple-element.12) | copy-start | bytes 3932164
  116.8 4.4 %copy-start.2 = (bf16[640,1024]{1,0:T(8,128)(2,1)S(1)}, bf16[640,1024]{1,0:T(8,128)(2,1)}, u32[]{:S(2)}) copy-start(bf16[640,1024]{1,0:T(8,128)(2,1)} %reshape.249) | copy-start | bytes 3932164
  183.5 2.9 %copy-start.12 = (f32[4,2]{0,1:T(2,128)S(1)}, f32[4,2]{0,1:T(2,128)}, u32[]{:S(2)}) copy-start(f32[4,2]{0,1:T(2,128)} %param.33) | copy-start | bytes 100
  183.5 2.9 %copy-start.13 = (s32[4,2]{0,1:T(2,128)S(1)}, s32[4,2]{0,1:T(2,128)}, u32[]{:S(2)}) copy-start(s32[4,2]{0,1:T(2,128)} %param.32) | copy-start | bytes 100
  183.5 2.9 %copy-start.5 = (bf16[4,4,1024]{2,1,0:T(4,128)(2,1)S(1)}, bf16[4,4,1024]{2,1,0:T(4,128)(2,1)}, u32[]{:S(2)}) copy-start(bf16[4,4,1024]{2,1,0:T(4,128)(2,1)} %get-tuple-element.17) | copy-start | bytes 98308
  248.3 1.4 copy-start.7
  248.3 1.5 copy-start.14
  249.1 1.6 copy-start.3
  249.1 2.3 copy-start.4

commit v14 on v13

--- a/solution.py
+++ b/solution.py
@@ -309,7 +309,8 @@
         out_shape=[jax.ShapeDtypeStruct(rows_shape, slabs.dtype),
                    jax.ShapeDtypeStruct(parts_shape, parts.dtype)] + weight_shapes,
         in_specs=[pl.BlockSpec(memory_space=pltpu.VMEM)] * 5,
-        out_specs=[pl.BlockSpec(memory_space=pltpu.VMEM)] * 5,
+        out_specs=[pl.BlockSpec(memory_space=pltpu.VMEM)] * 2
+        + [pl.BlockSpec(memory_space=pl.ANY)] * 3,
         scratch_shapes=[pltpu.VMEM((groups,) + parts.shape, parts.dtype)]
         + [pltpu.SemaphoreType.DMA((groups,))] * 4
         + [pltpu.SemaphoreType.DMA((2, shards, groups)), pltpu.SemaphoreType.DMA((shards, groups))]

time: 253 us -> 252 us (level)
  no operation moved by 1% of the time
where the time goes in v14:
time: 252 us; the launch traced here: 251 us
  Pallas kernels  208 us (83%)
  local copies, waits for them, and re-layouts  15.4 us (6%)
  other arithmetic  14.3 us (6%)
  matrix products  11.8 us (5%)
    pallas_call x3, Pallas kernels, axis_share(): pl.pallas_call(functools.partial(share_kernel, axis, count, stride, tuple...  123 us
    pallas_call x1, Pallas kernels, outbound(): pl.pallas_call(functools.partial(outbound_kernel, groups, shards, lanes),...  85 us
    dot_general x1, matrix products, expert_block(): jnp.dot(act, down_full, preferred_element_type=jnp.float32)  5.32 us

profile of v14, /device:TPU:32, one launch (start us, length us, event | category | flops | bytes accessed | tf_op | source)
XLA Modules:
  0.0 250.9 jit_solution(1805490941328361128)
XLA Ops:
  2.1 1.0 copy.47
  4.0 0.9 fusion.50
  5.3 0.9 reshape.244
  7.1 0.8 copy.33
  9.4 1.0 fusion.14
  10.5 1.0 fusion.16
  11.7 1.2 scatter_custom_fusion
  13.0 0.9 reshape.241.slab_ref
  13.9 85.0 %shard_map.194 = (bf16[4,16,10,1024]{3,2,1,0:T(8,128)(2,1)}, f32[4,16,8,128]{3,2,1,0:T(8,128)}, bf16[704,1024]{1,0:T(8,128)(2,1)}, bf16[704,1024]{1,0:T(8,128)(2,1)}, bf16[8,704,128]{2,1,0:T(8,128)(2,1)}) custom-call(bf16[16,10,1024]{2,1,0:T(8,128)(2,1)} %reshape.241.slab_ref, f32[8,128]{1,0:T(8,128)} %pad_maximum_fusion.5.part_ref, ...), custom_call_target="tpu_custom_call" | custom-call | tf_op jit(solution)/shard_map/pallas_call | solution.py:307
  98.9 1.3 slice_reduce_fusion.1
  101.1 1.0 fusion.20
  103.4 0.8 fusion.35.refs_0_
  104.1 8.9 %shard_map.195 = f32[8,4,1024]{2,1,0:T(4,128)} custom-call(f32[4,1024]{1,0:T(4,128)} %fusion.35.refs_0_), custom_call_target="tpu_custom_call" | custom-call | tf_op jit(solution)/shard_map/pallas_call | solution.py:96
  113.1 0.9 reduce_sum.110
  114.2 1.3 reshape.249
  115.6 4.4 %fusion.13 = f32[644,704]{1,0:T(8,128)} fusion(bf16[704,1024]{1,0:T(8,128)(2,1)} %get-tuple-element.13, bf16[4,1024]{1,0:T(4,128)(2,1)S(1)} %fusion.27, bf16[640,1024]{1,0:T(8,128)(2,1)} %reshape.249), kind=kOutput, calls=%fused_computation.20 | convolution fusion | flops 931151872 | bytes 4574208 | tf_op jit(solution)/shard_map/dot_general | solution.py:359
  119.9 5.3 %convolution_convert_fusion = bf16[644,1024]{1,0:T(8,128)(2,1)S(1)} fusion(f32[644,704]{1,0:T(8,128)} %fusion.13, bf16[704,1024]{1,0:T(8,128)(2,1)} %get-tuple-element.14, bf16[4,1024]{1,0:T(4,128)(2,1)S(1)} %fusion.27, bf16[640,1024]{1,0:T(8,128)(2,1)S(1)} %copy-done.2, bf16[8,704,128]{2,1,0:T(8,128)(2,1)} %get-tuple-element.15), kind=kOutput, calls=%fused_computation.12 | convolution fusion | flops 1864859136 | bytes 7334912 | tf_op jit(solution)/shard_map/dot_general | solution.py:362
  125.4 1.6 reshape.251.refs_0_
  127.6 54.7 %shard_map.196 = (bf16[4,16,10,1024]{3,2,1,0:T(8,128)(2,1)}, bf16[4,4,1024]{2,1,0:T(4,128)(2,1)}) custom-call(bf16[4,16,10,1024]{3,2,1,0:T(8,128)(2,1)} %reshape.251.refs_0_, bf16[4,1024]{1,0:T(4,128)(2,1)} %slice.62.refs_1_), custom_call_target="tpu_custom_call" | custom-call | tf_op jit(solution)/shard_map/pallas_call | solution.py:96
  182.3 2.9 %add_bitcast_fusion.refs_0_ = f32[16,10,1024]{2,1,0:T(8,128)} fusion(bf16[4,16,10,1024]{3,2,1,0:T(8,128)(2,1)} %get-tuple-element.16), kind=kLoop, calls=%fused_computation.19 | loop fusion | flops 1146880 | bytes 1966080 | tf_op jit(solution)/shard_map/add | solution.py:477
  185.9 59.8 %shard_map.197 = (f32[16,10,1024]{2,1,0:T(8,128)}, f32[16,4,1024]{2,1,0:T(4,128)}) custom-call(f32[16,10,1024]{2,1,0:T(8,128)} %add_bitcast_fusion.refs_0_, f32[4,1024]{1,0:T(4,128)} %bitcast_multiply_fusion.refs_1_), custom_call_target="tpu_custom_call" | custom-call | tf_op jit(solution)/shard_map/pallas_call | solution.py:96
  245.7 1.3 reshape.252
  247.1 0.8 gather_fusion
  248.7 0.8 multiply_reduce_fusion
  (90 shorter events, 11.2 us)
Async XLA Ops:
  0.6 102.7 %copy-start = (bf16[128,1024]{1,0:T(8,128)(2,1)S(1)}, bf16[128,1024]{1,0:T(8,128)(2,1)}, u32[]{:S(2)}) copy-start(bf16[128,1024]{1,0:T(8,128)(2,1)} %param.27) | copy-start | bytes 786436
  13.9 88.7 %copy-start.11 = (bf16[4,128]{1,0:T(4,128)(2,1)S(1)}, bf16[4,128]{1,0:T(4,128)(2,1)}, u32[]{:S(2)}) copy-start(bf16[4,128]{1,0:T(4,128)(2,1)} %param.20) | copy-start | bytes 3076
  13.9 88.8 %copy-start.9 = (bf16[4,128]{1,0:T(4,128)(2,1)S(1)}, bf16[4,128]{1,0:T(4,128)(2,1)}, u32[]{:S(2)}) copy-start(bf16[4,128]{1,0:T(4,128)(2,1)} %param.19) | copy-start | bytes 3076
  13.9 89.5 %copy-start.10 = (bf16[4,128]{1,0:T(4,128)(2,1)S(1)}, bf16[4,128]{1,0:T(4,128)(2,1)}, u32[]{:S(2)}) copy-start(bf16[4,128]{1,0:T(4,128)(2,1)} %param.21) | copy-start | bytes 3076
  13.9 100.1 %copy-start.8 = (bf16[4,1024]{1,0:T(4,128)(2,1)S(1)}, bf16[4,1024]{1,0:T(4,128)(2,1)}, u32[]{:S(2)}) copy-start(bf16[4,1024]{1,0:T(4,128)(2,1)} %param.28) | copy-start | bytes 24580
  13.9 100.2 %copy-start.6 = (f32[1024]{0:T(1024)S(1)}, f32[1024]{0:T(1024)}, u32[]{:S(2)}) copy-start(f32[1024]{0:T(1024)} %param.34) | copy-start | bytes 12292
  98.9 15.3 %copy-start.1 = (bf16[4,16,10,1024]{3,2,1,0:T(8,128)(2,1)S(1)}, bf16[4,16,10,1024]{3,2,1,0:T(8,128)(2,1)}, u32[]{:S(2)}) copy-start(bf16[4,16,10,1024]{3,2,1,0:T(8,128)(2,1)} %get-tuple-element.12) | copy-start | bytes 3932164
  115.5 4.4 %copy-start.2 = (bf16[640,1024]{1,0:T(8,128)(2,1)S(1)}, bf16[640,1024]{1,0:T(8,128)(2,1)}, u32[]{:S(2)}) copy-start(bf16[640,1024]{1,0:T(8,128)(2,1)} %reshape.249) | copy-start | bytes 3932164
  182.3 2.9 %copy-start.12 = (f32[4,2]{0,1:T(2,128)S(1)}, f32[4,2]{0,1:T(2,128)}, u32[]{:S(2)}) copy-start(f32[4,2]{0,1:T(2,128)} %param.33) | copy-start | bytes 100
  182.3 2.9 %copy-start.13 = (s32[4,2]{0,1:T(2,128)S(1)}, s32[4,2]{0,1:T(2,128)}, u32[]{:S(2)}) copy-start(s32[4,2]{0,1:T(2,128)} %param.32) | copy-start | bytes 100
  182.3 2.9 %copy-start.5 = (bf16[4,4,1024]{2,1,0:T(4,128)(2,1)S(1)}, bf16[4,4,1024]{2,1,0:T(4,128)(2,1)}, u32[]{:S(2)}) copy-start(bf16[4,4,1024]{2,1,0:T(4,128)(2,1)} %get-tuple-element.17) | copy-start | bytes 98308
  247.1 1.4 copy-start.7
  247.1 1.5 copy-start.14
  247.9 1.6 copy-start.3
  247.9 2.3 copy-start.4

commit v15 on v14

--- a/solution.py
+++ b/solution.py
@@ -25,7 +25,8 @@
     sources = refs[:width]
     landed = refs[width : 2 * width]
     send_sems = refs[2 * width : 3 * width]
-    recv_sems = refs[3 * width :]
+    recv_sems = refs[3 * width : 4 * width]
+    own_sem = refs[4 * width]
     index = lax.axis_index(axis)
     me = lax.rem(index // stride, count)
     base = index - me * stride
@@ -78,8 +79,12 @@
         return carry
 
     lax.fori_loop(1, count, launch, 0)
-    for which in range(width):
-        landed[which][me] = piece(which, me)[...]
+    own_copies = [
+        pltpu.make_async_copy(piece(which, me), landed[which].at[me], own_sem.at[which])
+        for which in range(width)
+    ]
+    for copy in own_copies:
+        copy.start()
 
     def finish(step, carry):
         for which in range(width):
@@ -88,6 +93,8 @@
         return carry
 
     lax.fori_loop(1, count, finish, 0)
+    for copy in own_copies:
+        copy.wait()
 
 
 def axis_share(payloads, modes, axis, count, stride, collective_id):
@@ -97,8 +104,9 @@
         functools.partial(share_kernel, axis, count, stride, tuple(modes)),
         out_shape=[jax.ShapeDtypeStruct(s, x.dtype) for s, x in zip(shapes, payloads)],
         in_specs=[pl.BlockSpec(memory_space=pltpu.VMEM)] * width,
-        out_specs=[pl.BlockSpec(memory_space=pltpu.VMEM)] * width,
-        scratch_shapes=[pltpu.SemaphoreType.DMA((count,))] * (2 * width),
+        out_specs=[pl.BlockSpec(memory_space=pl.ANY)] * width,
+        scratch_shapes=[pltpu.SemaphoreType.DMA((count,))] * (2 * width)
+        + [pltpu.SemaphoreType.DMA((width,))],
         compiler_params=pltpu.CompilerParams(collective_id=collective_id, has_side_effects=True),
     )(*payloads)
 

time: 252 us -> 250 us (level)
  no operation moved by 1% of the time
where the time goes in v15:
time: 250 us; the launch traced here: 249 us
  Pallas kernels  207 us (83%)
  local copies, waits for them, and re-layouts  15.4 us (6%)
  other arithmetic  14.3 us (6%)
  matrix products  11.7 us (5%)
    pallas_call x3, Pallas kernels, axis_share(): pl.pallas_call(functools.partial(share_kernel, axis, count, stride, tuple...  122 us
    pallas_call x1, Pallas kernels, outbound(): pl.pallas_call(functools.partial(outbound_kernel, groups, shards, lanes),...  85 us
    dot_general x1, matrix products, expert_block(): jnp.dot(act, down_full, preferred_element_type=jnp.float32)  5.32 us

profile of v15, /device:TPU:32, one launch (start us, length us, event | category | flops | bytes accessed | tf_op | source)
XLA Modules:
  0.0 249.0 jit_solution(6202720673534815340)
XLA Ops:
  2.1 1.0 copy.47
  4.0 0.9 fusion.50
  5.3 0.9 reshape.244
  7.1 0.8 copy.33
  9.4 1.0 fusion.14
  10.5 1.0 fusion.16
  11.7 1.2 scatter_custom_fusion
  13.0 0.9 reshape.241.slab_ref
  13.9 85.0 %shard_map.194 = (bf16[4,16,10,1024]{3,2,1,0:T(8,128)(2,1)}, f32[4,16,8,128]{3,2,1,0:T(8,128)}, bf16[704,1024]{1,0:T(8,128)(2,1)}, bf16[704,1024]{1,0:T(8,128)(2,1)}, bf16[8,704,128]{2,1,0:T(8,128)(2,1)}) custom-call(bf16[16,10,1024]{2,1,0:T(8,128)(2,1)} %reshape.241.slab_ref, f32[8,128]{1,0:T(8,128)} %pad_maximum_fusion.5.part_ref, ...), custom_call_target="tpu_custom_call" | custom-call | tf_op jit(solution)/shard_map/pallas_call | solution.py:315
  98.9 1.3 slice_reduce_fusion.1
  101.1 1.0 fusion.20
  103.4 0.8 fusion.35.refs_0_
  104.1 8.4 %shard_map.195 = f32[8,4,1024]{2,1,0:T(4,128)} custom-call(f32[4,1024]{1,0:T(4,128)} %fusion.35.refs_0_), custom_call_target="tpu_custom_call" | custom-call | tf_op jit(solution)/shard_map/pallas_call | solution.py:103
  112.5 0.9 reduce_sum.110
  113.7 1.3 reshape.249
  115.0 4.4 %fusion.13 = f32[644,704]{1,0:T(8,128)} fusion(bf16[704,1024]{1,0:T(8,128)(2,1)} %get-tuple-element.13, bf16[4,1024]{1,0:T(4,128)(2,1)S(1)} %fusion.27, bf16[640,1024]{1,0:T(8,128)(2,1)} %reshape.249), kind=kOutput, calls=%fused_computation.20 | convolution fusion | flops 931151872 | bytes 4574208 | tf_op jit(solution)/shard_map/dot_general | solution.py:367
  119.4 5.3 %convolution_convert_fusion = bf16[644,1024]{1,0:T(8,128)(2,1)S(1)} fusion(f32[644,704]{1,0:T(8,128)} %fusion.13, bf16[704,1024]{1,0:T(8,128)(2,1)} %get-tuple-element.14, bf16[4,1024]{1,0:T(4,128)(2,1)S(1)} %fusion.27, bf16[640,1024]{1,0:T(8,128)(2,1)S(1)} %copy-done.2, bf16[8,704,128]{2,1,0:T(8,128)(2,1)} %get-tuple-element.15), kind=kOutput, calls=%fused_computation.12 | convolution fusion | flops 1864859136 | bytes 7334912 | tf_op jit(solution)/shard_map/dot_general | solution.py:370
  124.8 1.6 reshape.251.refs_0_
  127.0 70.6 %shard_map.196 = (bf16[4,16,10,1024]{3,2,1,0:T(8,128)(2,1)}, bf16[4,4,1024]{2,1,0:T(4,128)(2,1)}) custom-call(bf16[4,16,10,1024]{3,2,1,0:T(8,128)(2,1)} %reshape.251.refs_0_, bf16[4,1024]{1,0:T(4,128)(2,1)} %slice.62.refs_1_), custom_call_target="tpu_custom_call" | custom-call | tf_op jit(solution)/shard_map/pallas_call | solution.py:103
  197.7 2.9 %add_bitcast_fusion.refs_0_ = f32[16,10,1024]{2,1,0:T(8,128)} fusion(bf16[4,16,10,1024]{3,2,1,0:T(8,128)(2,1)} %get-tuple-element.16), kind=kLoop, calls=%fused_computation.19 | loop fusion | flops 1146880 | bytes 1966080 | tf_op jit(solution)/shard_map/add | solution.py:485
  201.3 42.6 %shard_map.197 = (f32[16,10,1024]{2,1,0:T(8,128)}, f32[16,4,1024]{2,1,0:T(4,128)}) custom-call(f32[16,10,1024]{2,1,0:T(8,128)} %add_bitcast_fusion.refs_0_, f32[4,1024]{1,0:T(4,128)} %bitcast_multiply_fusion.refs_1_), custom_call_target="tpu_custom_call" | custom-call | tf_op jit(solution)/shard_map/pallas_call | solution.py:103
  243.9 1.3 reshape.252
  245.2 0.8 gather_fusion
  246.8 0.8 multiply_reduce_fusion
  (90 shorter events, 11.2 us)
Async XLA Ops:
  0.6 102.7 %copy-start = (bf16[128,1024]{1,0:T(8,128)(2,1)S(1)}, bf16[128,1024]{1,0:T(8,128)(2,1)}, u32[]{:S(2)}) copy-start(bf16[128,1024]{1,0:T(8,128)(2,1)} %param.27) | copy-start | bytes 786436
  13.9 88.7 %copy-start.11 = (bf16[4,128]{1,0:T(4,128)(2,1)S(1)}, bf16[4,128]{1,0:T(4,128)(2,1)}, u32[]{:S(2)}) copy-start(bf16[4,128]{1,0:T(4,128)(2,1)} %param.20) | copy-start | bytes 3076
  13.9 88.8 %copy-start.9 = (bf16[4,128]{1,0:T(4,128)(2,1)S(1)}, bf16[4,128]{1,0:T(4,128)(2,1)}, u32[]{:S(2)}) copy-start(bf16[4,128]{1,0:T(4,128)(2,1)} %param.19) | copy-start | bytes 3076
  13.9 89.5 %copy-start.10 = (bf16[4,128]{1,0:T(4,128)(2,1)S(1)}, bf16[4,128]{1,0:T(4,128)(2,1)}, u32[]{:S(2)}) copy-start(bf16[4,128]{1,0:T(4,128)(2,1)} %param.21) | copy-start | bytes 3076
  13.9 99.6 %copy-start.8 = (bf16[4,1024]{1,0:T(4,128)(2,1)S(1)}, bf16[4,1024]{1,0:T(4,128)(2,1)}, u32[]{:S(2)}) copy-start(bf16[4,1024]{1,0:T(4,128)(2,1)} %param.28) | copy-start | bytes 24580
  13.9 99.7 %copy-start.6 = (f32[1024]{0:T(1024)S(1)}, f32[1024]{0:T(1024)}, u32[]{:S(2)}) copy-start(f32[1024]{0:T(1024)} %param.34) | copy-start | bytes 12292
  98.9 14.8 %copy-start.1 = (bf16[4,16,10,1024]{3,2,1,0:T(8,128)(2,1)S(1)}, bf16[4,16,10,1024]{3,2,1,0:T(8,128)(2,1)}, u32[]{:S(2)}) copy-start(bf16[4,16,10,1024]{3,2,1,0:T(8,128)(2,1)} %get-tuple-element.12) | copy-start | bytes 3932164
  115.0 4.4 %copy-start.2 = (bf16[640,1024]{1,0:T(8,128)(2,1)S(1)}, bf16[640,1024]{1,0:T(8,128)(2,1)}, u32[]{:S(2)}) copy-start(bf16[640,1024]{1,0:T(8,128)(2,1)} %reshape.249) | copy-start | bytes 3932164
  197.7 2.9 %copy-start.12 = (f32[4,2]{0,1:T(2,128)S(1)}, f32[4,2]{0,1:T(2,128)}, u32[]{:S(2)}) copy-start(f32[4,2]{0,1:T(2,128)} %param.33) | copy-start | bytes 100
  197.7 2.9 %copy-start.13 = (s32[4,2]{0,1:T(2,128)S(1)}, s32[4,2]{0,1:T(2,128)}, u32[]{:S(2)}) copy-start(s32[4,2]{0,1:T(2,128)} %param.32) | copy-start | bytes 100
  197.7 2.9 %copy-start.5 = (bf16[4,4,1024]{2,1,0:T(4,128)(2,1)S(1)}, bf16[4,4,1024]{2,1,0:T(4,128)(2,1)}, u32[]{:S(2)}) copy-start(bf16[4,4,1024]{2,1,0:T(4,128)(2,1)} %get-tuple-element.17) | copy-start | bytes 98308
  245.2 1.4 copy-start.7
  245.2 1.5 copy-start.14
  246.0 1.6 copy-start.3
  246.0 2.3 copy-start.4

commit v16 on v15

--- a/solution.py
+++ b/solution.py
@@ -317,8 +317,7 @@
         out_shape=[jax.ShapeDtypeStruct(rows_shape, slabs.dtype),
                    jax.ShapeDtypeStruct(parts_shape, parts.dtype)] + weight_shapes,
         in_specs=[pl.BlockSpec(memory_space=pltpu.VMEM)] * 5,
-        out_specs=[pl.BlockSpec(memory_space=pltpu.VMEM)] * 2
-        + [pl.BlockSpec(memory_space=pl.ANY)] * 3,
+        out_specs=[pl.BlockSpec(memory_space=pl.ANY)] * 5,
         scratch_shapes=[pltpu.VMEM((groups,) + parts.shape, parts.dtype)]
         + [pltpu.SemaphoreType.DMA((groups,))] * 4
         + [pltpu.SemaphoreType.DMA((2, shards, groups)), pltpu.SemaphoreType.DMA((shards, groups))]

time: 250 us -> 248 us (level)
  the two profiles are of different devices: /device:TPU:32 before, /device:TPU:102 now
where the time goes in v16:
time: 248 us; the launch traced here: 247 us
  Pallas kernels  204 us (82%)
  local copies, waits for them, and re-layouts  15.4 us (6%)
  other arithmetic  14.3 us (6%)
  matrix products  11.7 us (5%)
    pallas_call x3, Pallas kernels, axis_share(): pl.pallas_call(functools.partial(share_kernel, axis, count, stride, tuple...  123 us
    pallas_call x1, Pallas kernels, outbound(): pl.pallas_call(functools.partial(outbound_kernel, groups, shards, lanes),...  81.8 us
    dot_general x1, matrix products, expert_block(): jnp.dot(act, down_full, preferred_element_type=jnp.float32)  5.32 us

profile of v16, /device:TPU:102, one launch (start us, length us, event | category | flops | bytes accessed | tf_op | source)
XLA Modules:
  0.0 246.9 jit_solution(4990935690050398628)
XLA Ops:
  2.1 1.0 copy.47
  4.0 0.9 fusion.50
  5.3 0.9 reshape.244
  7.1 0.8 copy.33
  9.4 1.0 fusion.14
  10.5 1.0 fusion.16
  11.7 1.2 scatter_custom_fusion
  13.0 0.9 reshape.241.slab_ref
  13.9 81.8 %shard_map.194 = (bf16[4,16,10,1024]{3,2,1,0:T(8,128)(2,1)}, f32[4,16,8,128]{3,2,1,0:T(8,128)}, bf16[704,1024]{1,0:T(8,128)(2,1)}, bf16[704,1024]{1,0:T(8,128)(2,1)}, bf16[8,704,128]{2,1,0:T(8,128)(2,1)}) custom-call(bf16[16,10,1024]{2,1,0:T(8,128)(2,1)} %reshape.241.slab_ref, f32[8,128]{1,0:T(8,128)} %pad_maximum_fusion.5.part_ref, ...), custom_call_target="tpu_custom_call" | custom-call | tf_op jit(solution)/shard_map/pallas_call | solution.py:315
  95.7 1.3 slice_reduce_fusion.1
  97.9 1.0 fusion.20
  100.1 0.8 fusion.35.refs_0_
  100.9 8.4 %shard_map.195 = f32[8,4,1024]{2,1,0:T(4,128)} custom-call(f32[4,1024]{1,0:T(4,128)} %fusion.35.refs_0_), custom_call_target="tpu_custom_call" | custom-call | tf_op jit(solution)/shard_map/pallas_call | solution.py:103
  109.3 0.9 reduce_sum.110
  110.5 1.3 reshape.249
  111.8 4.4 %fusion.13 = f32[644,704]{1,0:T(8,128)} fusion(bf16[704,1024]{1,0:T(8,128)(2,1)} %get-tuple-element.13, bf16[4,1024]{1,0:T(4,128)(2,1)S(1)} %fusion.27, bf16[640,1024]{1,0:T(8,128)(2,1)} %reshape.249), kind=kOutput, calls=%fused_computation.20 | convolution fusion | flops 931151872 | bytes 4574208 | tf_op jit(solution)/shard_map/dot_general | solution.py:366
  116.2 5.3 %convolution_convert_fusion = bf16[644,1024]{1,0:T(8,128)(2,1)S(1)} fusion(f32[644,704]{1,0:T(8,128)} %fusion.13, bf16[704,1024]{1,0:T(8,128)(2,1)} %get-tuple-element.14, bf16[4,1024]{1,0:T(4,128)(2,1)S(1)} %fusion.27, bf16[640,1024]{1,0:T(8,128)(2,1)S(1)} %copy-done.2, bf16[8,704,128]{2,1,0:T(8,128)(2,1)} %get-tuple-element.15), kind=kOutput, calls=%fused_computation.12 | convolution fusion | flops 1864859136 | bytes 7334912 | tf_op jit(solution)/shard_map/dot_general | solution.py:369
  121.6 1.6 reshape.251.refs_0_
  123.8 51.9 %shard_map.196 = (bf16[4,16,10,1024]{3,2,1,0:T(8,128)(2,1)}, bf16[4,4,1024]{2,1,0:T(4,128)(2,1)}) custom-call(bf16[4,16,10,1024]{3,2,1,0:T(8,128)(2,1)} %reshape.251.refs_0_, bf16[4,1024]{1,0:T(4,128)(2,1)} %slice.62.refs_1_), custom_call_target="tpu_custom_call" | custom-call | tf_op jit(solution)/shard_map/pallas_call | solution.py:103
  175.8 2.9 %add_bitcast_fusion.refs_0_ = f32[16,10,1024]{2,1,0:T(8,128)} fusion(bf16[4,16,10,1024]{3,2,1,0:T(8,128)(2,1)} %get-tuple-element.16), kind=kLoop, calls=%fused_computation.19 | loop fusion | flops 1146880 | bytes 1966080 | tf_op jit(solution)/shard_map/add | solution.py:484
  179.4 62.4 %shard_map.197 = (f32[16,10,1024]{2,1,0:T(8,128)}, f32[16,4,1024]{2,1,0:T(4,128)}) custom-call(f32[16,10,1024]{2,1,0:T(8,128)} %add_bitcast_fusion.refs_0_, f32[4,1024]{1,0:T(4,128)} %bitcast_multiply_fusion.refs_1_), custom_call_target="tpu_custom_call" | custom-call | tf_op jit(solution)/shard_map/pallas_call | solution.py:103
  241.8 1.3 reshape.252
  243.1 0.8 gather_fusion
  244.7 0.8 multiply_reduce_fusion
  (90 shorter events, 11.2 us)
Async XLA Ops:
  0.6 99.5 %copy-start = (bf16[128,1024]{1,0:T(8,128)(2,1)S(1)}, bf16[128,1024]{1,0:T(8,128)(2,1)}, u32[]{:S(2)}) copy-start(bf16[128,1024]{1,0:T(8,128)(2,1)} %param.27) | copy-start | bytes 786436
  13.9 85.5 %copy-start.11 = (bf16[4,128]{1,0:T(4,128)(2,1)S(1)}, bf16[4,128]{1,0:T(4,128)(2,1)}, u32[]{:S(2)}) copy-start(bf16[4,128]{1,0:T(4,128)(2,1)} %param.20) | copy-start | bytes 3076
  13.9 85.6 %copy-start.9 = (bf16[4,128]{1,0:T(4,128)(2,1)S(1)}, bf16[4,128]{1,0:T(4,128)(2,1)}, u32[]{:S(2)}) copy-start(bf16[4,128]{1,0:T(4,128)(2,1)} %param.19) | copy-start | bytes 3076
  13.9 86.3 %copy-start.10 = (bf16[4,128]{1,0:T(4,128)(2,1)S(1)}, bf16[4,128]{1,0:T(4,128)(2,1)}, u32[]{:S(2)}) copy-start(bf16[4,128]{1,0:T(4,128)(2,1)} %param.21) | copy-start | bytes 3076
  13.9 96.3 %copy-start.8 = (bf16[4,1024]{1,0:T(4,128)(2,1)S(1)}, bf16[4,1024]{1,0:T(4,128)(2,1)}, u32[]{:S(2)}) copy-start(bf16[4,1024]{1,0:T(4,128)(2,1)} %param.28) | copy-start | bytes 24580
  13.9 96.5 %copy-start.6 = (f32[1024]{0:T(1024)S(1)}, f32[1024]{0:T(1024)}, u32[]{:S(2)}) copy-start(f32[1024]{0:T(1024)} %param.34) | copy-start | bytes 12292
  95.7 14.8 %copy-start.1 = (bf16[4,16,10,1024]{3,2,1,0:T(8,128)(2,1)S(1)}, bf16[4,16,10,1024]{3,2,1,0:T(8,128)(2,1)}, u32[]{:S(2)}) copy-start(bf16[4,16,10,1024]{3,2,1,0:T(8,128)(2,1)} %get-tuple-element.12) | copy-start | bytes 3932164
  111.8 4.4 %copy-start.2 = (bf16[640,1024]{1,0:T(8,128)(2,1)S(1)}, bf16[640,1024]{1,0:T(8,128)(2,1)}, u32[]{:S(2)}) copy-start(bf16[640,1024]{1,0:T(8,128)(2,1)} %reshape.249) | copy-start | bytes 3932164
  175.7 2.9 %copy-start.12 = (f32[4,2]{0,1:T(2,128)S(1)}, f32[4,2]{0,1:T(2,128)}, u32[]{:S(2)}) copy-start(f32[4,2]{0,1:T(2,128)} %param.33) | copy-start | bytes 100
  175.8 2.9 %copy-start.13 = (s32[4,2]{0,1:T(2,128)S(1)}, s32[4,2]{0,1:T(2,128)}, u32[]{:S(2)}) copy-start(s32[4,2]{0,1:T(2,128)} %param.32) | copy-start | bytes 100
  175.8 2.9 %copy-start.5 = (bf16[4,4,1024]{2,1,0:T(4,128)(2,1)S(1)}, bf16[4,4,1024]{2,1,0:T(4,128)(2,1)}, u32[]{:S(2)}) copy-start(bf16[4,4,1024]{2,1,0:T(4,128)(2,1)} %get-tuple-element.17) | copy-start | bytes 98308
  243.1 1.4 copy-start.7
  243.1 1.5 copy-start.14
  243.9 1.6 copy-start.3
  243.9 2.3 copy-start.4
